TPU v7x, 128 devices: a whole 4x4x4 slice. The times are simulated.
128 devices in a mesh: sub: 16 (over x, y), row: 8 (over z, core).
Axes of the slice: x: 4, y: 4, z: 4, core: 2. Of those that a mesh axis runs over, the one named last changes fastest.
Arguments:
- sigma_top: float32 [6144, 6144], P('row', 'sub'), may hold values from -2 to 4, as said below
- coupling: float32 [16, 6144, 768], P('sub', 'row'), may hold values from -0.16 to 0.16
- child_inverse: float32 [16, 768, 768], P('sub', 'row'), may hold values from -1 to 10, as said below
- tile_mask: int32 [16, 24], P('sub'), may hold values 0 or 1
- obs_node: int32 [32768], P(('sub', 'row')), may hold values from 0 to 12287
- obs_noise: float32 [32768], P(('sub', 'row')), may hold values from 0.05 to 2
Outputs:
- sep_child: float32 [16, 6144, 768], P('sub', 'row')
- child_block: float32 [16, 768, 768], P('sub', 'row')
- loo_var: float32 [32768], P(('sub', 'row'))
Inputs may be any that keep to these rules, and one draw needn't show every extreme that they name: sigma_top is exactly symmetric. Each child_inverse[c] is exactly symmetric.
All inputs are finite; a program needn't handle non-finite values. No bound on the sum of `tile_mask` on one device may be relied on, other than what follows from the above.
Results may differ from a plain program's by a relative error of at most 0.000073.
Values sent between devices are 32-bit elements; how exact they have to be, the bound alone decides.
No kernel may reach another device: no remote copies, remote signals or barrier semaphores. Data moves between devices by JAX's collectives and lax.ppermute only.
A program may use at most 128 MiB of HBM per device.

v0:
```python
import jax
import jax.numpy as jnp
from jax import lax
from jax.sharding import PartitionSpec as P

TILE = 256


def local(sigma_top, coupling, child_inverse, tile_mask, obs_node, obs_noise):
    highest = lax.Precision.HIGHEST
    rows_here = coupling.shape[1]
    width_here = child_inverse.shape[1]
    tiles_here = rows_here // TILE
    row_index = lax.axis_index("row")
    mask_here = lax.dynamic_slice_in_dim(tile_mask[0], row_index * tiles_here, tiles_here)
    row_mask = jnp.repeat(mask_here, TILE).astype(jnp.float32)
    masked = coupling[0] * row_mask[:, None]
    gathered = lax.all_gather(masked, "row", axis=0, tiled=True)
    product = jnp.dot(
        lax.all_gather(sigma_top, "sub", axis=1, tiled=True),
        gathered,
        precision=highest,
        preferred_element_type=jnp.float32,
    )
    sep_part = -product
    update = lax.psum_scatter(
        lax.dot_general(
            masked,
            sep_part,
            (((0,), (0,)), ((), ())),
            precision=highest,
            preferred_element_type=jnp.float32,
        ),
        "row",
        scatter_dimension=0,
        tiled=True,
    )
    block_here = child_inverse[0] - update
    own_cols = lax.dynamic_slice_in_dim(block_here, row_index * width_here, width_here, 1)
    own_diag = jnp.diagonal(own_cols)
    every_var = lax.all_gather(own_diag, ("sub", "row"), axis=0, tiled=True)
    loo_var = every_var[obs_node] + obs_noise
    return (sep_part[None], block_here[None], loo_var)


def solution(mesh):
    placed = (
        P("row", "sub"),
        P("sub", "row", None),
        P("sub", "row", None),
        P("sub", None),
        P(("sub", "row")),
        P(("sub", "row")),
    )
    return jax.shard_map(
        local,
        mesh=mesh,
        in_specs=placed,
        out_specs=(P("sub", "row", None), P("sub", "row", None), P(("sub", "row"))),
        check_vma=False,
    )
```

profile of v0, /device:TPU:16, one launch (start us, length us, event | category | flops | bytes accessed | tf_op | source)
XLA Modules:
  0.0 448.0 jit_solution(1674996634150140336)
XLA Ops:
  7.2 0.0 all-gather.3.cloned.1.call-start
  7.2 0.7 convert_bitcast_fusion
  7.9 0.1 broadcast_in_dim.17
  8.0 3.3 bitcast_multiply_fusion
  11.3 0.0 all-gather.3.cloned.1.call-update
  11.3 0.0 all-gather.5.cloned.1.call-start
  11.4 0.7 all-gather.5.cloned.1.call-update
  12.1 0.0 copy-start
  12.1 0.0 reduce-scatter.2.cloned.1.call-start
  12.2 95.5 %all-gather.3.cloned.1.call-done = f32[6144,768]{1,0:T(8,128)} async-done(((f32[768,768]{1,0:T(8,128)}), f32[6144,768]{1,0:T(8,128)}) %all-gather.3.cloned.1.call-update) | async-done | bytes 18874384 | tf_op jit(solution)/shard_map/all_gather | solution.py:18
  107.7 124.6 %all-gather.5.cloned.1.call-done = f32[768,6144]{1,0:T(8,128)} async-done(((f32[768,384]{1,0:T(8,128)}), f32[768,6144]{1,0:T(8,128)}) %all-gather.5.cloned.1.call-update) | async-done | bytes 18874384 | tf_op jit(solution)/shard_map/all_gather | solution.py:20
  232.3 92.2 %fusion.2 = f32[768,768]{1,0:T(8,128)S(1)} fusion(f32[6144,768]{1,0:T(8,128)} %all-gather.3.cloned.1.call-done, f32[768,6144]{1,0:T(8,128)} %all-gather.5.cloned.1.call-done), kind=kOutput, calls=%fused_computation.12 | convolution fusion | flops 43486543872 | bytes 40108032 | tf_op jit(solution)/shard_map/dot_general | solution.py:19
  324.5 0.0 copy-start.1
  324.5 1.4 copy-done.1
  325.9 0.0 copy-done
  325.9 12.5 %fusion = f32[768,768]{1,0:T(8,128)} fusion(f32[768,768]{1,0:T(8,128)S(1)} %copy-done, f32[768,768]{1,0:T(8,128)S(1)} %fusion.2), kind=kOutput, calls=%fused_computation.3 | convolution fusion | flops 5436407808 | bytes 7077888 | tf_op jit(solution)/shard_map/dot_general | solution.py:27
  338.5 0.0 copy-start.6
  338.5 0.0 copy-start.2
  338.5 0.0 reduce-scatter.2.cloned.1.call-update
  338.5 0.6 copy-done.6
  339.1 1.0 copy-done.2
  340.1 1.6 negate_bitcast_fusion
  341.7 0.0 copy-start.4
  341.7 3.1 copy.10
  344.8 0.0 copy-start.5
  344.8 28.0 %reduce-scatter.2.cloned.1.call-done = f32[96,768]{1,0:T(8,128)} async-done(((f32[768,768]{1,0:T(8,128)}), f32[96,768]{1,0:T(8,128)}) %reduce-scatter.2.cloned.1.call-update) | async-done | bytes 294928 | tf_op jit(solution)/shard_map/reduce_scatter | solution.py:26
  372.8 0.0 copy-done.4
  372.8 1.0 bitcast_subtract_fusion
  373.8 0.0 copy-start.3
  373.8 0.1 constant_dynamic-slice_fusion
  373.9 1.2 gather_fusion
  375.2 0.3 dynamic-update-slice
  375.4 63.7 %all-reduce = f32[12288]{0:T(1024)S(1)} all-reduce(f32[12288]{0:T(1024)S(1)} %dynamic-update-slice), channel_id=1, replica_groups=mesh['sub'=16,'row'=8] {'sub','row'}, use_global_device_ids=true, to_apply=%add | all-reduce | flops 12288 | bytes 98304
  439.2 1.7 gather_fusion.1
  440.9 0.0 copy-done.5
  440.9 0.6 add.25
  441.5 0.0 copy-done.3
  (5 shorter events, 0.0 us)
Async XLA Ops:
  7.2 100.5 %all-gather.3.cloned.1.call-start = ((), (), s32[]{:S(2)}) async-start(), calls=%async_computation.1 | async-start | bytes 21233664 | tf_op jit(solution)/shard_map/all_gather | solution.py:18
  11.3 221.0 %all-gather.5.cloned.1.call-start = ((), (), s32[]{:S(2)}) async-start(), calls=%async_computation.2 | async-start | bytes 20054016 | tf_op jit(solution)/shard_map/all_gather | solution.py:20
  12.1 313.8 %copy-start = (f32[768,768]{1,0:T(8,128)S(1)}, f32[768,768]{1,0:T(8,128)}, u32[]{:S(2)}) copy-start(f32[768,768]{1,0:T(8,128)} %bitcast_multiply_fusion) | copy-start | bytes 7077892
  12.1 360.7 %reduce-scatter.2.cloned.1.call-start = ((), (), s32[]{:S(2)}) async-start(), calls=%async_computation.3 | async-start | bytes 2654208 | tf_op jit(solution)/shard_map/reduce_scatter | solution.py:26
  324.5 1.4 copy-start.1
  338.5 0.7 copy-start.6
  338.5 1.7 copy-start.2
  341.7 31.1 %copy-start.4 = (f32[1,96,768]{2,1,0:T(8,128)S(1)}, f32[1,96,768]{2,1,0:T(8,128)}, u32[]{:S(2)}) copy-start(f32[1,96,768]{2,1,0:T(8,128)} %param.8) | copy-start | bytes 884740
  344.8 96.1 %copy-start.5 = (f32[256]{0:T(256)S(1)}, f32[256]{0:T(256)}, u32[]{:S(2)}) copy-start(f32[256]{0:T(256)} %param.11) | copy-start | bytes 3076
  373.8 67.7 %copy-start.3 = (f32[96,768]{1,0:T(8,128)}, f32[96,768]{1,0:T(8,128)S(1)}, u32[]{:S(2)}) copy-start(f32[96,768]{1,0:T(8,128)S(1)} %bitcast_subtract_fusion) | copy-start | bytes 884740
Sparse Core Ops, SparseCore 0:
  11.5 96.1 all-gather.2
  109.9 122.4 all-gather.4
  338.6 34.1 reduce-scatter.1
where the time goes:
time: 450 us; the launch traced here: 448 us
  waiting for transfers between devices  249 us (55%)
  matrix products  105 us (23%)
  blocking collectives  63.7 us (14%)
  between operations  13.8 us (3%)
  local copies, waits for them, and re-layouts  9.55 us (2%)
  other arithmetic  7.17 us (2%)
    all_gather x1, waiting for transfers between devices, local(): lax.all_gather(sigma_top, 'sub', axis=1, tiled=True)  125 us
    all_gather x1, waiting for transfers between devices, local(): gathered = lax.all_gather(masked, 'row', axis=0, tiled=True)  95.5 us
    dot_general x1, matrix products, local(): jnp.dot(lax.all_gather(sigma_top, 'sub', axis=1, tiled=True), gathered, p...  92.2 us
    unnamed x1, blocking collectives  63.7 us
    reduce_scatter x1, waiting for transfers between devices, local(): lax.psum_scatter(lax.dot_general(masked, sep_part, (((0,), (0,)), ((), ()...  28 us
    dot_general x1, matrix products, local(): lax.dot_general(masked, sep_part, (((0,), (0,)), ((), ())), precision=hig...  12.5 us
  transfers between devices with their start and end apart: 3, of which 3 were waited for; matrix products, arithmetic and copies ran while one was open for 1% of the time, Pallas kernels for 0%

commit v1 on v0

v1 whole, which is shorter than its diff:
```python
import jax
import jax.numpy as jnp
from jax import lax
from jax.experimental import pallas as pl
from jax.experimental.pallas import tpu as pltpu
from jax.sharding import PartitionSpec as P

AXES = ("sub", "row")
BOTH = jnp.bfloat16


def place(x, y, z, c):
    return (x % 4) * 32 + (y % 4) * 8 + (z % 4) * 2 + c % 2


def send(value, dx=0, dy=0, dz=0, dc=0):
    pairs = [
        (place(x, y, z, c), place(x + dx, y + dy, z + dz, c + dc))
        for x in range(4)
        for y in range(4)
        for z in range(4)
        for c in range(2)
    ]
    return lax.ppermute(value, AXES, pairs)


def split(value):
    high = value.astype(BOTH)
    low = (value - high.astype(jnp.float32)).astype(BOTH)
    return high, low


def dot3(a, b, dims):
    a_high, a_low = a
    b_high, b_low = b
    one = lambda u, v: lax.dot_general(u, v, (dims, ((), ())), preferred_element_type=jnp.float32)
    return one(a_high, b_high) + (one(a_low, b_high) + one(a_high, b_low))


ROWS = ((1,), (0,))
COLS = ((0,), (0,))


def pair_loop(pairs, sources, where, mask, coupling_all, sums, s_buf, m_buf, m_index, s_sem, m_sem):
    x = where[0]
    y = where[1]
    count = len(pairs)
    half_of = count // 2

    def start(q, slot):
        source, unit, first, second = pairs[q]
        for part, (dx, dy) in enumerate((first, second)):
            block = ((x + dx) & 3) * 4 + ((y + dy) & 3)
            m_index[slot, part] = block
            pltpu.make_async_copy(
                sources[source].at[unit + part], s_buf.at[slot, :, pl.ds(part * 384, 384)], s_sem.at[slot, part]
            ).start()
            pltpu.make_async_copy(
                coupling_all.at[block], m_buf.at[slot, pl.ds(part * 384, 384), :], m_sem.at[slot, part]
            ).start()

    start(0, 0)

    def step(p, carry):
        slot = p % 2
        for q in range(1, count):

            @pl.when(p + 1 == q)
            def _():
                start(q, 1 - slot)

        for part in range(2):
            pltpu.make_async_copy(
                sources[0].at[0], s_buf.at[slot, :, pl.ds(part * 384, 384)], s_sem.at[slot, part]
            ).wait()
            pltpu.make_async_copy(
                coupling_all.at[0], m_buf.at[slot, pl.ds(part * 384, 384), :], m_sem.at[slot, part]
            ).wait()
        pieces = []
        for part in range(2):
            for third in range(3):
                tile = (m_index[slot, part] * 3 + third) >> 1
                factor = mask[tile].astype(jnp.float32)
                pieces.append(m_buf[slot, pl.ds(part * 384 + third * 128, 128), :] * factor)
        m_value = jnp.concatenate(pieces, axis=0)
        part_sum = dot3(split(s_buf[slot]), split(m_value), ROWS)
        row_half = p // half_of
        sums[row_half] = sums[row_half] + part_sum
        return carry

    lax.fori_loop(0, count, step, 0)


ORDER = (0, -1, 1, 2)


def first_pairs():
    out = []
    for k, dy in enumerate((0, -1, 1)):
        for unit in (0, 2):
            out.append((k, unit, (ORDER[unit], dy), (ORDER[unit + 1], dy)))
    for k, dx in enumerate((0, -1, 1)):
        for unit in (0, 2):
            out.append((3 + k, unit, (dx, ORDER[unit]), (dx, ORDER[unit + 1])))
    return out


def last_pairs():
    return [
        (0, 0, (ORDER[0], 2), (ORDER[1], 2)),
        (1, 0, (ORDER[2], 2), (ORDER[3], 2)),
        (2, 0, (2, ORDER[0]), (2, ORDER[1])),
        (3, 0, (2, ORDER[2]), (2, ORDER[3])),
    ]


def first_body(where, mask, coupling_all, *rest):
    sources, sums, scratch = rest[:6], rest[6], rest[7:]
    sums[...] = jnp.zeros_like(sums)
    pair_loop(first_pairs(), sources, where, mask, coupling_all, sums, *scratch)


def last_body(where, mask, coupling_all, s0, s1, s2, s3, before, own, diag_here, sep, mine, other, part_var, *scratch):
    sums, scratch = scratch[0], scratch[1:]
    sums[...] = before[...]
    pair_loop(last_pairs(), (s0, s1, s2, s3), where, mask, coupling_all, sums, *scratch)
    row = where[2]
    core = where[3]
    product = jnp.concatenate([sums[0], sums[1]], axis=0)
    sep[...] = -product
    tiles = [own[pl.ds(k * 256, 256), :] * mask[row * 3 + k].astype(jnp.float32) for k in range(3)]
    own_value = jnp.concatenate(tiles, axis=0)
    part_var[...] = diag_here[...] + jnp.sum(own_value * product, axis=0, keepdims=True)
    update = dot3(split(own_value), split(product), COLS)
    for zz in range(4):
        lower = update[zz * 192 : zz * 192 + 96]
        upper = update[zz * 192 + 96 : zz * 192 + 192]

        @pl.when(core == 0)
        def _():
            mine[zz] = lower
            other[zz] = upper

        @pl.when(core != 0)
        def _():
            mine[zz] = upper
            other[zz] = lower


ANY = pl.BlockSpec(memory_space=pl.ANY)
SMEM = pl.BlockSpec(memory_space=pltpu.SMEM)
VMEM = pl.BlockSpec(memory_space=pltpu.VMEM)


def buffers():
    return [
        pltpu.VMEM((2, 384, 768), jnp.float32),
        pltpu.VMEM((2, 768, 768), jnp.float32),
        pltpu.SMEM((2, 2), jnp.int32),
        pltpu.SemaphoreType.DMA((2, 2)),
        pltpu.SemaphoreType.DMA((2, 2)),
    ]


def shape(*dims):
    return jax.ShapeDtypeStruct(dims, jnp.float32)


def local(sigma_top, coupling, child_inverse, tile_mask, obs_node, obs_noise):
    sub = lax.axis_index("sub")
    row = lax.axis_index("row")
    x, y, z, core = sub // 4, sub % 4, row // 2, row % 2
    where = jnp.stack([x, y, row, core]).astype(jnp.int32)
    mask = tile_mask[0]
    coupling_all = lax.all_gather(coupling[0], "row", axis=0, tiled=True).reshape(16, 384, 768)

    a = sigma_top[:384]
    b = sigma_top[384:]
    a_minus = send(a, dx=1)
    b_minus = send(b, dy=1)
    a_plus = send(a, dx=-1)
    b_plus = send(b, dy=-1)
    a_two = jnp.concatenate([send(a_minus[:192], dx=1), send(a_plus[192:], dx=-1)], axis=0)
    b_two = jnp.concatenate([send(b_minus[:192], dy=1), send(b_plus[192:], dy=-1)], axis=0)
    a_line = jnp.stack([a, a_minus, a_plus, a_two])
    b_line = jnp.stack([b, b_minus, b_plus, b_two])
    a_line_minus = send(a_line, dy=1)
    b_line_minus = send(b_line, dx=1)
    a_line_plus = send(a_line, dy=-1)
    b_line_plus = send(b_line, dx=-1)
    a_far0 = send(a_line_minus[:2], dy=1)
    b_far0 = send(b_line_minus[:2], dx=1)
    a_far1 = send(a_line_plus[2:], dy=-1)
    b_far1 = send(b_line_plus[2:], dx=-1)

    sums = pl.pallas_call(
        first_body,
        out_shape=shape(2, 384, 768),
        in_specs=[SMEM, SMEM] + [ANY] * 7,
        out_specs=VMEM,
        scratch_shapes=buffers(),
        compiler_params=pltpu.CompilerParams(vmem_limit_bytes=48 << 20),
        cost_estimate=pl.CostEstimate(flops=16_000_000_000, bytes_accessed=45_000_000, transcendentals=0),
        name="first_pairs",
    )(where, mask, coupling_all, a_line, a_line_minus, a_line_plus, b_line, b_line_minus, b_line_plus)

    inverse = child_inverse[0]
    column = lax.broadcasted_iota(jnp.int32, (96, 768), 1)
    line = lax.broadcasted_iota(jnp.int32, (96, 768), 0) + row * 96
    diag_here = jnp.sum(jnp.where(column == line, inverse, 0.0), axis=0, keepdims=True)
    sep, mine, other, part_var = pl.pallas_call(
        last_body,
        out_shape=(shape(768, 768), shape(4, 96, 768), shape(4, 96, 768), shape(1, 768)),
        in_specs=[SMEM, SMEM] + [ANY] * 5 + [VMEM] * 3,
        out_specs=(VMEM, VMEM, VMEM, VMEM),
        scratch_shapes=[pltpu.VMEM((2, 384, 768), jnp.float32)] + buffers(),
        compiler_params=pltpu.CompilerParams(vmem_limit_bytes=56 << 20),
        cost_estimate=pl.CostEstimate(flops=8_000_000_000, bytes_accessed=25_000_000, transcendentals=0),
        name="last_pairs",
    )(where, mask, coupling_all, a_far0, a_far1, b_far0, b_far1, sums, coupling[0], diag_here)

    half_sum = mine + send(other, dc=1)
    part = part_var + send(part_var, dc=1)
    toward = lambda dz: lax.dynamic_index_in_dim(half_sum, (z + dz) % 4, 0, False)
    part = part + send(part, dz=1) + send(part, dz=-1) + send(part, dz=2)
    block_here = inverse + (toward(0) + send(toward(1), dz=1) + send(toward(-1), dz=-1) + send(toward(2), dz=2))
    by_y = jnp.concatenate([part, send(part, dy=-1), send(part, dy=2), send(part, dy=1)], axis=0)
    by_xy = jnp.stack([by_y, send(by_y, dx=-1), send(by_y, dx=2), send(by_y, dx=1)])
    child = obs_node // 768
    far_x = (child // 4 - x) % 4
    far_y = (child % 4 - y) % 4
    index = (far_x * 4 + far_y) * 768 + obs_node % 768
    loo_var = by_xy.reshape(-1)[index] + obs_noise
    return sep[None], block_here[None], loo_var


def solution(mesh):
    placed = (
        P("row", "sub"),
        P("sub", "row", None),
        P("sub", "row", None),
        P("sub", None),
        P(("sub", "row")),
        P(("sub", "row")),
    )
    return jax.shard_map(
        local,
        mesh=mesh,
        in_specs=placed,
        out_specs=(P("sub", "row", None), P("sub", "row", None), P(("sub", "row"))),
        check_vma=False,
    )
```

time: 450 us -> 195 us (0.43)
  waiting for transfers between devices: 249 us -> 79.6 us
  matrix products: 105 us -> 0 us
  blocking collectives: 63.7 us -> 0 us
  Pallas kernels: 0 us -> 40.9 us
  starting transfers between devices: 0.12 us -> 39.7 us
    all_gather x2 -> x1, waiting for transfers between devices: 220 us -> 4.16 us  [local(): lax.all_gather(coupling[0], 'row', axis=0, tiled=True).reshape(16, 384, 768)]
    dot_general x2 -> x0, matrix products: 105 us -> none  [the longest x1 92.2 us: local(): jnp.dot(lax.all_gather(sigma_top, 'sub', axis=1, tiled=True), gathered, p...]
    ppermute x0 -> x30, waiting for transfers between devices: none -> 74.7 us  [send(): return lax.ppermute(value, AXES, pairs)]
    unnamed x1 -> x0, blocking collectives: 63.7 us -> none
    pallas_call x0 -> x2, Pallas kernels: none -> 40.9 us  [the longest x1 24.1 us: local(): pl.pallas_call(first_body, out_shape=shape(2, 384, 768), in_specs=[SMEM,...]
    ppermute x0 -> x30, starting transfers between devices: none -> 39.6 us  [send(): return lax.ppermute(value, AXES, pairs)]
    reduce_scatter x1 -> x0, waiting for transfers between devices: 28 us -> none  [local(): lax.psum_scatter(lax.dot_general(masked, sep_part, (((0,), (0,)), ((), ()...]
    slice x0 -> x8, local copies, waits for them, and re-layouts: none -> 8.53 us  [the longest x1 2.38 us: local(): b_far1 = send(b_line_plus[2:], dx=-1)]
  transfers between devices with their start and end apart: 3 -> 31, of which waited for: 3 -> 15; matrix products, arithmetic and copies ran while one was open for 1% -> 8% of each run, Pallas kernels for 0% -> 12%
where the time goes in v1:
time: 195 us; the launch traced here: 193 us
  waiting for transfers between devices  79.6 us (41%)
  Pallas kernels  40.9 us (21%)
  starting transfers between devices  39.7 us (20%)
  between operations  14.2 us (7%)
  local copies, waits for them, and re-layouts  13.1 us (7%)
  other arithmetic  5.52 us (3%)
    ppermute x30, waiting for transfers between devices, send(): return lax.ppermute(value, AXES, pairs)  74.7 us
    ppermute x30, starting transfers between devices, send(): return lax.ppermute(value, AXES, pairs)  39.6 us
    pallas_call x1, Pallas kernels, local(): pl.pallas_call(first_body, out_shape=shape(2, 384, 768), in_specs=[SMEM,...  24.1 us
    pallas_call x1, Pallas kernels, local(): pl.pallas_call(last_body, out_shape=(shape(768, 768), shape(4, 96, 768),...  16.9 us
    all_gather x1, waiting for transfers between devices, local(): lax.all_gather(coupling[0], 'row', axis=0, tiled=True).reshape(16, 384, 768)  4.16 us
  transfers between devices with their start and end apart: 31, of which 15 were waited for; matrix products, arithmetic and copies ran while one was open for 8% of the time, Pallas kernels for 12%

profile of v1, /device:TPU:16, one launch (start us, length us, event | category | flops | bytes accessed | tf_op | source)
XLA Modules:
  0.0 193.0 jit_solution(7292913355844165091)
XLA Ops:
  7.2 0.7 all-gather.3.cloned.1.call-update
  8.6 1.4 collective-permute-start.8
  9.9 0.7 collective-permute-start.9
  10.7 1.5 collective-permute-start
  12.2 1.7 collective-permute-start.1
  13.9 9.8 %collective-permute-done.8 = f32[384,384]{1,0:T(8,128)S(1)} collective-permute-done((f32[384,384]{1,0:T(8,128)S(1)}, f32[384,384]{1,0:T(8,128)S(1)}, u32[]{:S(2)}, u32[]{:S(2)}) %collective-permute-start.8) | collective-permute-done | bytes 589856 | tf_op jit(solution)/shard_map/ppermute | solution.py:24
  23.8 1.4 collective-permute-start.10
  25.1 0.8 collective-permute-start.11
  26.4 1.1 collective-permute-start.2
  27.6 2.3 %collective-permute-start.3 = (f32[192,384]{1,0:T(8,128)S(1)}, f32[192,384]{1,0:T(8,128)S(1)}, u32[]{:S(2)}, u32[]{:S(2)}) collective-permute-start(f32[192,384]{1,0:T(8,128)S(1)} %slice.43), channel_id=1, source_target_pairs={{0,96},{1,97},{2,98},{3,99},{4,100},{5,101},{6,102},{7,103},{8,104... | collective-permute-start | bytes 884744 | tf_op jit(solution)/shard_map/ppermute | solution.py:24
  29.8 1.9 collective-permute-done.10
  31.7 1.1 collective-permute-done.11
  32.8 1.6 pad_maximum_fusion.1.rest_3_
  34.4 1.5 collective-permute-start.12
  35.9 1.7 collective-permute-start.14
  37.9 2.9 %collective-permute-start.4 = (f32[4,384,384]{2,1,0:T(8,128)S(1)}, f32[4,384,384]{2,1,0:T(8,128)}, u32[]{:S(2)}, u32[]{:S(2)}) collective-permute-start(f32[4,384,384]{2,1,0:T(8,128)S(1)} %pad_maximum_fusion.rest_0_), channel_id=1, source_target_pairs={{0,8},{1,9},{2,10},{3,11},{4,12},{5,13},{6,14},{7,15},{8,16},{9,17... | collective-permute-start | bytes 7077896 | tf_op jit(solution)/shard_map/ppermute | solution.py:24
  40.9 0.6 broadcast_in_dim.17.diag_here
  41.6 45.4 %collective-permute-done.12.rest_4_ = f32[4,384,384]{2,1,0:T(8,128)} collective-permute-done((f32[4,384,384]{2,1,0:T(8,128)}, f32[4,384,384]{2,1,0:T(8,128)}, u32[]{:S(2)}, u32[]{:S(2)}) %collective-permute-start.12) | collective-permute-done | bytes 2359328 | tf_op jit(solution)/shard_map/ppermute | solution.py:24
  86.9 1.3 slice.48
  88.7 2.4 %slice.49 = f32[2,384,384]{2,1,0:T(8,128)} slice(f32[4,384,384]{2,1,0:T(8,128)} %collective-permute-done.14.rest_5_), slice={[2:4], [0:384], [0:384]} | slice | bytes 2359296 | tf_op jit(solution)/shard_map/slice | solution.py:194
  91.0 3.0 %collective-permute-start.15 = (f32[2,384,384]{2,1,0:T(8,128)}, f32[2,384,384]{2,1,0:T(8,128)}, u32[]{:S(2)}, u32[]{:S(2)}) collective-permute-start(f32[2,384,384]{2,1,0:T(8,128)} %slice.49), channel_id=1, source_target_pairs={{0,96},{1,97},{2,98},{3,99},{4,100},{5,101},{6,102},{7,103},{8,104... | collective-permute-start | bytes 3538952 | tf_op jit(solution)/shard_map/ppermute | solution.py:24
  94.0 2.4 %slice.44 = f32[2,384,384]{2,1,0:T(8,128)} slice(f32[4,384,384]{2,1,0:T(8,128)} %collective-permute-done.4.rest_1_), slice={[0:2], [0:384], [0:384]} | slice | bytes 2359296 | tf_op jit(solution)/shard_map/slice | solution.py:191
  96.4 3.0 %collective-permute-start.5 = (f32[2,384,384]{2,1,0:T(8,128)}, f32[2,384,384]{2,1,0:T(8,128)}, u32[]{:S(2)}, u32[]{:S(2)}) collective-permute-start(f32[2,384,384]{2,1,0:T(8,128)} %slice.44), channel_id=1, source_target_pairs={{0,8},{1,9},{2,10},{3,11},{4,12},{5,13},{6,14},{7,15},{8,16},{9,17... | collective-permute-start | bytes 3538952 | tf_op jit(solution)/shard_map/ppermute | solution.py:24
  99.4 2.4 %slice.45 = f32[2,384,384]{2,1,0:T(8,128)} slice(f32[4,384,384]{2,1,0:T(8,128)} %collective-permute-done.6.rest_2_), slice={[2:4], [0:384], [0:384]} | slice | bytes 2359296 | tf_op jit(solution)/shard_map/slice | solution.py:193
  101.8 4.2 %all-gather.3.cloned.1.call-done = f32[1,6144,768]{2,1,0:T(8,128)} async-done(((f32[1,768,768]{2,1,0:T(8,128)}), f32[1,6144,768]{2,1,0:T(8,128)}) %all-gather.3.cloned.1.call-update) | async-done | bytes 18874384 | tf_op jit(solution)/shard_map/all_gather | solution.py:175
  105.9 24.1 %first_pairs.1.before = f32[2,384,768]{2,1,0:T(8,128)S(1)} custom-call(s32[4]{0:T(128)S(1)} %pad_add_fusion.where, s32[24]{0:T(128)S(1)} %bitcast.49, f32[16,384,768]{2,1,0:T(8,128)} %bitcast.58, f32[4,384,384]{2,1,0:T(8,128)S(1)} %pad_maximum_fusion.rest_0_, f32[4,384,384]{2,1,0:T(8,128)} %collective-permute-done.4.rest_1_, ...), custom_call_target="tpu_custom_call" | custom-call | flops 16000000000 | bytes 45000000 | tf_op jit(solution)/shard_map/first_pairs/pallas_call | solution.py:196
  130.0 1.4 copy-done.2
  131.5 16.9 %last_pairs.1 = (f32[768,768]{1,0:T(8,128)}, f32[4,96,768]{2,1,0:T(8,128)}, f32[4,96,768]{2,1,0:T(8,128)}, f32[1,768]{1,0:T(1,128)}) custom-call(s32[4]{0:T(128)} %copy-done, s32[24]{0:T(128)} %bitcast.48, f32[16,384,768]{2,1,0:T(8,128)} %bitcast.59, f32[2,384,384]{2,1,0:T(8,128)} %collective-permute-done.5.s0, f32[2,384,384]{2,1,0:T(8,128)} %collective-permute-done.7.s1, ...), custom_call_target="tpu_custom_call" | custom-call | flops 8000000000 | bytes 25000000 | tf_op jit(solution)/shard_map/last_pairs/pallas_call | solution.py:211
  148.9 2.5 %collective-permute-done.20 = f32[1,768]{1,0:T(1,128)S(1)} collective-permute-done((f32[1,768]{1,0:T(1,128)}, f32[1,768]{1,0:T(1,128)S(1)}, u32[]{:S(2)}, u32[]{:S(2)}) %collective-permute-start.20) | collective-permute-done | bytes 3104 | tf_op jit(solution)/shard_map/ppermute | solution.py:24
  151.5 0.7 add.132
  152.2 1.1 collective-permute-start.21
  153.3 2.1 %collective-permute-start.22 = (f32[1,768]{1,0:T(1,128)S(1)}, f32[1,768]{1,0:T(1,128)S(1)}, u32[]{:S(2)}, u32[]{:S(2)}) collective-permute-start(f32[1,768]{1,0:T(1,128)S(1)} %add.132), channel_id=1, source_target_pairs={{0,6},{1,7},{2,0},{3,1},{4,2},{5,3},{6,4},{7,5},{8,14},{9,15},{10,... | collective-permute-start | bytes 9224 | tf_op jit(solution)/shard_map/ppermute | solution.py:24
  155.4 1.2 collective-permute-start.23
  157.0 3.5 %collective-permute-done.23 = f32[1,768]{1,0:T(1,128)S(1)} collective-permute-done((f32[1,768]{1,0:T(1,128)S(1)}, f32[1,768]{1,0:T(1,128)S(1)}, u32[]{:S(2)}, u32[]{:S(2)}) %collective-permute-start.23) | collective-permute-done | bytes 3104 | tf_op jit(solution)/shard_map/ppermute | solution.py:24
  160.5 0.6 collective-permute-start.24
  161.1 2.7 %collective-permute-start.25 = (f32[1,768]{1,0:T(1,128)S(1)}, f32[1,768]{1,0:T(1,128)S(1)}, u32[]{:S(2)}, u32[]{:S(2)}) collective-permute-start(f32[1,768]{1,0:T(1,128)S(1)} %add_add_fusion), channel_id=1, source_target_pairs={{0,16},{1,17},{2,18},{3,19},{4,20},{5,21},{6,22},{7,23},{8,24},{9,... | collective-permute-start | bytes 9224 | tf_op jit(solution)/shard_map/ppermute | solution.py:24
  164.2 2.1 %collective-permute-done.25 = f32[1,768]{1,0:T(1,128)S(1)} collective-permute-done((f32[1,768]{1,0:T(1,128)S(1)}, f32[1,768]{1,0:T(1,128)S(1)}, u32[]{:S(2)}, u32[]{:S(2)}) %collective-permute-start.25) | collective-permute-done | bytes 3104 | tf_op jit(solution)/shard_map/ppermute | solution.py:24
  166.2 1.2 collective-permute-done.26
  167.5 2.8 %collective-permute-start.27 = (f32[4,768]{1,0:T(4,128)S(1)}, f32[4,768]{1,0:T(4,128)S(1)}, u32[]{:S(2)}, u32[]{:S(2)}) collective-permute-start(f32[4,768]{1,0:T(4,128)S(1)} %get-tuple-element.19), channel_id=1, source_target_pairs={{0,96},{1,97},{2,98},{3,99},{4,100},{5,101},{6,102},{7,103},{8,104... | collective-permute-start | bytes 36872 | tf_op jit(solution)/shard_map/ppermute | solution.py:24
  170.2 1.4 add.116
  171.9 3.2 %collective-permute-start.18 = (f32[96,768]{1,0:T(8,128)S(1)}, f32[96,768]{1,0:T(8,128)S(1)}, u32[]{:S(2)}, u32[]{:S(2)}) collective-permute-start(f32[96,768]{1,0:T(8,128)S(1)} %get-tuple-element.13), channel_id=1, source_target_pairs={{0,6},{1,7},{2,0},{3,1},{4,2},{5,3},{6,4},{7,5},{8,14},{9,15},{10,... | collective-permute-start | bytes 884744 | tf_op jit(solution)/shard_map/ppermute | solution.py:24
  175.1 0.9 collective-permute-start.28
  176.1 0.9 collective-permute-start.29
  176.9 3.5 %collective-permute-done.28 = f32[4,768]{1,0:T(4,128)S(1)} collective-permute-done((f32[4,768]{1,0:T(4,128)S(1)}, f32[4,768]{1,0:T(4,128)S(1)}, u32[]{:S(2)}, u32[]{:S(2)}) %collective-permute-start.28) | collective-permute-done | bytes 12320 | tf_op jit(solution)/shard_map/ppermute | solution.py:24
  181.0 1.7 gather_fusion
  182.8 0.6 add.144
  183.3 2.1 %collective-permute-done.17 = f32[96,768]{1,0:T(8,128)S(1)} collective-permute-done((f32[96,768]{1,0:T(8,128)S(1)}, f32[96,768]{1,0:T(8,128)S(1)}, u32[]{:S(2)}, u32[]{:S(2)}) %collective-permute-start.17) | collective-permute-done | bytes 294944 | tf_op jit(solution)/shard_map/ppermute | solution.py:24
  185.4 0.8 fusion.3
  (62 shorter events, 4.2 us)
Async XLA Ops:
  7.2 1.3 copy-start.3
  7.2 98.7 %all-gather.3.cloned.1.call-start = ((), (), s32[]{:S(2)}) async-start(), calls=%async_computation | async-start | bytes 21233664 | tf_op jit(solution)/shard_map/all_gather | solution.py:175
  8.6 15.1 %collective-permute-start.8 = (f32[384,384]{1,0:T(8,128)S(1)}, f32[384,384]{1,0:T(8,128)S(1)}, u32[]{:S(2)}, u32[]{:S(2)}) collective-permute-start(f32[384,384]{1,0:T(8,128)S(1)} %get-tuple-element.16), channel_id=1, source_target_pairs={{0,8},{1,9},{2,10},{3,11},{4,12},{5,13},{6,14},{7,15},{8,16},{9,17... | collective-permute-start | bytes 1769480 | tf_op jit(solution)/shard_map/ppermute | solution.py:24
  9.9 15.2 %collective-permute-start.9 = (f32[384,384]{1,0:T(8,128)S(1)}, f32[384,384]{1,0:T(8,128)S(1)}, u32[]{:S(2)}, u32[]{:S(2)}) collective-permute-start(f32[384,384]{1,0:T(8,128)S(1)} %get-tuple-element.16), channel_id=1, source_target_pairs={{0,24},{1,25},{2,26},{3,27},{4,28},{5,29},{6,30},{7,31},{8,0},{9,1... | collective-permute-start | bytes 1769480 | tf_op jit(solution)/shard_map/ppermute | solution.py:24
  10.7 15.7 %collective-permute-start = (f32[384,384]{1,0:T(8,128)S(1)}, f32[384,384]{1,0:T(8,128)S(1)}, u32[]{:S(2)}, u32[]{:S(2)}) collective-permute-start(f32[384,384]{1,0:T(8,128)S(1)} %get-tuple-element.17), channel_id=1, source_target_pairs={{0,32},{1,33},{2,34},{3,35},{4,36},{5,37},{6,38},{7,39},{8,40},{9,... | collective-permute-start | bytes 1769480 | tf_op jit(solution)/shard_map/ppermute | solution.py:24
  12.2 15.4 %collective-permute-start.1 = (f32[384,384]{1,0:T(8,128)S(1)}, f32[384,384]{1,0:T(8,128)S(1)}, u32[]{:S(2)}, u32[]{:S(2)}) collective-permute-start(f32[384,384]{1,0:T(8,128)S(1)} %get-tuple-element.17), channel_id=1, source_target_pairs={{0,96},{1,97},{2,98},{3,99},{4,100},{5,101},{6,102},{7,103},{8,104... | collective-permute-start | bytes 1769480 | tf_op jit(solution)/shard_map/ppermute | solution.py:24
  23.8 7.9 %collective-permute-start.10 = (f32[192,384]{1,0:T(8,128)S(1)}, f32[192,384]{1,0:T(8,128)S(1)}, u32[]{:S(2)}, u32[]{:S(2)}) collective-permute-start(f32[192,384]{1,0:T(8,128)S(1)} %slice.46), channel_id=1, source_target_pairs={{0,8},{1,9},{2,10},{3,11},{4,12},{5,13},{6,14},{7,15},{8,16},{9,17... | collective-permute-start | bytes 884744 | tf_op jit(solution)/shard_map/ppermute | solution.py:24
  25.1 7.7 %collective-permute-start.11 = (f32[192,384]{1,0:T(8,128)S(1)}, f32[192,384]{1,0:T(8,128)S(1)}, u32[]{:S(2)}, u32[]{:S(2)}) collective-permute-start(f32[192,384]{1,0:T(8,128)S(1)} %slice.47), channel_id=1, source_target_pairs={{0,24},{1,25},{2,26},{3,27},{4,28},{5,29},{6,30},{7,31},{8,0},{9,1... | collective-permute-start | bytes 884744 | tf_op jit(solution)/shard_map/ppermute | solution.py:24
  26.4 11.2 %collective-permute-start.2 = (f32[192,384]{1,0:T(8,128)S(1)}, f32[192,384]{1,0:T(8,128)S(1)}, u32[]{:S(2)}, u32[]{:S(2)}) collective-permute-start(f32[192,384]{1,0:T(8,128)S(1)} %slice.42), channel_id=1, source_target_pairs={{0,32},{1,33},{2,34},{3,35},{4,36},{5,37},{6,38},{7,39},{8,40},{9,... | collective-permute-start | bytes 884744 | tf_op jit(solution)/shard_map/ppermute | solution.py:24
  27.6 10.1 %collective-permute-start.3 = (f32[192,384]{1,0:T(8,128)S(1)}, f32[192,384]{1,0:T(8,128)S(1)}, u32[]{:S(2)}, u32[]{:S(2)}) collective-permute-start(f32[192,384]{1,0:T(8,128)S(1)} %slice.43), channel_id=1, source_target_pairs={{0,96},{1,97},{2,98},{3,99},{4,100},{5,101},{6,102},{7,103},{8,104... | collective-permute-start | bytes 884744 | tf_op jit(solution)/shard_map/ppermute | solution.py:24
  34.4 52.5 %collective-permute-start.12 = (f32[4,384,384]{2,1,0:T(8,128)}, f32[4,384,384]{2,1,0:T(8,128)}, u32[]{:S(2)}, u32[]{:S(2)}) collective-permute-start(f32[4,384,384]{2,1,0:T(8,128)} %pad_maximum_fusion.1.rest_3_), channel_id=1, source_target_pairs={{0,32},{1,33},{2,34},{3,35},{4,36},{5,37},{6,38},{7,39},{8,40},{9,... | collective-permute-start | bytes 7077896 | tf_op jit(solution)/shard_map/ppermute | solution.py:24
  35.9 52.8 %collective-permute-start.14 = (f32[4,384,384]{2,1,0:T(8,128)}, f32[4,384,384]{2,1,0:T(8,128)}, u32[]{:S(2)}, u32[]{:S(2)}) collective-permute-start(f32[4,384,384]{2,1,0:T(8,128)} %pad_maximum_fusion.1.rest_3_), channel_id=1, source_target_pairs={{0,96},{1,97},{2,98},{3,99},{4,100},{5,101},{6,102},{7,103},{8,104... | collective-permute-start | bytes 7077896 | tf_op jit(solution)/shard_map/ppermute | solution.py:24
  37.7 3.1 %copy-start.4 = (f32[1,96,768]{2,1,0:T(8,128)S(1)}, f32[1,96,768]{2,1,0:T(8,128)}, u32[]{:S(2)}) copy-start(f32[1,96,768]{2,1,0:T(8,128)} %param.8) | copy-start | bytes 884740
  37.9 56.1 %collective-permute-start.4 = (f32[4,384,384]{2,1,0:T(8,128)S(1)}, f32[4,384,384]{2,1,0:T(8,128)}, u32[]{:S(2)}, u32[]{:S(2)}) collective-permute-start(f32[4,384,384]{2,1,0:T(8,128)S(1)} %pad_maximum_fusion.rest_0_), channel_id=1, source_target_pairs={{0,8},{1,9},{2,10},{3,11},{4,12},{5,13},{6,14},{7,15},{8,16},{9,17... | collective-permute-start | bytes 7077896 | tf_op jit(solution)/shard_map/ppermute | solution.py:24
  40.8 58.6 %collective-permute-start.6 = (f32[4,384,384]{2,1,0:T(8,128)S(1)}, f32[4,384,384]{2,1,0:T(8,128)}, u32[]{:S(2)}, u32[]{:S(2)}) collective-permute-start(f32[4,384,384]{2,1,0:T(8,128)S(1)} %pad_maximum_fusion.rest_0_), channel_id=1, source_target_pairs={{0,24},{1,25},{2,26},{3,27},{4,28},{5,29},{6,30},{7,31},{8,0},{9,1... | collective-permute-start | bytes 7077896 | tf_op jit(solution)/shard_map/ppermute | solution.py:24
  41.6 64.3 %copy-start = (s32[4]{0:T(128)}, s32[4]{0:T(128)S(1)}, u32[]{:S(2)}) copy-start(s32[4]{0:T(128)S(1)} %pad_add_fusion.where) | copy-start | bytes 52
  88.3 43.1 %collective-permute-start.13 = (f32[2,384,384]{2,1,0:T(8,128)S(1)}, f32[2,384,384]{2,1,0:T(8,128)}, u32[]{:S(2)}, u32[]{:S(2)}) collective-permute-start(f32[2,384,384]{2,1,0:T(8,128)S(1)} %slice.48), channel_id=1, source_target_pairs={{0,32},{1,33},{2,34},{3,35},{4,36},{5,37},{6,38},{7,39},{8,40},{9,... | collective-permute-start | bytes 3538952 | tf_op jit(solution)/shard_map/ppermute | solution.py:24
  91.0 14.9 %copy-start.1 = (s32[1,24]{1,0:T(1,128)S(1)}, s32[1,24]{1,0:T(1,128)}, u32[]{:S(2)}) copy-start(s32[1,24]{1,0:T(1,128)} %param.9) | copy-start | bytes 292
  91.0 40.4 %collective-permute-start.15 = (f32[2,384,384]{2,1,0:T(8,128)}, f32[2,384,384]{2,1,0:T(8,128)}, u32[]{:S(2)}, u32[]{:S(2)}) collective-permute-start(f32[2,384,384]{2,1,0:T(8,128)} %slice.49), channel_id=1, source_target_pairs={{0,96},{1,97},{2,98},{3,99},{4,100},{5,101},{6,102},{7,103},{8,104... | collective-permute-start | bytes 3538952 | tf_op jit(solution)/shard_map/ppermute | solution.py:24
  96.4 35.1 %collective-permute-start.5 = (f32[2,384,384]{2,1,0:T(8,128)}, f32[2,384,384]{2,1,0:T(8,128)}, u32[]{:S(2)}, u32[]{:S(2)}) collective-permute-start(f32[2,384,384]{2,1,0:T(8,128)} %slice.44), channel_id=1, source_target_pairs={{0,8},{1,9},{2,10},{3,11},{4,12},{5,13},{6,14},{7,15},{8,16},{9,17... | collective-permute-start | bytes 3538952 | tf_op jit(solution)/shard_map/ppermute | solution.py:24
  101.8 29.7 %collective-permute-start.7 = (f32[2,384,384]{2,1,0:T(8,128)}, f32[2,384,384]{2,1,0:T(8,128)}, u32[]{:S(2)}, u32[]{:S(2)}) collective-permute-start(f32[2,384,384]{2,1,0:T(8,128)} %slice.45), channel_id=1, source_target_pairs={{0,24},{1,25},{2,26},{3,27},{4,28},{5,29},{6,30},{7,31},{8,0},{9,1... | collective-permute-start | bytes 3538952 | tf_op jit(solution)/shard_map/ppermute | solution.py:24
  130.0 1.4 copy-start.2
  148.3 21.9 %collective-permute-start.16 = (f32[4,96,768]{2,1,0:T(8,128)}, f32[4,96,768]{2,1,0:T(8,128)S(1)}, u32[]{:S(2)}, u32[]{:S(2)}) collective-permute-start(f32[4,96,768]{2,1,0:T(8,128)} %get-tuple-element.9), channel_id=1, source_target_pairs={{0,1},{1,0},{2,3},{3,2},{4,5},{5,4},{6,7},{7,6},{8,9},{9,8},{10,11... | collective-permute-start | bytes 3538952 | tf_op jit(solution)/shard_map/ppermute | solution.py:24
  148.7 2.8 %collective-permute-start.20 = (f32[1,768]{1,0:T(1,128)}, f32[1,768]{1,0:T(1,128)S(1)}, u32[]{:S(2)}, u32[]{:S(2)}) collective-permute-start(f32[1,768]{1,0:T(1,128)} %get-tuple-element.10), channel_id=1, source_target_pairs={{0,1},{1,0},{2,3},{3,2},{4,5},{5,4},{6,7},{7,6},{8,9},{9,8},{10,11... | collective-permute-start | bytes 9224 | tf_op jit(solution)/shard_map/ppermute | solution.py:24
  152.2 4.8 %collective-permute-start.21 = (f32[1,768]{1,0:T(1,128)S(1)}, f32[1,768]{1,0:T(1,128)S(1)}, u32[]{:S(2)}, u32[]{:S(2)}) collective-permute-start(f32[1,768]{1,0:T(1,128)S(1)} %add.132), channel_id=1, source_target_pairs={{0,2},{1,3},{2,4},{3,5},{4,6},{5,7},{6,0},{7,1},{8,10},{9,11},{10,... | collective-permute-start | bytes 9224 | tf_op jit(solution)/shard_map/ppermute | solution.py:24
  153.3 3.7 %collective-permute-start.22 = (f32[1,768]{1,0:T(1,128)S(1)}, f32[1,768]{1,0:T(1,128)S(1)}, u32[]{:S(2)}, u32[]{:S(2)}) collective-permute-start(f32[1,768]{1,0:T(1,128)S(1)} %add.132), channel_id=1, source_target_pairs={{0,6},{1,7},{2,0},{3,1},{4,2},{5,3},{6,4},{7,5},{8,14},{9,15},{10,... | collective-permute-start | bytes 9224 | tf_op jit(solution)/shard_map/ppermute | solution.py:24
  155.4 5.1 %collective-permute-start.23 = (f32[1,768]{1,0:T(1,128)S(1)}, f32[1,768]{1,0:T(1,128)S(1)}, u32[]{:S(2)}, u32[]{:S(2)}) collective-permute-start(f32[1,768]{1,0:T(1,128)S(1)} %add.132), channel_id=1, source_target_pairs={{0,4},{1,5},{2,6},{3,7},{4,0},{5,1},{6,2},{7,3},{8,12},{9,13},{10,... | collective-permute-start | bytes 9224 | tf_op jit(solution)/shard_map/ppermute | solution.py:24
  160.5 3.7 %collective-permute-start.24 = (f32[1,768]{1,0:T(1,128)S(1)}, f32[1,768]{1,0:T(1,128)S(1)}, u32[]{:S(2)}, u32[]{:S(2)}) collective-permute-start(f32[1,768]{1,0:T(1,128)S(1)} %add_add_fusion), channel_id=1, source_target_pairs={{0,24},{1,25},{2,26},{3,27},{4,28},{5,29},{6,30},{7,31},{8,0},{9,1... | collective-permute-start | bytes 9224 | tf_op jit(solution)/shard_map/ppermute | solution.py:24
  161.1 5.1 %collective-permute-start.25 = (f32[1,768]{1,0:T(1,128)S(1)}, f32[1,768]{1,0:T(1,128)S(1)}, u32[]{:S(2)}, u32[]{:S(2)}) collective-permute-start(f32[1,768]{1,0:T(1,128)S(1)} %add_add_fusion), channel_id=1, source_target_pairs={{0,16},{1,17},{2,18},{3,19},{4,20},{5,21},{6,22},{7,23},{8,24},{9,... | collective-permute-start | bytes 9224 | tf_op jit(solution)/shard_map/ppermute | solution.py:24
  163.8 3.6 %collective-permute-start.26 = (f32[1,768]{1,0:T(1,128)S(1)}, f32[1,768]{1,0:T(1,128)S(1)}, u32[]{:S(2)}, u32[]{:S(2)}) collective-permute-start(f32[1,768]{1,0:T(1,128)S(1)} %add_add_fusion), channel_id=1, source_target_pairs={{0,8},{1,9},{2,10},{3,11},{4,12},{5,13},{6,14},{7,15},{8,16},{9,17... | collective-permute-start | bytes 9224 | tf_op jit(solution)/shard_map/ppermute | solution.py:24
  167.5 8.6 %collective-permute-start.27 = (f32[4,768]{1,0:T(4,128)S(1)}, f32[4,768]{1,0:T(4,128)S(1)}, u32[]{:S(2)}, u32[]{:S(2)}) collective-permute-start(f32[4,768]{1,0:T(4,128)S(1)} %get-tuple-element.19), channel_id=1, source_target_pairs={{0,96},{1,97},{2,98},{3,99},{4,100},{5,101},{6,102},{7,103},{8,104... | collective-permute-start | bytes 36872 | tf_op jit(solution)/shard_map/ppermute | solution.py:24
  170.2 4.9 %copy-start.6 = (s32[256]{0:T(256)S(1)}, s32[256]{0:T(256)}, u32[]{:S(2)}) copy-start(s32[256]{0:T(256)} %param.10) | copy-start | bytes 3076
  171.7 11.1 %copy-start.7 = (f32[256]{0:T(256)S(1)}, f32[256]{0:T(256)}, u32[]{:S(2)}) copy-start(f32[256]{0:T(256)} %param.11) | copy-start | bytes 3076
  171.7 13.7 %copy-start.5 = (f32[1,96,768]{2,1,0:T(8,128)S(1)}, f32[1,96,768]{2,1,0:T(8,128)}, u32[]{:S(2)}) copy-start(f32[1,96,768]{2,1,0:T(8,128)} %param.8) | copy-start | bytes 884740
  171.8 13.6 %collective-permute-start.17 = (f32[96,768]{1,0:T(8,128)S(1)}, f32[96,768]{1,0:T(8,128)S(1)}, u32[]{:S(2)}, u32[]{:S(2)}) collective-permute-start(f32[96,768]{1,0:T(8,128)S(1)} %get-tuple-element.11), channel_id=1, source_target_pairs={{0,2},{1,3},{2,4},{3,5},{4,6},{5,7},{6,0},{7,1},{8,10},{9,11},{10,... | collective-permute-start | bytes 884744 | tf_op jit(solution)/shard_map/ppermute | solution.py:24
  171.9 13.5 %collective-permute-start.18 = (f32[96,768]{1,0:T(8,128)S(1)}, f32[96,768]{1,0:T(8,128)S(1)}, u32[]{:S(2)}, u32[]{:S(2)}) collective-permute-start(f32[96,768]{1,0:T(8,128)S(1)} %get-tuple-element.13), channel_id=1, source_target_pairs={{0,6},{1,7},{2,0},{3,1},{4,2},{5,3},{6,4},{7,5},{8,14},{9,15},{10,... | collective-permute-start | bytes 884744 | tf_op jit(solution)/shard_map/ppermute | solution.py:24
  175.1 10.3 %collective-permute-start.19 = (f32[96,768]{1,0:T(8,128)S(1)}, f32[96,768]{1,0:T(8,128)S(1)}, u32[]{:S(2)}, u32[]{:S(2)}) collective-permute-start(f32[96,768]{1,0:T(8,128)S(1)} %get-tuple-element.12), channel_id=1, source_target_pairs={{0,4},{1,5},{2,6},{3,7},{4,0},{5,1},{6,2},{7,3},{8,12},{9,13},{10,... | collective-permute-start | bytes 884744 | tf_op jit(solution)/shard_map/ppermute | solution.py:24
  175.1 5.3 %collective-permute-start.28 = (f32[4,768]{1,0:T(4,128)S(1)}, f32[4,768]{1,0:T(4,128)S(1)}, u32[]{:S(2)}, u32[]{:S(2)}) collective-permute-start(f32[4,768]{1,0:T(4,128)S(1)} %get-tuple-element.19), channel_id=1, source_target_pairs={{0,64},{1,65},{2,66},{3,67},{4,68},{5,69},{6,70},{7,71},{8,72},{9,... | collective-permute-start | bytes 36872 | tf_op jit(solution)/shard_map/ppermute | solution.py:24
  176.1 4.9 %collective-permute-start.29 = (f32[4,768]{1,0:T(4,128)S(1)}, f32[4,768]{1,0:T(4,128)S(1)}, u32[]{:S(2)}, u32[]{:S(2)}) collective-permute-start(f32[4,768]{1,0:T(4,128)S(1)} %get-tuple-element.19), channel_id=1, source_target_pairs={{0,32},{1,33},{2,34},{3,35},{4,36},{5,37},{6,38},{7,39},{8,40},{9,... | collective-permute-start | bytes 36872 | tf_op jit(solution)/shard_map/ppermute | solution.py:24
Sparse Core Ops, SparseCore 0:
  9.7 96.1 all-gather.2

commit v2 on v0

v2 whole, which is shorter than its diff:
```python
import jax
import jax.numpy as jnp
from jax import lax
from jax.experimental import pallas as pl
from jax.experimental.pallas import tpu as pltpu
from jax.sharding import PartitionSpec as P

AXES = ("sub", "row")
SHORT = jnp.bfloat16
FULL = jnp.float32


def place(x, y, z, c):
    return (x % 4) * 32 + (y % 4) * 8 + (z % 4) * 2 + c % 2


def send(value, dx=0, dy=0, dz=0, dc=0, turn=False):
    pairs = []
    for x in range(4):
        for y in range(4):
            for z in range(4):
                for c in range(2):
                    way = -1 if turn and c else 1
                    pairs.append((place(x, y, z, c), place(x + way * dx, y + way * dy, z + way * dz, c + dc)))
    return lax.ppermute(value, AXES, pairs)


def ring(value, axis, step, name):
    with jax.named_scope(name):
        return send(value, turn=True, **{"d" + axis: step})


def swap(value, name="swap"):
    with jax.named_scope(name):
        return send(value, dc=1)


def after(value, *earlier):
    return lax.optimization_barrier((value,) + earlier)[0]


def split(value):
    high = value.astype(SHORT)
    low = (value - high.astype(FULL)).astype(SHORT)
    return high, low


def dot3(a, b, dims):
    a_high, a_low = a
    b_high, b_low = b
    one = lambda u, v: lax.dot_general(u, v, (dims, ((), ())), preferred_element_type=FULL)
    return one(a_high, b_high) + (one(a_low, b_high) + one(a_high, b_low))


ROWS = ((1,), (0,))
COLS = ((0,), (0,))

LINES = ("a0", "a1", "a2", "a3", "b0", "b1", "b2", "b3")


def work_table(x, y, z, core, way):
    unit = jnp.arange(32, dtype=jnp.int32)
    group, line, spot = unit // 16, unit // 4 % 4, unit % 4
    step = lambda k: jnp.where(k == 3, 2, jnp.where(k == 0, 0, 2 * k - 3))
    x_step = jnp.where(group == 0, step(spot), step(line))
    y_step = jnp.where(group == 0, step(line), step(spot))
    at_x = (x + way * x_step) & 3
    at_y = (y + way * y_step) & 3
    far = ((at_x - z) * way) & 3
    other = (at_y >> 1) ^ core
    late = (far == 3) | ((far == 2) & (other == 1))
    array = jnp.where(far == 0, other, jnp.where(far == 1, 2 + other, jnp.where(far == 2, 3 + other, 4 + other)))
    begin = jnp.where((far == 2), 2, 0)
    half = array * 4 + begin + (at_y & 1)
    rank = jnp.where(line == 3, 2, late.astype(jnp.int32))
    early = jnp.sum((rank.reshape(2, 16) == 0).astype(jnp.int32), axis=1)
    key = (group * 3 + rank) * 32 + unit
    order = jnp.sum((key[None, :] < key[:, None]).astype(jnp.int32), axis=1)
    here = (order[None, :] == unit[:, None]).astype(jnp.int32)
    pick = lambda v: jnp.sum(here * v[None, :], axis=1)
    return jnp.stack([pick(unit), pick(half), pick(at_x * 4 + at_y)]), early


def pair_loop(begin, end, refs, table, mask, sums, s_buf, m_buf, spot, s_sem, m_sem):
    first_group = end[0] - begin[0]
    count = first_group + end[1] - begin[1]

    def start(q, slot):
        group = jnp.where(q < first_group, 0, 1)
        pair = jnp.where(q < first_group, begin[0] + q, begin[1] + q - first_group)
        spot[slot, 2] = group
        for part in range(2):
            entry = group * 16 + pair * 2 + part
            unit = table[0, entry]
            half = table[1, entry]
            spot[slot, part] = table[2, entry]
            s_target = s_buf.at[slot, :, pl.ds(part * 384, 384)]
            m_target = m_buf.at[slot, pl.ds(part * 384, 384), :]
            for number, name in enumerate(LINES):
                if name in refs:

                    @pl.when(unit >> 2 == number)
                    def _():
                        pltpu.make_async_copy(refs[name].at[unit & 3], s_target, s_sem.at[slot, part]).start()

            for number, name in enumerate(("own", "sib", "za", "zb", "zs", "zt")):
                if name in refs:

                    @pl.when(half >> 2 == number)
                    def _():
                        pltpu.make_async_copy(refs[name].at[half & 3], m_target, m_sem.at[slot, part]).start()

    def finish(slot):
        for part in range(2):
            target = s_buf.at[slot, :, pl.ds(part * 384, 384)]
            pltpu.make_async_copy(refs["a0"].at[0], target, s_sem.at[slot, part]).wait()
            target = m_buf.at[slot, pl.ds(part * 384, 384), :]
            pltpu.make_async_copy(refs["own"].at[0], target, m_sem.at[slot, part]).wait()
        pieces = []
        for part in range(2):
            block = spot[slot, part]
            for third in range(3):
                factor = mask[(block * 3 + third) >> 1].astype(FULL)
                pieces.append(m_buf[slot, pl.ds(part * 384 + third * 128, 128), :] * factor)
        part_sum = dot3(split(s_buf[slot]), split(jnp.concatenate(pieces, axis=0)), ROWS)
        group = spot[slot, 2]
        sums[group] = sums[group] + part_sum

    def step(p, carry):
        @pl.when(p < count)
        def _():
            start(p, p % 2)

        @pl.when(p > 0)
        def _():
            finish((p + 1) % 2)

        return carry

    lax.fori_loop(0, jnp.where(count > 0, count + 1, 0), step, 0)


HBM = pl.BlockSpec(memory_space=pl.ANY)
SMEM = pl.BlockSpec(memory_space=pltpu.SMEM)
VMEM = pl.BlockSpec(memory_space=pltpu.VMEM)


def buffers():
    return [
        pltpu.VMEM((2, 384, 768), FULL),
        pltpu.VMEM((2, 768, 768), FULL),
        pltpu.SMEM((2, 3), jnp.int32),
        pltpu.SemaphoreType.DMA((2, 2)),
        pltpu.SemaphoreType.DMA((2, 2)),
    ]


def shape(*dims):
    return jax.ShapeDtypeStruct(dims, FULL)


def cost(pairs):
    return pl.CostEstimate(flops=1_400_000_000 * pairs, bytes_accessed=3_600_000 * pairs, transcendentals=0)


def products(turn, where, mask, table, pieces, before, name):
    names = list(pieces)
    first = [] if before is None else [before]

    def body(where_ref, mask_ref, table_ref, *rest):
        refs = dict(zip(names, rest))
        rest = rest[len(names) :]
        if first:
            start, sums = rest[0], rest[1]
            sums[...] = start[...]
            rest = rest[2:]
        else:
            sums = rest[0]
            sums[...] = jnp.zeros_like(sums)
            rest = rest[1:]
        early = (where_ref[6] // 2, where_ref[7] // 2)
        begin, end = ((0, 0), early) if turn == 0 else (early, (6, 6))
        pair_loop(begin, end, refs, table_ref, mask_ref, sums, *rest)

    return pl.pallas_call(
        body,
        out_shape=shape(2, 384, 768),
        in_specs=[SMEM, SMEM, SMEM] + [HBM] * len(names) + [VMEM] * len(first),
        out_specs=VMEM,
        scratch_shapes=buffers(),
        compiler_params=pltpu.CompilerParams(vmem_limit_bytes=54 << 20),
        cost_estimate=cost(6),
        name=name,
    )(where, mask, table, *pieces.values(), *first)


def last_products(where, mask, table, pieces, before, own, diag_here):
    names = list(pieces)

    def body(where_ref, mask_ref, table_ref, *rest):
        refs = dict(zip(names, rest))
        start, own_ref, diag_ref, sep, part_var, sums = rest[len(names) : len(names) + 6]
        sums[...] = start[...]
        pair_loop((6, 6), (8, 8), refs, table_ref, mask_ref, sums, *rest[len(names) + 6 :])
        row = where_ref[5]
        total = diag_ref[...]
        for k in range(3):
            factor = mask_ref[row * 3 + k].astype(FULL)
            if k == 1:
                piece = jnp.concatenate([sums[0, 256:384], sums[1, 0:128]], axis=0)
            else:
                piece = sums[k // 2, pl.ds(128 if k == 2 else 0, 256), :]
            sep[pl.ds(k * 256, 256), :] = -piece
            total = total + factor * jnp.sum(own_ref[pl.ds(k * 256, 256), :] * piece, axis=0, keepdims=True)
        part_var[...] = total

    return pl.pallas_call(
        body,
        out_shape=(shape(768, 768), shape(1, 768)),
        in_specs=[SMEM, SMEM, SMEM] + [HBM] * len(names) + [VMEM] * 3,
        out_specs=(VMEM, VMEM),
        scratch_shapes=[pltpu.VMEM((2, 384, 768), FULL)] + buffers(),
        compiler_params=pltpu.CompilerParams(vmem_limit_bytes=54 << 20),
        cost_estimate=cost(4),
        name="last_products",
    )(where, mask, table, *pieces.values(), before, own, diag_here)


def update_body(where, mask, own, sep, mine, other):
    row = where[5]
    core = where[3]
    tiles = [own[pl.ds(k * 256, 256), :] * mask[row * 3 + k].astype(FULL) for k in range(3)]
    update = -dot3(split(jnp.concatenate(tiles, axis=0)), split(sep[...]), COLS)
    for zz in range(4):
        lower = update[zz * 192 : zz * 192 + 96]
        upper = update[zz * 192 + 96 : zz * 192 + 192]

        @pl.when(core == 0)
        def _():
            mine[zz] = lower
            other[zz] = upper

        @pl.when(core != 0)
        def _():
            mine[zz] = upper
            other[zz] = lower


def local(sigma_top, coupling, child_inverse, tile_mask, obs_node, obs_noise):
    sub = lax.axis_index("sub")
    row = lax.axis_index("row")
    x, y, z, core = sub // 4, sub % 4, row // 2, row % 2
    way = 1 - 2 * core
    table, early = work_table(x, y, z, core, way)
    where = jnp.concatenate([jnp.stack([x, y, z, core, way, row]).astype(jnp.int32), early])
    mask = tile_mask[0]

    a = sigma_top[:384]
    b = sigma_top[384:]
    m = coupling[0].reshape(2, 384, 768)
    xm, ym = ring(a, "x", 1, "p1"), ring(b, "y", 1, "p1")
    xp, yp = ring(a, "x", -1, "p1"), ring(b, "y", -1, "p1")
    za = ring(m, "z", -1, "p1z")

    one = (xm, ym, xp, yp)
    x2 = ring(after(xm, *one), "x", 1, "p2")
    y2 = ring(after(ym, *one), "y", 1, "p2")
    sib = swap(after(m, *one), "p2s")

    two = (x2, y2, sib, za)
    empty = jnp.zeros((1, 384, 384), FULL)
    a0 = jnp.concatenate([a[None], xm[None], xp[None], empty]).at[3].set(x2)
    b0 = jnp.concatenate([b[None], ym[None], yp[None], empty]).at[3].set(y2)
    a1, b1 = ring(after(a0, *two), "y", 1, "p3"), ring(after(b0, *two), "x", 1, "p3")
    a2, b2 = ring(after(a0, *two), "y", -1, "p3"), ring(after(b0, *two), "x", -1, "p3")
    zb = ring(after(jnp.concatenate([sib, za]), *two), "z", -1, "p3z")

    three = (a1, b1, a2, b2, zb)
    a3, b3 = ring(after(a1, *three), "y", 1, "p4"), ring(after(b1, *three), "x", 1, "p4")
    zt = swap(after(za, *three), "p4s")
    zs = swap(after(zb, *three), "p4s")

    pieces = dict(a0=a0, a1=a1, a2=a2, b0=b0, b1=b1, b2=b2, own=m, sib=sib, za=za, zb=zb)
    sums = products(0, where, mask, table, pieces, None, "early_products")
    pieces.update(zs=zs, zt=zt)
    sums = products(1, where, mask, table, pieces, sums, "middle_products")
    pieces.update(a3=a3, b3=b3)

    inverse = child_inverse[0]
    column = lax.broadcasted_iota(jnp.int32, (96, 768), 1)
    line = lax.broadcasted_iota(jnp.int32, (96, 768), 0) + row * 96
    diag_here = jnp.sum(jnp.where(column == line, inverse, 0.0), axis=0, keepdims=True)
    sep, part_var = last_products(where, mask, table, pieces, sums, coupling[0], diag_here)
    mine, other = pl.pallas_call(
        update_body,
        out_shape=(shape(4, 96, 768), shape(4, 96, 768)),
        in_specs=[SMEM, SMEM, VMEM, VMEM],
        out_specs=(VMEM, VMEM),
        compiler_params=pltpu.CompilerParams(vmem_limit_bytes=36 << 20),
        cost_estimate=cost(2),
        name="update",
    )(where, mask, coupling[0], sep)

    part = part_var + swap(part_var)
    half_sum = mine + swap(other)
    part = part + send(part, dz=1) + send(part, dz=-1) + send(part, dz=2)
    toward = lambda dz: lax.dynamic_index_in_dim(half_sum, (z + dz) % 4, 0, False)
    block_here = inverse + (toward(0) + send(toward(1), dz=1) + send(toward(-1), dz=-1) + send(toward(2), dz=2))
    part = after(part, half_sum)
    by_y = jnp.concatenate([part, send(part, dy=-1), send(part, dy=2), send(part, dy=1)], axis=0)
    by_xy = jnp.stack([by_y, send(by_y, dx=-1), send(by_y, dx=2), send(by_y, dx=1)])
    child = obs_node // 768
    far_x = (child // 4 - x) % 4
    far_y = (child % 4 - y) % 4
    index = (far_x * 4 + far_y) * 768 + obs_node % 768
    loo_var = by_xy.reshape(-1)[index] + obs_noise
    return sep[None], block_here[None], loo_var


def solution(mesh):
    placed = (
        P("row", "sub"),
        P("sub", "row", None),
        P("sub", "row", None),
        P("sub", None),
        P(("sub", "row")),
        P(("sub", "row")),
    )
    return jax.shard_map(
        local,
        mesh=mesh,
        in_specs=placed,
        out_specs=(P("sub", "row", None), P("sub", "row", None), P(("sub", "row"))),
        check_vma=False,
    )
```

time: 450 us -> 190 us (0.42)
  waiting for transfers between devices: 249 us -> 82.7 us
  matrix products: 105 us -> 0 us
  blocking collectives: 63.7 us -> 0 us
  Pallas kernels: 0 us -> 48.3 us
  starting transfers between devices: 0.12 us -> 40 us
  between operations: 13.8 us -> 1.04 us
    all_gather x2 -> x0, waiting for transfers between devices: 220 us -> none  [the longest x1 125 us: local(): lax.all_gather(sigma_top, 'sub', axis=1, tiled=True)]
    dot_general x2 -> x0, matrix products: 105 us -> none  [the longest x1 92.2 us: local(): jnp.dot(lax.all_gather(sigma_top, 'sub', axis=1, tiled=True), gathered, p...]
    ppermute x0 -> x31, waiting for transfers between devices: none -> 82.7 us  [send(): return lax.ppermute(value, AXES, pairs)]
    unnamed x1 -> x0, blocking collectives: 63.7 us -> none
    pallas_call x0 -> x4, Pallas kernels: none -> 48.3 us  [the longest x2 31.2 us: products(): pl.pallas_call(body, out_shape=shape(2, 384, 768), in_specs=[SMEM, SMEM,...]
    ppermute x0 -> x31, starting transfers between devices: none -> 40 us  [send(): return lax.ppermute(value, AXES, pairs)]
    reduce_scatter x1 -> x0, waiting for transfers between devices: 28 us -> none  [local(): lax.psum_scatter(lax.dot_general(masked, sep_part, (((0,), (0,)), ((), ()...]
  transfers between devices with their start and end apart: 3 -> 31, of which waited for: 3 -> 10; matrix products, arithmetic and copies ran while one was open for 1% -> 4% of each run, Pallas kernels for 0% -> 17%
where the time goes in v2:
time: 190 us; the launch traced here: 188 us
  waiting for transfers between devices  82.7 us (44%)
  Pallas kernels  48.3 us (25%)
  starting transfers between devices  40 us (21%)
  local copies, waits for them, and re-layouts  10 us (5%)
  other arithmetic  6.02 us (3%)
    ppermute x31, waiting for transfers between devices, send(): return lax.ppermute(value, AXES, pairs)  82.7 us
    ppermute x31, starting transfers between devices, send(): return lax.ppermute(value, AXES, pairs)  40 us
    pallas_call x2, Pallas kernels, products(): pl.pallas_call(body, out_shape=shape(2, 384, 768), in_specs=[SMEM, SMEM,...  31.2 us
    pallas_call x1, Pallas kernels, last_products(): pl.pallas_call(body, out_shape=(shape(768, 768), shape(1, 768)), in_specs...  13.4 us
    unnamed x34, local copies, waits for them, and re-layouts  5.23 us
  transfers between devices with their start and end apart: 31, of which 10 were waited for; matrix products, arithmetic and copies ran while one was open for 4% of the time, Pallas kernels for 17%

profile of v2, /device:TPU:16, one launch (start us, length us, event | category | flops | bytes accessed | tf_op | source)
XLA Modules:
  0.0 188.1 jit_solution(3841849281222922563)
XLA Ops:
  0.6 1.5 slice_bitcast_fusion
  2.2 1.6 collective-permute-start
  3.8 1.7 collective-permute-start.1
  5.5 1.3 collective-permute-start.2
  6.8 0.7 collective-permute-start.3
  7.5 4.0 %collective-permute-start.7 = (f32[2,384,768]{2,1,0:T(8,128)S(1)}, f32[2,384,768]{2,1,0:T(8,128)}, u32[]{:S(2)}, u32[]{:S(2)}) collective-permute-start(f32[2,384,768]{2,1,0:T(8,128)S(1)} %bitcast.58), channel_id=1, source_target_pairs={{0,6},{1,3},{2,0},{3,5},{4,2},{5,7},{6,4},{7,1},{8,14},{9,11},{10,... | collective-permute-start | bytes 7077896 | tf_op jit(solution)/shard_map/p1z/ppermute | solution.py:25
  11.6 6.7 %collective-permute-done = f32[384,384]{1,0:T(8,128)S(1)} collective-permute-done((f32[384,384]{1,0:T(8,128)S(1)}, f32[384,384]{1,0:T(8,128)S(1)}, u32[]{:S(2)}, u32[]{:S(2)}) %collective-permute-start) | collective-permute-done | bytes 589856 | tf_op jit(solution)/shard_map/p1/ppermute | solution.py:25
  18.3 1.7 collective-permute-done.2
  20.0 2.3 %collective-permute-start.5 = (f32[384,384]{1,0:T(8,128)S(1)}, f32[384,384]{1,0:T(8,128)S(1)}, u32[]{:S(2)}, u32[]{:S(2)}) collective-permute-start(f32[384,384]{1,0:T(8,128)S(1)} %collective-permute-done.2), channel_id=1, source_target_pairs={{0,8},{1,25},{2,10},{3,27},{4,12},{5,29},{6,14},{7,31},{8,16},{9,1... | collective-permute-start | bytes 1769480 | tf_op jit(solution)/shard_map/p2/ppermute | solution.py:25
  22.8 15.1 %collective-permute-done.7.rest_8_ = f32[2,384,768]{2,1,0:T(8,128)} collective-permute-done((f32[2,384,768]{2,1,0:T(8,128)S(1)}, f32[2,384,768]{2,1,0:T(8,128)}, u32[]{:S(2)}, u32[]{:S(2)}) %collective-permute-start.7) | collective-permute-done | bytes 2359328 | tf_op jit(solution)/shard_map/p1z/ppermute | solution.py:25
  37.9 2.8 %pad_maximum_fusion = f32[4,384,768]{2,1,0:T(8,128)S(1)} fusion(f32[2,384,768]{2,1,0:T(8,128)} %collective-permute-done.7.rest_8_, f32[2,384,768]{2,1,0:T(8,128)S(1)} %collective-permute-done.6.rest_7_), kind=kLoop, calls=%fused_computation.1 | loop fusion | flops 1179648 | bytes 9437184 | tf_op jit(solution)/shard_map/concatenate | solution.py:276
  40.8 3.9 %collective-permute-start.12 = (f32[4,384,768]{2,1,0:T(8,128)S(1)}, f32[4,384,768]{2,1,0:T(8,128)}, u32[]{:S(2)}, u32[]{:S(2)}) collective-permute-start(f32[4,384,768]{2,1,0:T(8,128)S(1)} %pad_maximum_fusion), channel_id=1, source_target_pairs={{0,6},{1,3},{2,0},{3,5},{4,2},{5,7},{6,4},{7,1},{8,14},{9,11},{10,... | collective-permute-start | bytes 14155784 | tf_op jit(solution)/shard_map/p3z/ppermute | solution.py:25
  45.6 3.0 %collective-permute-start.11 = (f32[4,384,384]{2,1,0:T(8,128)S(1)}, f32[4,384,384]{2,1,0:T(8,128)S(1)}, u32[]{:S(2)}, u32[]{:S(2)}) collective-permute-start(f32[4,384,384]{2,1,0:T(8,128)S(1)} %bitcast_dynamic-update-slice_fusion.rest_3_), channel_id=1, source_target_pairs={{0,96},{1,33},{2,98},{3,35},{4,100},{5,37},{6,102},{7,39},{8,104},... | collective-permute-start | bytes 7077896 | tf_op jit(solution)/shard_map/p3/ppermute | solution.py:25
  48.6 1.3 collective-permute-start.8
  49.8 0.7 collective-permute-start.9
  50.6 46.2 %collective-permute-done.10.rest_4_ = f32[4,384,384]{2,1,0:T(8,128)S(1)} collective-permute-done((f32[4,384,384]{2,1,0:T(8,128)S(1)}, f32[4,384,384]{2,1,0:T(8,128)S(1)}, u32[]{:S(2)}, u32[]{:S(2)}) %collective-permute-start.10) | collective-permute-done | bytes 2359328 | tf_op jit(solution)/shard_map/p3/ppermute | solution.py:25
  96.9 1.4 copy-done.8
  98.2 0.7 copy-done.9
  99.0 0.7 copy-done.10
  99.7 0.7 copy-done.11
  100.4 2.5 %collective-permute-start.15 = (f32[4,384,384]{2,1,0:T(8,128)}, f32[4,384,384]{2,1,0:T(8,128)}, u32[]{:S(2)}, u32[]{:S(2)}) collective-permute-start(f32[4,384,384]{2,1,0:T(8,128)} %copy-done.10), channel_id=1, source_target_pairs={{0,8},{1,25},{2,10},{3,27},{4,12},{5,29},{6,14},{7,31},{8,16},{9,1... | collective-permute-start | bytes 7077896 | tf_op jit(solution)/shard_map/p4/ppermute | solution.py:25
  103.0 0.6 broadcast_in_dim.66.rest_16_
  103.7 0.7 concatenate.19.where_ref.where
  104.7 0.6 pad_add_fusion.table_ref
  105.4 16.8 %early_products.1.rest_12_ = f32[2,384,768]{2,1,0:T(8,128)} custom-call(s32[8]{0:T(128)} %concatenate.19.where_ref.where, s32[24]{0:T(128)} %bitcast.61, s32[3,32]{1,0:T(4,128)} %pad_add_fusion.table_ref, f32[4,384,384]{2,1,0:T(8,128)} %copy-done.6, f32[4,384,384]{2,1,0:T(8,128)} %copy-done.10, f32[4,384,384]{2,1,0:T(8,128)} %copy-done.11, ...), custom_call_target="tpu_custom_call" | custom-call | flops 8400000000 | bytes 21600000 | tf_op jit(solution)/shard_map/early_products/pallas_call | solution.py:185
  122.2 14.4 %middle_products.1.rest_14_ = f32[2,384,768]{2,1,0:T(8,128)} custom-call(s32[8]{0:T(128)} %concatenate.19.where_ref.where, s32[24]{0:T(128)} %bitcast.62, s32[3,32]{1,0:T(4,128)} %pad_add_fusion.table_ref, f32[4,384,384]{2,1,0:T(8,128)} %copy-done.6, f32[4,384,384]{2,1,0:T(8,128)} %copy-done.10, f32[4,384,384]{2,1,0:T(8,128)} %copy-done.11, ...), custom_call_target="tpu_custom_call" | custom-call | flops 8400000000 | bytes 21600000 | tf_op jit(solution)/shard_map/middle_products/pallas_call | solution.py:185
  136.7 13.4 %last_products.1 = (f32[768,768]{1,0:T(8,128)}, f32[1,768]{1,0:T(1,128)}) custom-call(s32[8]{0:T(128)} %concatenate.19.where_ref.where, s32[24]{0:T(128)} %bitcast.63, s32[3,32]{1,0:T(4,128)} %pad_add_fusion.table_ref, f32[4,384,384]{2,1,0:T(8,128)} %copy-done.6, f32[4,384,384]{2,1,0:T(8,128)} %copy-done.10, f32[4,384,384]{2,1,0:T(8,128)} %copy-done.11, ...), custom_call_target="tpu_custom_call" | custom-call | flops 5600000000 | bytes 14400000 | tf_op jit(solution)/shard_map/last_products/pallas_call | solution.py:217
  150.1 1.7 copy-done.4
  151.7 3.8 %update.1 = (f32[4,96,768]{2,1,0:T(8,128)S(1)}, f32[4,96,768]{2,1,0:T(8,128)S(1)}) custom-call(s32[8]{0:T(128)S(1)} %copy-done.2, s32[24]{0:T(128)S(1)} %bitcast.64, f32[768,768]{1,0:T(8,128)S(1)} %bitcast.60, f32[768,768]{1,0:T(8,128)S(1)} %copy-done.4), custom_call_target="tpu_custom_call" | custom-call | flops 2800000000 | bytes 7200000 | tf_op jit(solution)/shard_map/update/pallas_call | solution.py:294
  155.6 0.5 collective-permute-start.21
  156.1 2.3 %collective-permute-done.21 = f32[1,768]{1,0:T(1,128)S(1)} collective-permute-done((f32[1,768]{1,0:T(1,128)S(1)}, f32[1,768]{1,0:T(1,128)S(1)}, u32[]{:S(2)}, u32[]{:S(2)}) %collective-permute-start.21) | collective-permute-done | bytes 3104 | tf_op jit(solution)/shard_map/swap/ppermute | solution.py:25
  158.8 2.9 %collective-permute-start.23 = (f32[1,768]{1,0:T(1,128)S(1)}, f32[1,768]{1,0:T(1,128)S(1)}, u32[]{:S(2)}, u32[]{:S(2)}) collective-permute-start(f32[1,768]{1,0:T(1,128)S(1)} %add.404), channel_id=1, source_target_pairs={{0,6},{1,7},{2,0},{3,1},{4,2},{5,3},{6,4},{7,5},{8,14},{9,15},{10,... | collective-permute-start | bytes 9224 | tf_op jit(solution)/shard_map/ppermute | solution.py:25
  161.7 0.5 collective-permute-start.24
  162.2 1.1 collective-permute-done.22
  163.3 3.5 %collective-permute-done.24 = f32[1,768]{1,0:T(1,128)S(1)} collective-permute-done((f32[1,768]{1,0:T(1,128)S(1)}, f32[1,768]{1,0:T(1,128)S(1)}, u32[]{:S(2)}, u32[]{:S(2)}) %collective-permute-start.24) | collective-permute-done | bytes 3104 | tf_op jit(solution)/shard_map/ppermute | solution.py:25
  167.0 1.6 collective-permute-start.25
  168.6 2.0 %collective-permute-start.26 = (f32[1,768]{1,0:T(1,128)S(1)}, f32[1,768]{1,0:T(1,128)S(1)}, u32[]{:S(2)}, u32[]{:S(2)}) collective-permute-start(f32[1,768]{1,0:T(1,128)S(1)} %add_add_fusion), channel_id=1, source_target_pairs={{0,16},{1,17},{2,18},{3,19},{4,20},{5,21},{6,22},{7,23},{8,24},{9,... | collective-permute-start | bytes 9224 | tf_op jit(solution)/shard_map/ppermute | solution.py:25
  171.1 1.1 collective-permute-start.18
  172.1 2.2 %collective-permute-start.19 = (f32[96,768]{1,0:T(8,128)S(1)}, f32[96,768]{1,0:T(8,128)S(1)}, u32[]{:S(2)}, u32[]{:S(2)}) collective-permute-start(f32[96,768]{1,0:T(8,128)S(1)} %get-tuple-element.62), channel_id=1, source_target_pairs={{0,6},{1,7},{2,0},{3,1},{4,2},{5,3},{6,4},{7,5},{8,14},{9,15},{10,... | collective-permute-start | bytes 884744 | tf_op jit(solution)/shard_map/ppermute | solution.py:25
  174.4 1.9 collective-permute-start.20
  176.3 1.5 collective-permute-start.28
  177.8 0.9 collective-permute-start.29
  178.7 1.3 collective-permute-done.28
  180.2 2.9 %collective-permute-done.29 = f32[4,768]{1,0:T(4,128)S(1)} collective-permute-done((f32[4,768]{1,0:T(4,128)S(1)}, f32[4,768]{1,0:T(4,128)S(1)}, u32[]{:S(2)}, u32[]{:S(2)}) %collective-permute-start.29) | collective-permute-done | bytes 12320 | tf_op jit(solution)/shard_map/ppermute | solution.py:25
  183.1 1.8 collective-permute-done.30
  185.0 1.7 gather_fusion
  186.7 0.6 add.416
  187.3 0.8 fusion.3
  (80 shorter events, 3.5 us)
Async XLA Ops:
  0.6 6.9 %copy-start = (f32[1,768,768]{2,1,0:T(8,128)S(1)}, f32[1,768,768]{2,1,0:T(8,128)}, u32[]{:S(2)}) copy-start(f32[1,768,768]{2,1,0:T(8,128)} %param.11) | copy-start | bytes 7077892
  2.2 16.1 %collective-permute-start = (f32[384,384]{1,0:T(8,128)S(1)}, f32[384,384]{1,0:T(8,128)S(1)}, u32[]{:S(2)}, u32[]{:S(2)}) collective-permute-start(f32[384,384]{1,0:T(8,128)S(1)} %get-tuple-element.66), channel_id=1, source_target_pairs={{0,32},{1,97},{2,34},{3,99},{4,36},{5,101},{6,38},{7,103},{8,40},{... | collective-permute-start | bytes 1769480 | tf_op jit(solution)/shard_map/p1/ppermute | solution.py:25
  3.8 14.5 %collective-permute-start.1 = (f32[384,384]{1,0:T(8,128)S(1)}, f32[384,384]{1,0:T(8,128)S(1)}, u32[]{:S(2)}, u32[]{:S(2)}) collective-permute-start(f32[384,384]{1,0:T(8,128)S(1)} %get-tuple-element.66), channel_id=1, source_target_pairs={{0,96},{1,33},{2,98},{3,35},{4,100},{5,37},{6,102},{7,39},{8,104},... | collective-permute-start | bytes 1769480 | tf_op jit(solution)/shard_map/p1/ppermute | solution.py:25
  5.5 14.5 %collective-permute-start.2 = (f32[384,384]{1,0:T(8,128)S(1)}, f32[384,384]{1,0:T(8,128)S(1)}, u32[]{:S(2)}, u32[]{:S(2)}) collective-permute-start(f32[384,384]{1,0:T(8,128)S(1)} %get-tuple-element.65), channel_id=1, source_target_pairs={{0,8},{1,25},{2,10},{3,27},{4,12},{5,29},{6,14},{7,31},{8,16},{9,1... | collective-permute-start | bytes 1769480 | tf_op jit(solution)/shard_map/p1/ppermute | solution.py:25
  6.8 13.2 %collective-permute-start.3 = (f32[384,384]{1,0:T(8,128)S(1)}, f32[384,384]{1,0:T(8,128)S(1)}, u32[]{:S(2)}, u32[]{:S(2)}) collective-permute-start(f32[384,384]{1,0:T(8,128)S(1)} %get-tuple-element.65), channel_id=1, source_target_pairs={{0,24},{1,9},{2,26},{3,11},{4,28},{5,13},{6,30},{7,15},{8,0},{9,17... | collective-permute-start | bytes 1769480 | tf_op jit(solution)/shard_map/p1/ppermute | solution.py:25
  7.5 30.4 %collective-permute-start.7 = (f32[2,384,768]{2,1,0:T(8,128)S(1)}, f32[2,384,768]{2,1,0:T(8,128)}, u32[]{:S(2)}, u32[]{:S(2)}) collective-permute-start(f32[2,384,768]{2,1,0:T(8,128)S(1)} %bitcast.58), channel_id=1, source_target_pairs={{0,6},{1,3},{2,0},{3,5},{4,2},{5,7},{6,4},{7,1},{8,14},{9,11},{10,... | collective-permute-start | bytes 7077896 | tf_op jit(solution)/shard_map/p1z/ppermute | solution.py:25
  20.0 17.9 %collective-permute-start.6 = (f32[2,384,768]{2,1,0:T(8,128)S(1)}, f32[2,384,768]{2,1,0:T(8,128)S(1)}, u32[]{:S(2)}, u32[]{:S(2)}) collective-permute-start(f32[2,384,768]{2,1,0:T(8,128)S(1)} %bitcast.59), channel_id=1, source_target_pairs={{0,1},{1,0},{2,3},{3,2},{4,5},{5,4},{6,7},{7,6},{8,9},{9,8},{10,11... | collective-permute-start | bytes 7077896 | tf_op jit(solution)/shard_map/p2s/ppermute | solution.py:25
  20.0 20.8 %collective-permute-start.5 = (f32[384,384]{1,0:T(8,128)S(1)}, f32[384,384]{1,0:T(8,128)S(1)}, u32[]{:S(2)}, u32[]{:S(2)}) collective-permute-start(f32[384,384]{1,0:T(8,128)S(1)} %collective-permute-done.2), channel_id=1, source_target_pairs={{0,8},{1,25},{2,10},{3,27},{4,12},{5,29},{6,14},{7,31},{8,16},{9,1... | collective-permute-start | bytes 1769480 | tf_op jit(solution)/shard_map/p2/ppermute | solution.py:25
  22.3 18.5 %collective-permute-start.4 = (f32[384,384]{1,0:T(8,128)S(1)}, f32[384,384]{1,0:T(8,128)S(1)}, u32[]{:S(2)}, u32[]{:S(2)}) collective-permute-start(f32[384,384]{1,0:T(8,128)S(1)} %collective-permute-done), channel_id=1, source_target_pairs={{0,32},{1,97},{2,34},{3,99},{4,36},{5,101},{6,38},{7,103},{8,40},{... | collective-permute-start | bytes 1769480 | tf_op jit(solution)/shard_map/p2/ppermute | solution.py:25
  37.9 2.8 %copy-start.5 = (f32[2,384,768]{2,1,0:T(8,128)}, f32[2,384,768]{2,1,0:T(8,128)S(1)}, u32[]{:S(2)}) copy-start(f32[2,384,768]{2,1,0:T(8,128)S(1)} %collective-permute-done.6.rest_7_) | copy-start | bytes 7077892
  40.8 56.1 %collective-permute-start.12 = (f32[4,384,768]{2,1,0:T(8,128)S(1)}, f32[4,384,768]{2,1,0:T(8,128)}, u32[]{:S(2)}, u32[]{:S(2)}) collective-permute-start(f32[4,384,768]{2,1,0:T(8,128)S(1)} %pad_maximum_fusion), channel_id=1, source_target_pairs={{0,6},{1,3},{2,0},{3,5},{4,2},{5,7},{6,4},{7,1},{8,14},{9,11},{10,... | collective-permute-start | bytes 14155784 | tf_op jit(solution)/shard_map/p3z/ppermute | solution.py:25
  45.1 57.7 %copy-start.12 = (f32[1,96,768]{2,1,0:T(8,128)S(1)}, f32[1,96,768]{2,1,0:T(8,128)}, u32[]{:S(2)}) copy-start(f32[1,96,768]{2,1,0:T(8,128)} %param.12) | copy-start | bytes 884740
  45.2 51.6 %copy-start.7 = (f32[4,384,384]{2,1,0:T(8,128)}, f32[4,384,384]{2,1,0:T(8,128)S(1)}, u32[]{:S(2)}) copy-start(f32[4,384,384]{2,1,0:T(8,128)S(1)} %bitcast_dynamic-update-slice_fusion.rest_3_) | copy-start | bytes 7077892
  45.2 60.1 %copy-start.6 = (f32[4,384,384]{2,1,0:T(8,128)}, f32[4,384,384]{2,1,0:T(8,128)S(1)}, u32[]{:S(2)}) copy-start(f32[4,384,384]{2,1,0:T(8,128)S(1)} %bitcast_dynamic-update-slice_fusion.1.rest_0_) | copy-start | bytes 7077892
  45.2 51.5 %collective-permute-start.10 = (f32[4,384,384]{2,1,0:T(8,128)S(1)}, f32[4,384,384]{2,1,0:T(8,128)S(1)}, u32[]{:S(2)}, u32[]{:S(2)}) collective-permute-start(f32[4,384,384]{2,1,0:T(8,128)S(1)} %bitcast_dynamic-update-slice_fusion.rest_3_), channel_id=1, source_target_pairs={{0,32},{1,97},{2,34},{3,99},{4,36},{5,101},{6,38},{7,103},{8,40},{... | collective-permute-start | bytes 7077896 | tf_op jit(solution)/shard_map/p3/ppermute | solution.py:25
  45.6 51.2 %collective-permute-start.11 = (f32[4,384,384]{2,1,0:T(8,128)S(1)}, f32[4,384,384]{2,1,0:T(8,128)S(1)}, u32[]{:S(2)}, u32[]{:S(2)}) collective-permute-start(f32[4,384,384]{2,1,0:T(8,128)S(1)} %bitcast_dynamic-update-slice_fusion.rest_3_), channel_id=1, source_target_pairs={{0,96},{1,33},{2,98},{3,35},{4,100},{5,37},{6,102},{7,39},{8,104},... | collective-permute-start | bytes 7077896 | tf_op jit(solution)/shard_map/p3/ppermute | solution.py:25
  48.6 48.2 %collective-permute-start.8 = (f32[4,384,384]{2,1,0:T(8,128)S(1)}, f32[4,384,384]{2,1,0:T(8,128)S(1)}, u32[]{:S(2)}, u32[]{:S(2)}) collective-permute-start(f32[4,384,384]{2,1,0:T(8,128)S(1)} %bitcast_dynamic-update-slice_fusion.1.rest_0_), channel_id=1, source_target_pairs={{0,8},{1,25},{2,10},{3,27},{4,12},{5,29},{6,14},{7,31},{8,16},{9,1... | collective-permute-start | bytes 7077896 | tf_op jit(solution)/shard_map/p3/ppermute | solution.py:25
  49.8 47.0 %collective-permute-start.9 = (f32[4,384,384]{2,1,0:T(8,128)S(1)}, f32[4,384,384]{2,1,0:T(8,128)S(1)}, u32[]{:S(2)}, u32[]{:S(2)}) collective-permute-start(f32[4,384,384]{2,1,0:T(8,128)S(1)} %bitcast_dynamic-update-slice_fusion.1.rest_0_), channel_id=1, source_target_pairs={{0,24},{1,9},{2,26},{3,11},{4,28},{5,13},{6,30},{7,15},{8,0},{9,17... | collective-permute-start | bytes 7077896 | tf_op jit(solution)/shard_map/p3/ppermute | solution.py:25
  96.8 1.4 copy-start.8
  96.8 2.2 %copy-start.9 = (f32[4,384,384]{2,1,0:T(8,128)}, f32[4,384,384]{2,1,0:T(8,128)S(1)}, u32[]{:S(2)}) copy-start(f32[4,384,384]{2,1,0:T(8,128)S(1)} %collective-permute-done.11.rest_5_) | copy-start | bytes 7077892
  96.8 2.9 %copy-start.10 = (f32[4,384,384]{2,1,0:T(8,128)}, f32[4,384,384]{2,1,0:T(8,128)S(1)}, u32[]{:S(2)}) copy-start(f32[4,384,384]{2,1,0:T(8,128)S(1)} %collective-permute-done.8.rest_1_) | copy-start | bytes 7077892
  96.8 3.5 %copy-start.11 = (f32[4,384,384]{2,1,0:T(8,128)}, f32[4,384,384]{2,1,0:T(8,128)S(1)}, u32[]{:S(2)}) copy-start(f32[4,384,384]{2,1,0:T(8,128)S(1)} %collective-permute-done.9.rest_2_) | copy-start | bytes 7077892
  98.2 23.9 %collective-permute-start.13 = (f32[4,384,768]{2,1,0:T(8,128)}, f32[4,384,768]{2,1,0:T(8,128)}, u32[]{:S(2)}, u32[]{:S(2)}) collective-permute-start(f32[4,384,768]{2,1,0:T(8,128)} %collective-permute-done.12.rest_9_), channel_id=1, source_target_pairs={{0,1},{1,0},{2,3},{3,2},{4,5},{5,4},{6,7},{7,6},{8,9},{9,8},{10,11... | collective-permute-start | bytes 14155784 | tf_op jit(solution)/shard_map/p4s/ppermute | solution.py:25
  99.0 23.2 %collective-permute-start.14 = (f32[2,384,768]{2,1,0:T(8,128)}, f32[2,384,768]{2,1,0:T(8,128)}, u32[]{:S(2)}, u32[]{:S(2)}) collective-permute-start(f32[2,384,768]{2,1,0:T(8,128)} %collective-permute-done.7.rest_8_), channel_id=1, source_target_pairs={{0,1},{1,0},{2,3},{3,2},{4,5},{5,4},{6,7},{7,6},{8,9},{9,8},{10,11... | collective-permute-start | bytes 7077896 | tf_op jit(solution)/shard_map/p4s/ppermute | solution.py:25
  100.4 36.3 %collective-permute-start.16 = (f32[4,384,384]{2,1,0:T(8,128)}, f32[4,384,384]{2,1,0:T(8,128)}, u32[]{:S(2)}, u32[]{:S(2)}) collective-permute-start(f32[4,384,384]{2,1,0:T(8,128)} %copy-done.8), channel_id=1, source_target_pairs={{0,32},{1,97},{2,34},{3,99},{4,36},{5,101},{6,38},{7,103},{8,40},{... | collective-permute-start | bytes 7077896 | tf_op jit(solution)/shard_map/p4/ppermute | solution.py:25
  100.4 36.3 %collective-permute-start.15 = (f32[4,384,384]{2,1,0:T(8,128)}, f32[4,384,384]{2,1,0:T(8,128)}, u32[]{:S(2)}, u32[]{:S(2)}) collective-permute-start(f32[4,384,384]{2,1,0:T(8,128)} %copy-done.10), channel_id=1, source_target_pairs={{0,8},{1,25},{2,10},{3,27},{4,12},{5,29},{6,14},{7,31},{8,16},{9,1... | collective-permute-start | bytes 7077896 | tf_op jit(solution)/shard_map/p4/ppermute | solution.py:25
  136.6 13.4 %copy-start.1 = (f32[1,768,768]{2,1,0:T(8,128)S(1)}, f32[1,768,768]{2,1,0:T(8,128)}, u32[]{:S(2)}) copy-start(f32[1,768,768]{2,1,0:T(8,128)} %param.11) | copy-start | bytes 7077892
  136.6 13.4 %copy-start.2 = (s32[8]{0:T(128)S(1)}, s32[8]{0:T(128)}, u32[]{:S(2)}) copy-start(s32[8]{0:T(128)} %concatenate.19.where_ref.where) | copy-start | bytes 100
  136.7 13.4 %copy-start.3 = (s32[1,24]{1,0:T(1,128)S(1)}, s32[1,24]{1,0:T(1,128)}, u32[]{:S(2)}) copy-start(s32[1,24]{1,0:T(1,128)} %param.13) | copy-start | bytes 292
  150.1 1.7 copy-start.4
  151.7 3.9 %copy-start.14 = (f32[1,768]{1,0:T(1,128)S(1)}, f32[1,768]{1,0:T(1,128)}, u32[]{:S(2)}) copy-start(f32[1,768]{1,0:T(1,128)} %get-tuple-element.55) | copy-start | bytes 9220
  155.5 11.3 %collective-permute-start.17 = (f32[4,96,768]{2,1,0:T(8,128)S(1)}, f32[4,96,768]{2,1,0:T(8,128)S(1)}, u32[]{:S(2)}, u32[]{:S(2)}) collective-permute-start(f32[4,96,768]{2,1,0:T(8,128)S(1)} %get-tuple-element.54), channel_id=1, source_target_pairs={{0,1},{1,0},{2,3},{3,2},{4,5},{5,4},{6,7},{7,6},{8,9},{9,8},{10,11... | collective-permute-start | bytes 3538952 | tf_op jit(solution)/shard_map/swap/ppermute | solution.py:25
  155.6 2.8 %collective-permute-start.21 = (f32[1,768]{1,0:T(1,128)S(1)}, f32[1,768]{1,0:T(1,128)S(1)}, u32[]{:S(2)}, u32[]{:S(2)}) collective-permute-start(f32[1,768]{1,0:T(1,128)S(1)} %copy-done.14), channel_id=1, source_target_pairs={{0,1},{1,0},{2,3},{3,2},{4,5},{5,4},{6,7},{7,6},{8,9},{9,8},{10,11... | collective-permute-start | bytes 9224 | tf_op jit(solution)/shard_map/swap/ppermute | solution.py:25
  158.4 4.8 %collective-permute-start.22 = (f32[1,768]{1,0:T(1,128)S(1)}, f32[1,768]{1,0:T(1,128)S(1)}, u32[]{:S(2)}, u32[]{:S(2)}) collective-permute-start(f32[1,768]{1,0:T(1,128)S(1)} %add.404), channel_id=1, source_target_pairs={{0,2},{1,3},{2,4},{3,5},{4,6},{5,7},{6,0},{7,1},{8,10},{9,11},{10,... | collective-permute-start | bytes 9224 | tf_op jit(solution)/shard_map/ppermute | solution.py:25
  158.8 4.5 %collective-permute-start.23 = (f32[1,768]{1,0:T(1,128)S(1)}, f32[1,768]{1,0:T(1,128)S(1)}, u32[]{:S(2)}, u32[]{:S(2)}) collective-permute-start(f32[1,768]{1,0:T(1,128)S(1)} %add.404), channel_id=1, source_target_pairs={{0,6},{1,7},{2,0},{3,1},{4,2},{5,3},{6,4},{7,5},{8,14},{9,15},{10,... | collective-permute-start | bytes 9224 | tf_op jit(solution)/shard_map/ppermute | solution.py:25
  161.7 5.1 %collective-permute-start.24 = (f32[1,768]{1,0:T(1,128)S(1)}, f32[1,768]{1,0:T(1,128)S(1)}, u32[]{:S(2)}, u32[]{:S(2)}) collective-permute-start(f32[1,768]{1,0:T(1,128)S(1)} %add.404), channel_id=1, source_target_pairs={{0,4},{1,5},{2,6},{3,7},{4,0},{5,1},{6,2},{7,3},{8,12},{9,13},{10,... | collective-permute-start | bytes 9224 | tf_op jit(solution)/shard_map/ppermute | solution.py:25
  166.8 11.0 %copy-start.15 = (s32[256]{0:T(256)S(1)}, s32[256]{0:T(256)}, u32[]{:S(2)}) copy-start(s32[256]{0:T(256)} %param.14) | copy-start | bytes 3076
  167.0 19.7 %copy-start.16 = (f32[256]{0:T(256)S(1)}, f32[256]{0:T(256)}, u32[]{:S(2)}) copy-start(f32[256]{0:T(256)} %param.15) | copy-start | bytes 3076
  167.0 20.3 %copy-start.13 = (f32[1,96,768]{2,1,0:T(8,128)S(1)}, f32[1,96,768]{2,1,0:T(8,128)}, u32[]{:S(2)}) copy-start(f32[1,96,768]{2,1,0:T(8,128)} %param.12) | copy-start | bytes 884740
  167.0 7.4 %collective-permute-start.25 = (f32[1,768]{1,0:T(1,128)S(1)}, f32[1,768]{1,0:T(1,128)S(1)}, u32[]{:S(2)}, u32[]{:S(2)}) collective-permute-start(f32[1,768]{1,0:T(1,128)S(1)} %add_add_fusion), channel_id=1, source_target_pairs={{0,24},{1,25},{2,26},{3,27},{4,28},{5,29},{6,30},{7,31},{8,0},{9,1... | collective-permute-start | bytes 9224 | tf_op jit(solution)/shard_map/ppermute | solution.py:25
  168.6 7.6 %collective-permute-start.26 = (f32[1,768]{1,0:T(1,128)S(1)}, f32[1,768]{1,0:T(1,128)S(1)}, u32[]{:S(2)}, u32[]{:S(2)}) collective-permute-start(f32[1,768]{1,0:T(1,128)S(1)} %add_add_fusion), channel_id=1, source_target_pairs={{0,16},{1,17},{2,18},{3,19},{4,20},{5,21},{6,22},{7,23},{8,24},{9,... | collective-permute-start | bytes 9224 | tf_op jit(solution)/shard_map/ppermute | solution.py:25
  170.6 5.6 %collective-permute-start.27 = (f32[1,768]{1,0:T(1,128)S(1)}, f32[1,768]{1,0:T(1,128)S(1)}, u32[]{:S(2)}, u32[]{:S(2)}) collective-permute-start(f32[1,768]{1,0:T(1,128)S(1)} %add_add_fusion), channel_id=1, source_target_pairs={{0,8},{1,9},{2,10},{3,11},{4,12},{5,13},{6,14},{7,15},{8,16},{9,17... | collective-permute-start | bytes 9224 | tf_op jit(solution)/shard_map/ppermute | solution.py:25
  171.1 16.2 %collective-permute-start.18 = (f32[96,768]{1,0:T(8,128)S(1)}, f32[96,768]{1,0:T(8,128)S(1)}, u32[]{:S(2)}, u32[]{:S(2)}) collective-permute-start(f32[96,768]{1,0:T(8,128)S(1)} %get-tuple-element.60), channel_id=1, source_target_pairs={{0,2},{1,3},{2,4},{3,5},{4,6},{5,7},{6,0},{7,1},{8,10},{9,11},{10,... | collective-permute-start | bytes 884744 | tf_op jit(solution)/shard_map/ppermute | solution.py:25
  172.1 15.2 %collective-permute-start.19 = (f32[96,768]{1,0:T(8,128)S(1)}, f32[96,768]{1,0:T(8,128)S(1)}, u32[]{:S(2)}, u32[]{:S(2)}) collective-permute-start(f32[96,768]{1,0:T(8,128)S(1)} %get-tuple-element.62), channel_id=1, source_target_pairs={{0,6},{1,7},{2,0},{3,1},{4,2},{5,3},{6,4},{7,5},{8,14},{9,15},{10,... | collective-permute-start | bytes 884744 | tf_op jit(solution)/shard_map/ppermute | solution.py:25
  174.4 12.9 %collective-permute-start.20 = (f32[96,768]{1,0:T(8,128)S(1)}, f32[96,768]{1,0:T(8,128)S(1)}, u32[]{:S(2)}, u32[]{:S(2)}) collective-permute-start(f32[96,768]{1,0:T(8,128)S(1)} %get-tuple-element.61), channel_id=1, source_target_pairs={{0,4},{1,5},{2,6},{3,7},{4,0},{5,1},{6,2},{7,3},{8,12},{9,13},{10,... | collective-permute-start | bytes 884744 | tf_op jit(solution)/shard_map/ppermute | solution.py:25
  176.3 3.8 %collective-permute-start.28 = (f32[4,768]{1,0:T(4,128)S(1)}, f32[4,768]{1,0:T(4,128)S(1)}, u32[]{:S(2)}, u32[]{:S(2)}) collective-permute-start(f32[4,768]{1,0:T(4,128)S(1)} %get-tuple-element.68), channel_id=1, source_target_pairs={{0,96},{1,97},{2,98},{3,99},{4,100},{5,101},{6,102},{7,103},{8,104... | collective-permute-start | bytes 36872 | tf_op jit(solution)/shard_map/ppermute | solution.py:25
  177.8 5.3 %collective-permute-start.29 = (f32[4,768]{1,0:T(4,128)S(1)}, f32[4,768]{1,0:T(4,128)S(1)}, u32[]{:S(2)}, u32[]{:S(2)}) collective-permute-start(f32[4,768]{1,0:T(4,128)S(1)} %get-tuple-element.68), channel_id=1, source_target_pairs={{0,64},{1,65},{2,66},{3,67},{4,68},{5,69},{6,70},{7,71},{8,72},{9,... | collective-permute-start | bytes 36872 | tf_op jit(solution)/shard_map/ppermute | solution.py:25
  180.0 4.9 %collective-permute-start.30 = (f32[4,768]{1,0:T(4,128)S(1)}, f32[4,768]{1,0:T(4,128)S(1)}, u32[]{:S(2)}, u32[]{:S(2)}) collective-permute-start(f32[4,768]{1,0:T(4,128)S(1)} %get-tuple-element.68), channel_id=1, source_target_pairs={{0,32},{1,33},{2,34},{3,35},{4,36},{5,37},{6,38},{7,39},{8,40},{9,... | collective-permute-start | bytes 36872 | tf_op jit(solution)/shard_map/ppermute | solution.py:25

commit v3 on v2

v3 whole, which is shorter than its diff:
```python
import jax
import jax.numpy as jnp
from jax import lax
from jax.experimental import pallas as pl
from jax.experimental.pallas import tpu as pltpu
from jax.sharding import PartitionSpec as P

AXES = ("sub", "row")
SHORT = jnp.bfloat16
FULL = jnp.float32


def place(x, y, z, c):
    return (x % 4) * 32 + (y % 4) * 8 + (z % 4) * 2 + c % 2


def send(value, dx=0, dy=0, dz=0, dc=0, turn=False):
    pairs = []
    for x in range(4):
        for y in range(4):
            for z in range(4):
                for c in range(2):
                    way = -1 if turn and c else 1
                    pairs.append((place(x, y, z, c), place(x + way * dx, y + way * dy, z + way * dz, c + dc)))
    return lax.ppermute(value, AXES, pairs)


def ring(value, axis, step, name):
    with jax.named_scope(name):
        return send(value, turn=True, **{"d" + axis: step})


def swap(value, name="swap"):
    with jax.named_scope(name):
        return send(value, dc=1)


def after(value, *earlier):
    return lax.optimization_barrier((value,) + earlier)[0]


def split(value):
    high = value.astype(SHORT)
    low = (value - high.astype(FULL)).astype(SHORT)
    return high, low


def dot3(a, b, dims):
    a_high, a_low = a
    b_high, b_low = b
    one = lambda u, v: lax.dot_general(u, v, (dims, ((), ())), preferred_element_type=FULL)
    return one(a_high, b_high) + (one(a_low, b_high) + one(a_high, b_low))


ROWS = ((1,), (0,))

LINES = ("a0", "a1", "a2", "a3", "b0", "b1", "b2", "b3")
BLOCKS = ("own", "sib", "za", "zb", "zc", "zu", "zs", "zt")


def work_table(x, y, z, core, way):
    unit = jnp.arange(32, dtype=jnp.int32)
    group, line, spot = unit // 16, unit // 4 % 4, unit % 4
    step = lambda k: jnp.where(k == 3, 2, jnp.where(k == 0, 0, 2 * k - 3))
    x_step = jnp.where(group == 0, step(spot), step(line))
    y_step = jnp.where(group == 0, step(line), step(spot))
    at_x = (x + way * x_step) & 3
    at_y = (y + way * y_step) & 3
    far = ((at_x - z) * way) & 3
    half = (far * 2 + ((at_y >> 1) ^ core)) * 2 + (at_y & 1)
    rank = jnp.where(line == 3, 2, jnp.where((line == 2) | (far == 2), 1, 0))
    early = jnp.sum((rank.reshape(2, 16) == 0).astype(jnp.int32), axis=1)
    key = (group * 3 + rank) * 32 + unit
    order = jnp.sum((key[None, :] < key[:, None]).astype(jnp.int32), axis=1)
    here = (order[None, :] == unit[:, None]).astype(jnp.int32)
    pick = lambda v: jnp.sum(here * v[None, :], axis=1)
    return jnp.stack([pick(unit), pick(half), pick(at_x * 4 + at_y)]), early


def pair_loop(begin, end, refs, table, mask, sums, meanwhile, s_buf, m_buf, spot, s_sem, m_sem):
    first_group = end[0] - begin[0]
    count = first_group + end[1] - begin[1]

    def start(q, slot):
        group = jnp.where(q < first_group, 0, 1)
        pair = jnp.where(q < first_group, begin[0] + q, begin[1] + q - first_group)
        spot[slot, 2] = group
        for part in range(2):
            entry = group * 16 + pair * 2 + part
            unit = table[0, entry]
            half = table[1, entry]
            spot[slot, part] = table[2, entry]
            s_target = s_buf.at[slot, :, pl.ds(part * 384, 384)]
            m_target = m_buf.at[slot, pl.ds(part * 384, 384), :]
            for number, name in enumerate(LINES):
                if name in refs:

                    @pl.when(unit >> 2 == number)
                    def _():
                        pltpu.make_async_copy(refs[name].at[unit & 3], s_target, s_sem.at[slot, part]).start()

            for number, name in enumerate(BLOCKS):
                if name in refs:

                    @pl.when(half >> 1 == number)
                    def _():
                        pltpu.make_async_copy(refs[name].at[half & 1], m_target, m_sem.at[slot, part]).start()

    def finish(slot):
        for part in range(2):
            target = s_buf.at[slot, :, pl.ds(part * 384, 384)]
            pltpu.make_async_copy(refs["a0"].at[0], target, s_sem.at[slot, part]).wait()
            target = m_buf.at[slot, pl.ds(part * 384, 384), :]
            pltpu.make_async_copy(refs["own"].at[0], target, m_sem.at[slot, part]).wait()
        pieces = []
        for part in range(2):
            block = spot[slot, part]
            for third in range(3):
                factor = mask[(block * 3 + third) >> 1].astype(FULL)
                pieces.append(m_buf[slot, pl.ds(part * 384 + third * 128, 128), :] * factor)
        part_sum = dot3(split(s_buf[slot]), split(jnp.concatenate(pieces, axis=0)), ROWS)
        group = spot[slot, 2]
        sums[group] = sums[group] + part_sum

    start(0, 0)
    if meanwhile is not None:
        meanwhile()

    def step(p, carry):
        @pl.when(p + 1 < count)
        def _():
            start(p + 1, (p + 1) % 2)

        finish(p % 2)
        return carry

    lax.fori_loop(0, count, step, 0)


HBM = pl.BlockSpec(memory_space=pl.ANY)
SMEM = pl.BlockSpec(memory_space=pltpu.SMEM)
VMEM = pl.BlockSpec(memory_space=pltpu.VMEM)


def buffers():
    return [
        pltpu.VMEM((2, 384, 768), FULL),
        pltpu.VMEM((2, 768, 768), FULL),
        pltpu.SMEM((2, 3), jnp.int32),
        pltpu.SemaphoreType.DMA((2, 2)),
        pltpu.SemaphoreType.DMA((2, 2)),
    ]


def shape(*dims):
    return jax.ShapeDtypeStruct(dims, FULL)


def cost(pairs):
    return pl.CostEstimate(flops=1_400_000_000 * pairs, bytes_accessed=3_600_000 * pairs, transcendentals=0)


def early_products(where, mask, table, pieces):
    names = list(pieces)

    def body(where_ref, mask_ref, table_ref, *rest):
        refs = dict(zip(names, rest))
        sums, *scratch = rest[len(names) :]

        def meanwhile():
            sums[...] = jnp.zeros_like(sums)

        end = (where_ref[6] // 2, where_ref[7] // 2)
        pair_loop((0, 0), end, refs, table_ref, mask_ref, sums, meanwhile, *scratch)

    return pl.pallas_call(
        body,
        out_shape=shape(2, 384, 768),
        in_specs=[SMEM, SMEM, SMEM] + [HBM] * len(names),
        out_specs=VMEM,
        scratch_shapes=buffers(),
        compiler_params=pltpu.CompilerParams(vmem_limit_bytes=60 << 20),
        cost_estimate=cost(6),
        name="early_products",
    )(where, mask, table, *pieces.values())


def middle_products(where, mask, table, pieces, before):
    names = list(pieces)

    def body(where_ref, mask_ref, table_ref, *rest):
        refs = dict(zip(names, rest))
        before_ref, own_ref, sums, own_high, own_low, sem, *scratch = rest[len(names) :]
        copy = pltpu.make_async_copy(before_ref, sums, sem)
        copy.start()

        def meanwhile():
            row = where_ref[5]
            tiles = [
                mask_ref[row * 3 + k].astype(FULL) * own_ref[pl.ds(k * 256, 256), :] for k in range(3)
            ]
            high, low = split(jnp.concatenate(tiles, axis=0).T)
            own_high[...] = high
            own_low[...] = low
            copy.wait()

        early = (where_ref[6] // 2, where_ref[7] // 2)
        pair_loop(early, (6, 6), refs, table_ref, mask_ref, sums, meanwhile, *scratch)

    half = jax.ShapeDtypeStruct((768, 768), SHORT)
    return pl.pallas_call(
        body,
        out_shape=(shape(2, 384, 768), half, half),
        in_specs=[SMEM, SMEM, SMEM] + [HBM] * (len(names) + 1) + [VMEM],
        out_specs=(VMEM, VMEM, VMEM),
        scratch_shapes=[pltpu.SemaphoreType.DMA] + buffers(),
        compiler_params=pltpu.CompilerParams(vmem_limit_bytes=60 << 20),
        cost_estimate=cost(6),
        name="middle_products",
    )(where, mask, table, *pieces.values(), before, pieces["own"].reshape(768, 768))


def last_products(where, mask, table, pieces, before, own_high, own_low, diag_here):
    names = list(pieces)

    def body(where_ref, mask_ref, table_ref, *rest):
        refs = dict(zip(names, rest))
        before_ref, high_ref, low_ref, diag_ref, sep, part_var, mine, other = rest[len(names) : len(names) + 8]
        sums, minus, high, low, sems, *scratch = rest[len(names) + 8 :]
        core = where_ref[3]
        copies = [
            pltpu.make_async_copy(before_ref, sums, sems.at[0]),
            pltpu.make_async_copy(high_ref, high, sems.at[1]),
            pltpu.make_async_copy(low_ref, low, sems.at[2]),
        ]

        def meanwhile():
            for copy in copies:
                copy.start()
            copies[0].wait()

        pair_loop((6, 6), (8, 8), refs, table_ref, mask_ref, sums, meanwhile, *scratch)
        product = jnp.concatenate([sums[0], sums[1]], axis=0)
        minus[...] = -product
        put = pltpu.make_async_copy(minus, sep, sems.at[3])
        put.start()
        copies[1].wait()
        copies[2].wait()
        update = dot3((high[...], low[...]), split(product), ROWS)
        row = lax.broadcasted_iota(jnp.int32, (768, 768), 0)
        column = lax.broadcasted_iota(jnp.int32, (768, 768), 1)
        part_var[...] = diag_ref[...] + jnp.sum(jnp.where(row == column, update, 0.0), axis=0, keepdims=True)
        for zz in range(4):
            lower = update[zz * 192 : zz * 192 + 96]
            upper = update[zz * 192 + 96 : zz * 192 + 192]

            @pl.when(core == 0)
            def _():
                mine[zz] = lower
                other[zz] = upper

            @pl.when(core != 0)
            def _():
                mine[zz] = upper
                other[zz] = lower

        put.wait()

    return pl.pallas_call(
        body,
        out_shape=(shape(768, 768), shape(1, 768), shape(4, 96, 768), shape(4, 96, 768)),
        in_specs=[SMEM, SMEM, SMEM] + [HBM] * (len(names) + 3) + [VMEM],
        out_specs=(HBM, VMEM, VMEM, VMEM),
        scratch_shapes=[
            pltpu.VMEM((2, 384, 768), FULL),
            pltpu.VMEM((768, 768), FULL),
            pltpu.VMEM((768, 768), SHORT),
            pltpu.VMEM((768, 768), SHORT),
            pltpu.SemaphoreType.DMA((4,)),
        ]
        + buffers(),
        compiler_params=pltpu.CompilerParams(vmem_limit_bytes=60 << 20),
        cost_estimate=cost(6),
        name="last_products",
    )(where, mask, table, *pieces.values(), before, own_high, own_low, diag_here)


def local(sigma_top, coupling, child_inverse, tile_mask, obs_node, obs_noise):
    sub = lax.axis_index("sub")
    row = lax.axis_index("row")
    x, y, z, core = sub // 4, sub % 4, row // 2, row % 2
    way = 1 - 2 * core
    table, early = work_table(x, y, z, core, way)
    where = jnp.concatenate([jnp.stack([x, y, z, core, way, row]).astype(jnp.int32), early])
    mask = tile_mask[0]

    inverse = child_inverse[0]
    column = lax.broadcasted_iota(jnp.int32, (96, 768), 1)
    line = lax.broadcasted_iota(jnp.int32, (96, 768), 0) + row * 96
    diag_here = jnp.sum(jnp.where(column == line, inverse, 0.0), axis=0, keepdims=True)
    child = obs_node // 768
    far_x = (child // 4 - x) % 4
    far_y = (child % 4 - y) % 4
    index = (far_x * 4 + far_y) * 768 + obs_node % 768

    a = sigma_top[:384]
    b = sigma_top[384:]
    m = coupling[0].reshape(2, 384, 768)
    za = ring(m, "z", -1, "p1z")
    xm, ym = ring(a, "x", 1, "p1"), ring(b, "y", 1, "p1")
    xp, yp = ring(a, "x", -1, "p1"), ring(b, "y", -1, "p1")

    one = (xm, ym, xp, yp)
    x2, y2 = ring(after(xm, *one), "x", 1, "p2"), ring(after(ym, *one), "y", 1, "p2")
    sib = swap(after(m, *one), "p2s")

    two = (x2, y2, sib, za)
    empty = jnp.zeros((1, 384, 384), FULL)
    a0 = jnp.concatenate([a[None], xm[None], xp[None], empty]).at[3].set(x2)
    b0 = jnp.concatenate([b[None], ym[None], yp[None], empty]).at[3].set(y2)
    a1, b1 = ring(after(a0, *two), "y", 1, "p3"), ring(after(b0, *two), "x", 1, "p3")
    zb = ring(after(sib, *two), "z", -1, "p3z")

    three = (a1, b1, zb, table, where, diag_here, index)
    a2, b2 = ring(after(a0, *three), "y", -1, "p4"), ring(after(b0, *three), "x", -1, "p4")
    zc = ring(after(za, *three), "z", -1, "p4z")
    zs = swap(after(zb, *three), "p4s")
    zt = swap(after(za, *three), "p4s")
    pieces = dict(a0=a0, a1=a1, b0=b0, b1=b1, own=m, sib=sib, za=za, zb=zb, zs=zs, zt=zt)
    sums = early_products(where, mask, table, pieces)

    four = (a2, b2, zc, zs, zt, sums)
    a3, b3 = ring(after(a1, *four), "y", 1, "p5"), ring(after(b1, *four), "x", 1, "p5")
    zu = swap(after(zc, *four), "p5s")
    pieces.update(a2=a2, b2=b2, zc=zc, zu=zu)
    sums, own_high, own_low = middle_products(where, mask, table, pieces, sums)

    pieces.update(a3=a3, b3=b3)
    sep, part_var, mine, other = last_products(where, mask, table, pieces, sums, own_high, own_low, diag_here)

    part = part_var + swap(part_var)
    half_sum = mine + swap(other)
    part = part + send(part, dz=1) + send(part, dz=-1) + send(part, dz=2)
    toward = lambda dz: lax.dynamic_index_in_dim(half_sum, (z + dz) % 4, 0, False)
    block_here = inverse + (toward(0) + send(toward(1), dz=1) + send(toward(-1), dz=-1) + send(toward(2), dz=2))
    part = after(part, half_sum)
    by_y = jnp.concatenate([part, send(part, dy=-1), send(part, dy=2), send(part, dy=1)], axis=0)
    by_xy = jnp.stack([by_y, send(by_y, dx=-1), send(by_y, dx=2), send(by_y, dx=1)])
    loo_var = by_xy.reshape(-1)[index] + obs_noise
    return sep[None], block_here[None], loo_var


def solution(mesh):
    placed = (
        P("row", "sub"),
        P("sub", "row", None),
        P("sub", "row", None),
        P("sub", None),
        P(("sub", "row")),
        P(("sub", "row")),
    )
    return jax.shard_map(
        local,
        mesh=mesh,
        in_specs=placed,
        out_specs=(P("sub", "row", None), P("sub", "row", None), P(("sub", "row"))),
        check_vma=False,
    )
```

time: 190 us -> 187 us (0.984)
  waiting for transfers between devices: 82.7 us -> 74.6 us
  starting transfers between devices: 40 us -> 44.5 us
    ppermute x31 -> x33, waiting for transfers between devices: 82.7 us -> 74.6 us  [send(): return lax.ppermute(value, AXES, pairs)]
    ppermute x31 -> x33, starting transfers between devices: 40 us -> 44.5 us  [send(): return lax.ppermute(value, AXES, pairs)]
    concatenate x1 -> x0, other arithmetic: 2.82 us -> none  [local(): zb = ring(after(jnp.concatenate([sib, za]), *two), 'z', -1, 'p3z')]
    concatenate x1, other arithmetic: 0.38 us -> 2.56 us  [local(): b0 = jnp.concatenate([b[None], ym[None], yp[None], empty]).at[3].set(y2)]
    unnamed x34 -> x16, local copies, waits for them, and re-layouts: 5.23 us -> 4.33 us
    pallas_call x4 -> x3, Pallas kernels: 48.3 us -> 48.6 us  [the longest x1 16.6 us: early_products(): pl.pallas_call(body, out_shape=shape(2, 384, 768), in_specs=[SMEM, SMEM,...]
  transfers between devices with their start and end apart: 31 -> 33, of which waited for: 10 -> 18; matrix products, arithmetic and copies ran while one was open for 4% -> 5% of each run, Pallas kernels for 17% -> 18%
where the time goes in v3:
time: 187 us; the launch traced here: 186 us
  waiting for transfers between devices  74.6 us (40%)
  Pallas kernels  48.6 us (26%)
  starting transfers between devices  44.5 us (24%)
  local copies, waits for them, and re-layouts  10.7 us (6%)
  other arithmetic  7.32 us (4%)
    ppermute x33, waiting for transfers between devices, send(): return lax.ppermute(value, AXES, pairs)  74.6 us
    ppermute x33, starting transfers between devices, send(): return lax.ppermute(value, AXES, pairs)  44.5 us
    pallas_call x1, Pallas kernels, early_products(): pl.pallas_call(body, out_shape=shape(2, 384, 768), in_specs=[SMEM, SMEM,...  16.6 us
    pallas_call x1, Pallas kernels, middle_products(): pl.pallas_call(body, out_shape=(shape(2, 384, 768), half, half), in_specs...  16.1 us
    pallas_call x1, Pallas kernels, last_products(): pl.pallas_call(body, out_shape=(shape(768, 768), shape(1, 768), shape(4,...  15.9 us
    unnamed x16, local copies, waits for them, and re-layouts  4.33 us
  transfers between devices with their start and end apart: 33, of which 18 were waited for; matrix products, arithmetic and copies ran while one was open for 5% of the time, Pallas kernels for 18%

profile of v3, /device:TPU:16, one launch (start us, length us, event | category | flops | bytes accessed | tf_op | source)
XLA Modules:
  0.0 186.5 jit_solution(16084471118387649705)
XLA Ops:
  0.6 1.5 slice_bitcast_fusion
  2.2 1.6 collective-permute-start
  3.8 1.7 collective-permute-start.1
  5.5 1.3 collective-permute-start.2
  6.8 0.7 collective-permute-start.3
  7.5 4.0 %collective-permute-start.7 = (f32[2,384,768]{2,1,0:T(8,128)S(1)}, f32[2,384,768]{2,1,0:T(8,128)S(1)}, u32[]{:S(2)}, u32[]{:S(2)}) collective-permute-start(f32[2,384,768]{2,1,0:T(8,128)S(1)} %bitcast.58), channel_id=1, source_target_pairs={{0,6},{1,3},{2,0},{3,5},{4,2},{5,7},{6,4},{7,1},{8,14},{9,11},{10,... | collective-permute-start | bytes 7077896 | tf_op jit(solution)/shard_map/p1z/ppermute | solution.py:25
  11.6 6.7 %collective-permute-done = f32[384,384]{1,0:T(8,128)S(1)} collective-permute-done((f32[384,384]{1,0:T(8,128)S(1)}, f32[384,384]{1,0:T(8,128)S(1)}, u32[]{:S(2)}, u32[]{:S(2)}) %collective-permute-start) | collective-permute-done | bytes 589856 | tf_op jit(solution)/shard_map/p1/ppermute | solution.py:25
  18.3 1.7 collective-permute-done.2
  20.0 2.3 %collective-permute-start.5 = (f32[384,384]{1,0:T(8,128)S(1)}, f32[384,384]{1,0:T(8,128)S(1)}, u32[]{:S(2)}, u32[]{:S(2)}) collective-permute-start(f32[384,384]{1,0:T(8,128)S(1)} %collective-permute-done.2), channel_id=1, source_target_pairs={{0,8},{1,25},{2,10},{3,27},{4,12},{5,29},{6,14},{7,31},{8,16},{9,1... | collective-permute-start | bytes 1769480 | tf_op jit(solution)/shard_map/p2/ppermute | solution.py:25
  22.9 2.6 %maximum_maximum_fusion.1 = (f32[4,384,384]{2,1,0:T(8,128)}, f32[4,384,384]{2,1,0:T(8,128)}) fusion(f32[1,384,384]{2,1,0:T(8,128)S(1)} %bitcast.63, f32[1,384,384]{2,1,0:T(8,128)S(1)} %bitcast.62, f32[1,384,384]{2,1,0:T(8,128)S(1)} %get-tuple-element.77, f32[4]{0:T(128)S(1)} %pad.19.clone, f32[1,384,384]{2,1,0:T(8,128)S(1)} %bitcast.61, ...), kind=kLoop, calls=%fused_computation.2 | loop fusion | flops 3538944 | bytes 8257552 | tf_op jit(solution)/shard_map/concatenate | solution.py:320
  25.4 4.4 %collective-permute-done.5 = f32[384,384]{1,0:T(8,128)S(1)} collective-permute-done((f32[384,384]{1,0:T(8,128)S(1)}, f32[384,384]{1,0:T(8,128)S(1)}, u32[]{:S(2)}, u32[]{:S(2)}) %collective-permute-start.5) | collective-permute-done | bytes 589856 | tf_op jit(solution)/shard_map/p2/ppermute | solution.py:25
  29.9 0.9 bitcast_dynamic-update-slice_fusion.rest_2_
  30.7 2.7 %collective-permute-done.4 = f32[384,384]{1,0:T(8,128)S(1)} collective-permute-done((f32[384,384]{1,0:T(8,128)S(1)}, f32[384,384]{1,0:T(8,128)S(1)}, u32[]{:S(2)}, u32[]{:S(2)}) %collective-permute-start.4) | collective-permute-done | bytes 589856 | tf_op jit(solution)/shard_map/p2/ppermute | solution.py:25
  33.5 0.8 bitcast_dynamic-update-slice_fusion.1.rest_0_
  34.3 3.6 %collective-permute-done.7.rest_6_ = f32[2,384,768]{2,1,0:T(8,128)S(1)} collective-permute-done((f32[2,384,768]{2,1,0:T(8,128)S(1)}, f32[2,384,768]{2,1,0:T(8,128)S(1)}, u32[]{:S(2)}, u32[]{:S(2)}) %collective-permute-start.7) | collective-permute-done | bytes 2359328 | tf_op jit(solution)/shard_map/p1z/ppermute | solution.py:25
  38.2 1.3 collective-permute-start.8
  39.5 3.7 %collective-permute-start.10 = (f32[2,384,768]{2,1,0:T(8,128)}, f32[2,384,768]{2,1,0:T(8,128)}, u32[]{:S(2)}, u32[]{:S(2)}) collective-permute-start(f32[2,384,768]{2,1,0:T(8,128)} %collective-permute-done.6.rest_5_), channel_id=1, source_target_pairs={{0,6},{1,3},{2,0},{3,5},{4,2},{5,7},{6,4},{7,1},{8,14},{9,11},{10,... | collective-permute-start | bytes 7077896 | tf_op jit(solution)/shard_map/p3z/ppermute | solution.py:25
  45.7 22.6 %collective-permute-done.9.rest_3_ = f32[4,384,384]{2,1,0:T(8,128)} collective-permute-done((f32[4,384,384]{2,1,0:T(8,128)}, f32[4,384,384]{2,1,0:T(8,128)}, u32[]{:S(2)}, u32[]{:S(2)}) %collective-permute-start.9) | collective-permute-done | bytes 2359328 | tf_op jit(solution)/shard_map/p3/ppermute | solution.py:25
  68.3 1.6 collective-permute-done.10.rest_7_
  70.4 3.0 %collective-permute-start.14 = (f32[4,384,384]{2,1,0:T(8,128)}, f32[4,384,384]{2,1,0:T(8,128)}, u32[]{:S(2)}, u32[]{:S(2)}) collective-permute-start(f32[4,384,384]{2,1,0:T(8,128)} %bitcast_dynamic-update-slice_fusion.rest_2_), channel_id=1, source_target_pairs={{0,96},{1,33},{2,98},{3,35},{4,100},{5,37},{6,102},{7,39},{8,104},... | collective-permute-start | bytes 7077896 | tf_op jit(solution)/shard_map/p4/ppermute | solution.py:25
  73.3 0.7 collective-permute-start.13
  74.1 3.7 %collective-permute-start.15 = (f32[2,384,768]{2,1,0:T(8,128)S(1)}, f32[2,384,768]{2,1,0:T(8,128)}, u32[]{:S(2)}, u32[]{:S(2)}) collective-permute-start(f32[2,384,768]{2,1,0:T(8,128)S(1)} %collective-permute-done.7.rest_6_), channel_id=1, source_target_pairs={{0,6},{1,3},{2,0},{3,5},{4,2},{5,7},{6,4},{7,1},{8,14},{9,11},{10,... | collective-permute-start | bytes 7077896 | tf_op jit(solution)/shard_map/p4z/ppermute | solution.py:25
  77.8 1.4 copy-done.2
  79.2 1.5 copy-done.3
  80.6 16.6 %early_products.1.rest_14_ = f32[2,384,768]{2,1,0:T(8,128)} custom-call(s32[8]{0:T(128)} %concatenate.16.where_ref, s32[24]{0:T(128)} %bitcast.70, s32[3,32]{1,0:T(4,128)} %pad_add_fusion.table_ref, f32[4,384,384]{2,1,0:T(8,128)} %bitcast_dynamic-update-slice_fusion.1.rest_0_, f32[4,384,384]{2,1,0:T(8,128)} %collective-permute-done.8.rest_1_, ...), custom_call_target="tpu_custom_call" | custom-call | flops 8400000000 | bytes 21600000 | tf_op jit(solution)/shard_map/early_products/pallas_call | solution.py:176
  97.2 2.8 %collective-permute-done.14.rest_11_ = f32[4,384,384]{2,1,0:T(8,128)} collective-permute-done((f32[4,384,384]{2,1,0:T(8,128)}, f32[4,384,384]{2,1,0:T(8,128)}, u32[]{:S(2)}, u32[]{:S(2)}) %collective-permute-start.14) | collective-permute-done | bytes 2359328 | tf_op jit(solution)/shard_map/p4/ppermute | solution.py:25
  100.0 2.5 %collective-permute-done.13.rest_10_ = f32[4,384,384]{2,1,0:T(8,128)} collective-permute-done((f32[4,384,384]{2,1,0:T(8,128)}, f32[4,384,384]{2,1,0:T(8,128)}, u32[]{:S(2)}, u32[]{:S(2)}) %collective-permute-start.13) | collective-permute-done | bytes 2359328 | tf_op jit(solution)/shard_map/p4/ppermute | solution.py:25
  102.5 1.6 collective-permute-done.15.rest_12_
  104.1 1.3 collective-permute-start.17
  105.4 3.5 %collective-permute-done.16.rest_13_ = f32[2,384,768]{2,1,0:T(8,128)S(1)} collective-permute-done((f32[2,384,768]{2,1,0:T(8,128)}, f32[2,384,768]{2,1,0:T(8,128)S(1)}, u32[]{:S(2)}, u32[]{:S(2)}) %collective-permute-start.16) | collective-permute-done | bytes 2359328 | tf_op jit(solution)/shard_map/p5s/ppermute | solution.py:25
  108.9 1.5 copy-done.4
  110.4 16.1 %middle_products.1 = (f32[2,384,768]{2,1,0:T(8,128)}, bf16[768,768]{1,0:T(8,128)(2,1)}, bf16[768,768]{1,0:T(8,128)(2,1)}) custom-call(s32[8]{0:T(128)} %concatenate.16.where_ref, s32[24]{0:T(128)} %bitcast.71, s32[3,32]{1,0:T(4,128)} %pad_add_fusion.table_ref, f32[4,384,384]{2,1,0:T(8,128)} %bitcast_dynamic-update-slice_fusion.1.rest_0_, ...), custom_call_target="tpu_custom_call" | custom-call | flops 8400000000 | bytes 21600000 | tf_op jit(solution)/shard_map/middle_products/pallas_call | solution.py:211
  126.5 8.0 %collective-permute-done.18.rest_15_ = f32[4,384,384]{2,1,0:T(8,128)} collective-permute-done((f32[4,384,384]{2,1,0:T(8,128)}, f32[4,384,384]{2,1,0:T(8,128)}, u32[]{:S(2)}, u32[]{:S(2)}) %collective-permute-start.18) | collective-permute-done | bytes 2359328 | tf_op jit(solution)/shard_map/p5/ppermute | solution.py:25
  134.5 15.9 %last_products.1 = (f32[768,768]{1,0:T(8,128)}, f32[1,768]{1,0:T(1,128)}, f32[4,96,768]{2,1,0:T(8,128)}, f32[4,96,768]{2,1,0:T(8,128)}) custom-call(s32[8]{0:T(128)} %concatenate.16.where_ref, s32[24]{0:T(128)} %bitcast.72, s32[3,32]{1,0:T(4,128)} %pad_add_fusion.table_ref, f32[4,384,384]{2,1,0:T(8,128)} %bitcast_dynamic-update-slice_fusion.1.rest_0_, ...), custom_call_target="tpu_custom_call" | custom-call | flops 8400000000 | bytes 21600000 | tf_op jit(solution)/shard_map/last_products/pallas_call | solution.py:269
  151.0 2.5 %collective-permute-done.23 = f32[1,768]{1,0:T(1,128)S(1)} collective-permute-done((f32[1,768]{1,0:T(1,128)}, f32[1,768]{1,0:T(1,128)S(1)}, u32[]{:S(2)}, u32[]{:S(2)}) %collective-permute-start.23) | collective-permute-done | bytes 3104 | tf_op jit(solution)/shard_map/swap/ppermute | solution.py:25
  154.2 3.8 %collective-permute-start.25 = (f32[1,768]{1,0:T(1,128)S(1)}, f32[1,768]{1,0:T(1,128)S(1)}, u32[]{:S(2)}, u32[]{:S(2)}) collective-permute-start(f32[1,768]{1,0:T(1,128)S(1)} %add.372), channel_id=1, source_target_pairs={{0,6},{1,7},{2,0},{3,1},{4,2},{5,3},{6,4},{7,5},{8,14},{9,15},{10,... | collective-permute-start | bytes 9224 | tf_op jit(solution)/shard_map/ppermute | solution.py:25
  158.0 1.5 collective-permute-start.26
  159.6 3.5 %collective-permute-done.26 = f32[1,768]{1,0:T(1,128)S(1)} collective-permute-done((f32[1,768]{1,0:T(1,128)S(1)}, f32[1,768]{1,0:T(1,128)S(1)}, u32[]{:S(2)}, u32[]{:S(2)}) %collective-permute-start.26) | collective-permute-done | bytes 3104 | tf_op jit(solution)/shard_map/ppermute | solution.py:25
  163.1 1.4 add.356
  165.1 2.9 %collective-permute-start.28 = (f32[1,768]{1,0:T(1,128)S(1)}, f32[1,768]{1,0:T(1,128)S(1)}, u32[]{:S(2)}, u32[]{:S(2)}) collective-permute-start(f32[1,768]{1,0:T(1,128)S(1)} %add_add_fusion), channel_id=1, source_target_pairs={{0,16},{1,17},{2,18},{3,19},{4,20},{5,21},{6,22},{7,23},{8,24},{9,... | collective-permute-start | bytes 9224 | tf_op jit(solution)/shard_map/ppermute | solution.py:25
  168.0 2.1 %collective-permute-start.29 = (f32[1,768]{1,0:T(1,128)S(1)}, f32[1,768]{1,0:T(1,128)S(1)}, u32[]{:S(2)}, u32[]{:S(2)}) collective-permute-start(f32[1,768]{1,0:T(1,128)S(1)} %add_add_fusion), channel_id=1, source_target_pairs={{0,8},{1,9},{2,10},{3,11},{4,12},{5,13},{6,14},{7,15},{8,16},{9,17... | collective-permute-start | bytes 9224 | tf_op jit(solution)/shard_map/ppermute | solution.py:25
  170.2 3.2 %collective-permute-start.21 = (f32[96,768]{1,0:T(8,128)S(1)}, f32[96,768]{1,0:T(8,128)S(1)}, u32[]{:S(2)}, u32[]{:S(2)}) collective-permute-start(f32[96,768]{1,0:T(8,128)S(1)} %get-tuple-element.76), channel_id=1, source_target_pairs={{0,6},{1,7},{2,0},{3,1},{4,2},{5,3},{6,4},{7,5},{8,14},{9,15},{10,... | collective-permute-start | bytes 884744 | tf_op jit(solution)/shard_map/ppermute | solution.py:25
  173.7 3.0 %collective-permute-start.30 = (f32[4,768]{1,0:T(4,128)S(1)}, f32[4,768]{1,0:T(4,128)S(1)}, u32[]{:S(2)}, u32[]{:S(2)}) collective-permute-start(f32[4,768]{1,0:T(4,128)S(1)} %get-tuple-element.82), channel_id=1, source_target_pairs={{0,96},{1,97},{2,98},{3,99},{4,100},{5,101},{6,102},{7,103},{8,104... | collective-permute-start | bytes 36872 | tf_op jit(solution)/shard_map/ppermute | solution.py:25
  176.7 1.4 collective-permute-done.30
  178.2 3.8 %collective-permute-done.31 = f32[4,768]{1,0:T(4,128)S(1)} collective-permute-done((f32[4,768]{1,0:T(4,128)S(1)}, f32[4,768]{1,0:T(4,128)S(1)}, u32[]{:S(2)}, u32[]{:S(2)}) %collective-permute-start.31) | collective-permute-done | bytes 12320 | tf_op jit(solution)/shard_map/ppermute | solution.py:25
  181.9 1.4 collective-permute-done.32
  183.3 1.7 gather_fusion
  185.7 0.8 fusion.3
  (64 shorter events, 6.8 us)
Async XLA Ops:
  0.6 6.9 %copy-start = (f32[1,768,768]{2,1,0:T(8,128)S(1)}, f32[1,768,768]{2,1,0:T(8,128)}, u32[]{:S(2)}) copy-start(f32[1,768,768]{2,1,0:T(8,128)} %param.11) | copy-start | bytes 7077892
  2.2 16.1 %collective-permute-start = (f32[384,384]{1,0:T(8,128)S(1)}, f32[384,384]{1,0:T(8,128)S(1)}, u32[]{:S(2)}, u32[]{:S(2)}) collective-permute-start(f32[384,384]{1,0:T(8,128)S(1)} %get-tuple-element.80), channel_id=1, source_target_pairs={{0,32},{1,97},{2,34},{3,99},{4,36},{5,101},{6,38},{7,103},{8,40},{... | collective-permute-start | bytes 1769480 | tf_op jit(solution)/shard_map/p1/ppermute | solution.py:25
  3.8 14.5 %collective-permute-start.1 = (f32[384,384]{1,0:T(8,128)S(1)}, f32[384,384]{1,0:T(8,128)S(1)}, u32[]{:S(2)}, u32[]{:S(2)}) collective-permute-start(f32[384,384]{1,0:T(8,128)S(1)} %get-tuple-element.80), channel_id=1, source_target_pairs={{0,96},{1,33},{2,98},{3,35},{4,100},{5,37},{6,102},{7,39},{8,104},... | collective-permute-start | bytes 1769480 | tf_op jit(solution)/shard_map/p1/ppermute | solution.py:25
  5.5 14.5 %collective-permute-start.2 = (f32[384,384]{1,0:T(8,128)S(1)}, f32[384,384]{1,0:T(8,128)S(1)}, u32[]{:S(2)}, u32[]{:S(2)}) collective-permute-start(f32[384,384]{1,0:T(8,128)S(1)} %get-tuple-element.79), channel_id=1, source_target_pairs={{0,8},{1,25},{2,10},{3,27},{4,12},{5,29},{6,14},{7,31},{8,16},{9,1... | collective-permute-start | bytes 1769480 | tf_op jit(solution)/shard_map/p1/ppermute | solution.py:25
  6.8 13.2 %collective-permute-start.3 = (f32[384,384]{1,0:T(8,128)S(1)}, f32[384,384]{1,0:T(8,128)S(1)}, u32[]{:S(2)}, u32[]{:S(2)}) collective-permute-start(f32[384,384]{1,0:T(8,128)S(1)} %get-tuple-element.79), channel_id=1, source_target_pairs={{0,24},{1,9},{2,26},{3,11},{4,28},{5,13},{6,30},{7,15},{8,0},{9,17... | collective-permute-start | bytes 1769480 | tf_op jit(solution)/shard_map/p1/ppermute | solution.py:25
  7.5 30.4 %collective-permute-start.7 = (f32[2,384,768]{2,1,0:T(8,128)S(1)}, f32[2,384,768]{2,1,0:T(8,128)S(1)}, u32[]{:S(2)}, u32[]{:S(2)}) collective-permute-start(f32[2,384,768]{2,1,0:T(8,128)S(1)} %bitcast.58), channel_id=1, source_target_pairs={{0,6},{1,3},{2,0},{3,5},{4,2},{5,7},{6,4},{7,1},{8,14},{9,11},{10,... | collective-permute-start | bytes 7077896 | tf_op jit(solution)/shard_map/p1z/ppermute | solution.py:25
  20.0 17.9 %collective-permute-start.6 = (f32[2,384,768]{2,1,0:T(8,128)S(1)}, f32[2,384,768]{2,1,0:T(8,128)}, u32[]{:S(2)}, u32[]{:S(2)}) collective-permute-start(f32[2,384,768]{2,1,0:T(8,128)S(1)} %bitcast.59), channel_id=1, source_target_pairs={{0,1},{1,0},{2,3},{3,2},{4,5},{5,4},{6,7},{7,6},{8,9},{9,8},{10,11... | collective-permute-start | bytes 7077896 | tf_op jit(solution)/shard_map/p2s/ppermute | solution.py:25
  20.0 9.9 %collective-permute-start.5 = (f32[384,384]{1,0:T(8,128)S(1)}, f32[384,384]{1,0:T(8,128)S(1)}, u32[]{:S(2)}, u32[]{:S(2)}) collective-permute-start(f32[384,384]{1,0:T(8,128)S(1)} %collective-permute-done.2), channel_id=1, source_target_pairs={{0,8},{1,25},{2,10},{3,27},{4,12},{5,29},{6,14},{7,31},{8,16},{9,1... | collective-permute-start | bytes 1769480 | tf_op jit(solution)/shard_map/p2/ppermute | solution.py:25
  22.4 11.1 %collective-permute-start.4 = (f32[384,384]{1,0:T(8,128)S(1)}, f32[384,384]{1,0:T(8,128)S(1)}, u32[]{:S(2)}, u32[]{:S(2)}) collective-permute-start(f32[384,384]{1,0:T(8,128)S(1)} %collective-permute-done), channel_id=1, source_target_pairs={{0,32},{1,97},{2,34},{3,99},{4,36},{5,101},{6,38},{7,103},{8,40},{... | collective-permute-start | bytes 1769480 | tf_op jit(solution)/shard_map/p2/ppermute | solution.py:25
  25.4 17.8 %copy-start.5 = (f32[1,96,768]{2,1,0:T(8,128)S(1)}, f32[1,96,768]{2,1,0:T(8,128)}, u32[]{:S(2)}) copy-start(f32[1,96,768]{2,1,0:T(8,128)} %param.12) | copy-start | bytes 884740
  25.4 20.2 %copy-start.6 = (s32[256]{0:T(256)S(1)}, s32[256]{0:T(256)}, u32[]{:S(2)}) copy-start(s32[256]{0:T(256)} %param.14) | copy-start | bytes 3076
  37.9 42.7 %copy-start.1 = (f32[2,384,768]{2,1,0:T(8,128)}, f32[2,384,768]{2,1,0:T(8,128)S(1)}, u32[]{:S(2)}) copy-start(f32[2,384,768]{2,1,0:T(8,128)S(1)} %collective-permute-done.7.rest_6_) | copy-start | bytes 7077892
  37.9 30.4 %collective-permute-start.9 = (f32[4,384,384]{2,1,0:T(8,128)}, f32[4,384,384]{2,1,0:T(8,128)}, u32[]{:S(2)}, u32[]{:S(2)}) collective-permute-start(f32[4,384,384]{2,1,0:T(8,128)} %bitcast_dynamic-update-slice_fusion.rest_2_), channel_id=1, source_target_pairs={{0,32},{1,97},{2,34},{3,99},{4,36},{5,101},{6,38},{7,103},{8,40},{... | collective-permute-start | bytes 7077896 | tf_op jit(solution)/shard_map/p3/ppermute | solution.py:25
  38.2 30.1 %collective-permute-start.8 = (f32[4,384,384]{2,1,0:T(8,128)}, f32[4,384,384]{2,1,0:T(8,128)}, u32[]{:S(2)}, u32[]{:S(2)}) collective-permute-start(f32[4,384,384]{2,1,0:T(8,128)} %bitcast_dynamic-update-slice_fusion.1.rest_0_), channel_id=1, source_target_pairs={{0,8},{1,25},{2,10},{3,27},{4,12},{5,29},{6,14},{7,31},{8,16},{9,1... | collective-permute-start | bytes 7077896 | tf_op jit(solution)/shard_map/p3/ppermute | solution.py:25
  39.5 30.4 %collective-permute-start.10 = (f32[2,384,768]{2,1,0:T(8,128)}, f32[2,384,768]{2,1,0:T(8,128)}, u32[]{:S(2)}, u32[]{:S(2)}) collective-permute-start(f32[2,384,768]{2,1,0:T(8,128)} %collective-permute-done.6.rest_5_), channel_id=1, source_target_pairs={{0,6},{1,3},{2,0},{3,5},{4,2},{5,7},{6,4},{7,1},{8,14},{9,11},{10,... | collective-permute-start | bytes 7077896 | tf_op jit(solution)/shard_map/p3z/ppermute | solution.py:25
  69.9 7.9 %collective-permute-start.12 = (f32[2,384,768]{2,1,0:T(8,128)S(1)}, f32[2,384,768]{2,1,0:T(8,128)S(1)}, u32[]{:S(2)}, u32[]{:S(2)}) collective-permute-start(f32[2,384,768]{2,1,0:T(8,128)S(1)} %collective-permute-done.7.rest_6_), channel_id=1, source_target_pairs={{0,1},{1,0},{2,3},{3,2},{4,5},{5,4},{6,7},{7,6},{8,9},{9,8},{10,11... | collective-permute-start | bytes 7077896 | tf_op jit(solution)/shard_map/p4s/ppermute | solution.py:25
  69.9 9.3 %collective-permute-start.11 = (f32[2,384,768]{2,1,0:T(8,128)}, f32[2,384,768]{2,1,0:T(8,128)S(1)}, u32[]{:S(2)}, u32[]{:S(2)}) collective-permute-start(f32[2,384,768]{2,1,0:T(8,128)} %collective-permute-done.10.rest_7_), channel_id=1, source_target_pairs={{0,1},{1,0},{2,3},{3,2},{4,5},{5,4},{6,7},{7,6},{8,9},{9,8},{10,11... | collective-permute-start | bytes 7077896 | tf_op jit(solution)/shard_map/p4s/ppermute | solution.py:25
  70.4 29.6 %collective-permute-start.14 = (f32[4,384,384]{2,1,0:T(8,128)}, f32[4,384,384]{2,1,0:T(8,128)}, u32[]{:S(2)}, u32[]{:S(2)}) collective-permute-start(f32[4,384,384]{2,1,0:T(8,128)} %bitcast_dynamic-update-slice_fusion.rest_2_), channel_id=1, source_target_pairs={{0,96},{1,33},{2,98},{3,35},{4,100},{5,37},{6,102},{7,39},{8,104},... | collective-permute-start | bytes 7077896 | tf_op jit(solution)/shard_map/p4/ppermute | solution.py:25
  73.3 29.2 %collective-permute-start.13 = (f32[4,384,384]{2,1,0:T(8,128)}, f32[4,384,384]{2,1,0:T(8,128)}, u32[]{:S(2)}, u32[]{:S(2)}) collective-permute-start(f32[4,384,384]{2,1,0:T(8,128)} %bitcast_dynamic-update-slice_fusion.1.rest_0_), channel_id=1, source_target_pairs={{0,24},{1,9},{2,26},{3,11},{4,28},{5,13},{6,30},{7,15},{8,0},{9,17... | collective-permute-start | bytes 7077896 | tf_op jit(solution)/shard_map/p4/ppermute | solution.py:25
  74.1 30.1 %collective-permute-start.15 = (f32[2,384,768]{2,1,0:T(8,128)S(1)}, f32[2,384,768]{2,1,0:T(8,128)}, u32[]{:S(2)}, u32[]{:S(2)}) collective-permute-start(f32[2,384,768]{2,1,0:T(8,128)S(1)} %collective-permute-done.7.rest_6_), channel_id=1, source_target_pairs={{0,6},{1,3},{2,0},{3,5},{4,2},{5,7},{6,4},{7,1},{8,14},{9,11},{10,... | collective-permute-start | bytes 7077896 | tf_op jit(solution)/shard_map/p4z/ppermute | solution.py:25
  77.8 1.4 copy-start.2
  79.2 1.5 copy-start.3
  104.1 4.7 %collective-permute-start.16 = (f32[2,384,768]{2,1,0:T(8,128)}, f32[2,384,768]{2,1,0:T(8,128)S(1)}, u32[]{:S(2)}, u32[]{:S(2)}) collective-permute-start(f32[2,384,768]{2,1,0:T(8,128)} %collective-permute-done.15.rest_12_), channel_id=1, source_target_pairs={{0,1},{1,0},{2,3},{3,2},{4,5},{5,4},{6,7},{7,6},{8,9},{9,8},{10,11... | collective-permute-start | bytes 7077896 | tf_op jit(solution)/shard_map/p5s/ppermute | solution.py:25
  104.1 30.4 %collective-permute-start.18 = (f32[4,384,384]{2,1,0:T(8,128)}, f32[4,384,384]{2,1,0:T(8,128)}, u32[]{:S(2)}, u32[]{:S(2)}) collective-permute-start(f32[4,384,384]{2,1,0:T(8,128)} %collective-permute-done.9.rest_3_), channel_id=1, source_target_pairs={{0,32},{1,97},{2,34},{3,99},{4,36},{5,101},{6,38},{7,103},{8,40},{... | collective-permute-start | bytes 7077896 | tf_op jit(solution)/shard_map/p5/ppermute | solution.py:25
  104.1 30.4 %collective-permute-start.17 = (f32[4,384,384]{2,1,0:T(8,128)}, f32[4,384,384]{2,1,0:T(8,128)}, u32[]{:S(2)}, u32[]{:S(2)}) collective-permute-start(f32[4,384,384]{2,1,0:T(8,128)} %collective-permute-done.8.rest_1_), channel_id=1, source_target_pairs={{0,8},{1,25},{2,10},{3,27},{4,12},{5,29},{6,14},{7,31},{8,16},{9,1... | collective-permute-start | bytes 7077896 | tf_op jit(solution)/shard_map/p5/ppermute | solution.py:25
  108.9 1.5 copy-start.4
  150.4 12.7 %collective-permute-start.19 = (f32[4,96,768]{2,1,0:T(8,128)}, f32[4,96,768]{2,1,0:T(8,128)S(1)}, u32[]{:S(2)}, u32[]{:S(2)}) collective-permute-start(f32[4,96,768]{2,1,0:T(8,128)} %get-tuple-element.66), channel_id=1, source_target_pairs={{0,1},{1,0},{2,3},{3,2},{4,5},{5,4},{6,7},{7,6},{8,9},{9,8},{10,11... | collective-permute-start | bytes 3538952 | tf_op jit(solution)/shard_map/swap/ppermute | solution.py:25
  150.5 3.0 %collective-permute-start.23 = (f32[1,768]{1,0:T(1,128)}, f32[1,768]{1,0:T(1,128)S(1)}, u32[]{:S(2)}, u32[]{:S(2)}) collective-permute-start(f32[1,768]{1,0:T(1,128)} %get-tuple-element.67), channel_id=1, source_target_pairs={{0,1},{1,0},{2,3},{3,2},{4,5},{5,4},{6,7},{7,6},{8,9},{9,8},{10,11... | collective-permute-start | bytes 9224 | tf_op jit(solution)/shard_map/swap/ppermute | solution.py:25
  154.2 5.4 %collective-permute-start.24 = (f32[1,768]{1,0:T(1,128)S(1)}, f32[1,768]{1,0:T(1,128)S(1)}, u32[]{:S(2)}, u32[]{:S(2)}) collective-permute-start(f32[1,768]{1,0:T(1,128)S(1)} %add.372), channel_id=1, source_target_pairs={{0,2},{1,3},{2,4},{3,5},{4,6},{5,7},{6,0},{7,1},{8,10},{9,11},{10,... | collective-permute-start | bytes 9224 | tf_op jit(solution)/shard_map/ppermute | solution.py:25
  154.2 5.4 %collective-permute-start.25 = (f32[1,768]{1,0:T(1,128)S(1)}, f32[1,768]{1,0:T(1,128)S(1)}, u32[]{:S(2)}, u32[]{:S(2)}) collective-permute-start(f32[1,768]{1,0:T(1,128)S(1)} %add.372), channel_id=1, source_target_pairs={{0,6},{1,7},{2,0},{3,1},{4,2},{5,3},{6,4},{7,5},{8,14},{9,15},{10,... | collective-permute-start | bytes 9224 | tf_op jit(solution)/shard_map/ppermute | solution.py:25
  158.0 5.1 %collective-permute-start.26 = (f32[1,768]{1,0:T(1,128)S(1)}, f32[1,768]{1,0:T(1,128)S(1)}, u32[]{:S(2)}, u32[]{:S(2)}) collective-permute-start(f32[1,768]{1,0:T(1,128)S(1)} %add.372), channel_id=1, source_target_pairs={{0,4},{1,5},{2,6},{3,7},{4,0},{5,1},{6,2},{7,3},{8,12},{9,13},{10,... | collective-permute-start | bytes 9224 | tf_op jit(solution)/shard_map/ppermute | solution.py:25
  164.5 20.5 %copy-start.7 = (f32[256]{0:T(256)S(1)}, f32[256]{0:T(256)}, u32[]{:S(2)}) copy-start(f32[256]{0:T(256)} %param.15) | copy-start | bytes 3076
  164.6 8.9 %collective-permute-start.27 = (f32[1,768]{1,0:T(1,128)S(1)}, f32[1,768]{1,0:T(1,128)S(1)}, u32[]{:S(2)}, u32[]{:S(2)}) collective-permute-start(f32[1,768]{1,0:T(1,128)S(1)} %add_add_fusion), channel_id=1, source_target_pairs={{0,24},{1,25},{2,26},{3,27},{4,28},{5,29},{6,30},{7,31},{8,0},{9,1... | collective-permute-start | bytes 9224 | tf_op jit(solution)/shard_map/ppermute | solution.py:25
  165.1 8.6 %collective-permute-start.28 = (f32[1,768]{1,0:T(1,128)S(1)}, f32[1,768]{1,0:T(1,128)S(1)}, u32[]{:S(2)}, u32[]{:S(2)}) collective-permute-start(f32[1,768]{1,0:T(1,128)S(1)} %add_add_fusion), channel_id=1, source_target_pairs={{0,16},{1,17},{2,18},{3,19},{4,20},{5,21},{6,22},{7,23},{8,24},{9,... | collective-permute-start | bytes 9224 | tf_op jit(solution)/shard_map/ppermute | solution.py:25
  168.0 5.7 %collective-permute-start.29 = (f32[1,768]{1,0:T(1,128)S(1)}, f32[1,768]{1,0:T(1,128)S(1)}, u32[]{:S(2)}, u32[]{:S(2)}) collective-permute-start(f32[1,768]{1,0:T(1,128)S(1)} %add_add_fusion), channel_id=1, source_target_pairs={{0,8},{1,9},{2,10},{3,11},{4,12},{5,13},{6,14},{7,15},{8,16},{9,17... | collective-permute-start | bytes 9224 | tf_op jit(solution)/shard_map/ppermute | solution.py:25
  170.1 15.5 %collective-permute-start.20 = (f32[96,768]{1,0:T(8,128)S(1)}, f32[96,768]{1,0:T(8,128)S(1)}, u32[]{:S(2)}, u32[]{:S(2)}) collective-permute-start(f32[96,768]{1,0:T(8,128)S(1)} %get-tuple-element.74), channel_id=1, source_target_pairs={{0,2},{1,3},{2,4},{3,5},{4,6},{5,7},{6,0},{7,1},{8,10},{9,11},{10,... | collective-permute-start | bytes 884744 | tf_op jit(solution)/shard_map/ppermute | solution.py:25
  170.2 15.5 %collective-permute-start.21 = (f32[96,768]{1,0:T(8,128)S(1)}, f32[96,768]{1,0:T(8,128)S(1)}, u32[]{:S(2)}, u32[]{:S(2)}) collective-permute-start(f32[96,768]{1,0:T(8,128)S(1)} %get-tuple-element.76), channel_id=1, source_target_pairs={{0,6},{1,7},{2,0},{3,1},{4,2},{5,3},{6,4},{7,5},{8,14},{9,15},{10,... | collective-permute-start | bytes 884744 | tf_op jit(solution)/shard_map/ppermute | solution.py:25
  173.4 12.2 %collective-permute-start.22 = (f32[96,768]{1,0:T(8,128)S(1)}, f32[96,768]{1,0:T(8,128)S(1)}, u32[]{:S(2)}, u32[]{:S(2)}) collective-permute-start(f32[96,768]{1,0:T(8,128)S(1)} %get-tuple-element.75), channel_id=1, source_target_pairs={{0,4},{1,5},{2,6},{3,7},{4,0},{5,1},{6,2},{7,3},{8,12},{9,13},{10,... | collective-permute-start | bytes 884744 | tf_op jit(solution)/shard_map/ppermute | solution.py:25
  173.7 4.4 %collective-permute-start.30 = (f32[4,768]{1,0:T(4,128)S(1)}, f32[4,768]{1,0:T(4,128)S(1)}, u32[]{:S(2)}, u32[]{:S(2)}) collective-permute-start(f32[4,768]{1,0:T(4,128)S(1)} %get-tuple-element.82), channel_id=1, source_target_pairs={{0,96},{1,97},{2,98},{3,99},{4,100},{5,101},{6,102},{7,103},{8,104... | collective-permute-start | bytes 36872 | tf_op jit(solution)/shard_map/ppermute | solution.py:25
  176.7 5.2 %collective-permute-start.31 = (f32[4,768]{1,0:T(4,128)S(1)}, f32[4,768]{1,0:T(4,128)S(1)}, u32[]{:S(2)}, u32[]{:S(2)}) collective-permute-start(f32[4,768]{1,0:T(4,128)S(1)} %get-tuple-element.82), channel_id=1, source_target_pairs={{0,64},{1,65},{2,66},{3,67},{4,68},{5,69},{6,70},{7,71},{8,72},{9,... | collective-permute-start | bytes 36872 | tf_op jit(solution)/shard_map/ppermute | solution.py:25
  178.1 5.2 %collective-permute-start.32 = (f32[4,768]{1,0:T(4,128)S(1)}, f32[4,768]{1,0:T(4,128)S(1)}, u32[]{:S(2)}, u32[]{:S(2)}) collective-permute-start(f32[4,768]{1,0:T(4,128)S(1)} %get-tuple-element.82), channel_id=1, source_target_pairs={{0,32},{1,33},{2,34},{3,35},{4,36},{5,37},{6,38},{7,39},{8,40},{9,... | collective-permute-start | bytes 36872 | tf_op jit(solution)/shard_map/ppermute | solution.py:25

commit v4 on v3

--- a/solution.py
+++ b/solution.py
@@ -53,6 +53,7 @@
 
 
 ROWS = ((1,), (0,))
+SLOTS = 3
 
 LINES = ("a0", "a1", "a2", "a3", "b0", "b1", "b2", "b3")
 BLOCKS = ("own", "sib", "za", "zb", "zc", "zu", "zs", "zt")
@@ -66,7 +67,7 @@
     y_step = jnp.where(group == 0, step(line), step(spot))
     at_x = (x + way * x_step) & 3
     at_y = (y + way * y_step) & 3
-    far = ((at_x - z) * way) & 3
+    far = ((z - at_x) * way) & 3
     half = (far * 2 + ((at_y >> 1) ^ core)) * 2 + (at_y & 1)
     rank = jnp.where(line == 3, 2, jnp.where((line == 2) | (far == 2), 1, 0))
     early = jnp.sum((rank.reshape(2, 16) == 0).astype(jnp.int32), axis=1)
@@ -109,7 +110,7 @@
     def finish(slot):
         for part in range(2):
             target = s_buf.at[slot, :, pl.ds(part * 384, 384)]
-            pltpu.make_async_copy(refs["a0"].at[0], target, s_sem.at[slot, part]).wait()
+            pltpu.make_async_copy(refs["b0" if "b0" in refs else "b3"].at[0], target, s_sem.at[slot, part]).wait()
             target = m_buf.at[slot, pl.ds(part * 384, 384), :]
             pltpu.make_async_copy(refs["own"].at[0], target, m_sem.at[slot, part]).wait()
         pieces = []
@@ -122,16 +123,23 @@
         group = spot[slot, 2]
         sums[group] = sums[group] + part_sum
 
-    start(0, 0)
+    for ahead in range(SLOTS - 1):
+
+        @pl.when(ahead < count)
+        def _():
+            start(ahead, ahead)
+
     if meanwhile is not None:
         meanwhile()
 
     def step(p, carry):
-        @pl.when(p + 1 < count)
+        later = p + SLOTS - 1
+
+        @pl.when(later < count)
         def _():
-            start(p + 1, (p + 1) % 2)
-
-        finish(p % 2)
+            start(later, lax.rem(later, SLOTS))
+
+        finish(lax.rem(p, SLOTS))
         return carry
 
     lax.fori_loop(0, count, step, 0)
@@ -144,11 +152,11 @@
 
 def buffers():
     return [
-        pltpu.VMEM((2, 384, 768), FULL),
-        pltpu.VMEM((2, 768, 768), FULL),
-        pltpu.SMEM((2, 3), jnp.int32),
-        pltpu.SemaphoreType.DMA((2, 2)),
-        pltpu.SemaphoreType.DMA((2, 2)),
+        pltpu.VMEM((SLOTS, 384, 768), FULL),
+        pltpu.VMEM((SLOTS, 768, 768), FULL),
+        pltpu.SMEM((SLOTS, 3), jnp.int32),
+        pltpu.SemaphoreType.DMA((SLOTS, 2)),
+        pltpu.SemaphoreType.DMA((SLOTS, 2)),
     ]
 
 
@@ -306,7 +314,7 @@
     a = sigma_top[:384]
     b = sigma_top[384:]
     m = coupling[0].reshape(2, 384, 768)
-    za = ring(m, "z", -1, "p1z")
+    za = ring(m, "z", 1, "p1z")
     xm, ym = ring(a, "x", 1, "p1"), ring(b, "y", 1, "p1")
     xp, yp = ring(a, "x", -1, "p1"), ring(b, "y", -1, "p1")
 
@@ -319,11 +327,11 @@
     a0 = jnp.concatenate([a[None], xm[None], xp[None], empty]).at[3].set(x2)
     b0 = jnp.concatenate([b[None], ym[None], yp[None], empty]).at[3].set(y2)
     a1, b1 = ring(after(a0, *two), "y", 1, "p3"), ring(after(b0, *two), "x", 1, "p3")
-    zb = ring(after(sib, *two), "z", -1, "p3z")
+    zb = ring(after(sib, *two), "z", 1, "p3z")
 
     three = (a1, b1, zb, table, where, diag_here, index)
     a2, b2 = ring(after(a0, *three), "y", -1, "p4"), ring(after(b0, *three), "x", -1, "p4")
-    zc = ring(after(za, *three), "z", -1, "p4z")
+    zc = ring(after(za, *three), "z", 1, "p4z")
     zs = swap(after(zb, *three), "p4s")
     zt = swap(after(za, *three), "p4s")
     pieces = dict(a0=a0, a1=a1, b0=b0, b1=b1, own=m, sib=sib, za=za, zb=zb, zs=zs, zt=zt)
@@ -336,7 +344,8 @@
     sums, own_high, own_low = middle_products(where, mask, table, pieces, sums)
 
     pieces.update(a3=a3, b3=b3)
-    sep, part_var, mine, other = last_products(where, mask, table, pieces, sums, own_high, own_low, diag_here)
+    final = {name: pieces[name] for name in BLOCKS + ("a3", "b3")}
+    sep, part_var, mine, other = last_products(where, mask, table, final, sums, own_high, own_low, diag_here)
 
     part = part_var + swap(part_var)
     half_sum = mine + swap(other)

time: 187 us -> 187 us (level)
  waiting for transfers between devices: 74.6 us -> 88.1 us
  starting transfers between devices: 44.5 us -> 32.7 us
  Pallas kernels: 48.6 us -> 46.7 us
    ppermute x33, waiting for transfers between devices: 74.6 us -> 88.1 us  [send(): return lax.ppermute(value, AXES, pairs)]
    ppermute x33, starting transfers between devices: 44.5 us -> 32.7 us  [send(): return lax.ppermute(value, AXES, pairs)]
  transfers between devices with their start and end apart: 33 -> 33, of which waited for: 18 -> 19; matrix products, arithmetic and copies ran while one was open for 5% -> 5% of each run, Pallas kernels for 18% -> 16%
where the time goes in v4:
time: 187 us; the launch traced here: 186 us
  waiting for transfers between devices  88.1 us (47%)
  Pallas kernels  46.7 us (25%)
  starting transfers between devices  32.7 us (17%)
  local copies, waits for them, and re-layouts  10.6 us (6%)
  other arithmetic  7.37 us (4%)
    ppermute x33, waiting for transfers between devices, send(): return lax.ppermute(value, AXES, pairs)  88.1 us
    ppermute x33, starting transfers between devices, send(): return lax.ppermute(value, AXES, pairs)  32.7 us
    pallas_call x1, Pallas kernels, last_products(): pl.pallas_call(body, out_shape=(shape(768, 768), shape(1, 768), shape(4,...  16 us
    pallas_call x1, Pallas kernels, early_products(): pl.pallas_call(body, out_shape=shape(2, 384, 768), in_specs=[SMEM, SMEM,...  15.7 us
    pallas_call x1, Pallas kernels, middle_products(): pl.pallas_call(body, out_shape=(shape(2, 384, 768), half, half), in_specs...  15 us
    unnamed x16, local copies, waits for them, and re-layouts  4.24 us
  transfers between devices with their start and end apart: 33, of which 19 were waited for; matrix products, arithmetic and copies ran while one was open for 5% of the time, Pallas kernels for 16%

profile of v4, /device:TPU:16, one launch (start us, length us, event | category | flops | bytes accessed | tf_op | source)
XLA Modules:
  0.0 186.3 jit_solution(4949104428987489782)
XLA Ops:
  0.6 1.5 slice_bitcast_fusion
  2.2 1.6 collective-permute-start
  3.8 1.7 collective-permute-start.2
  5.5 1.3 collective-permute-start.1
  6.8 0.7 collective-permute-start.3
  7.5 1.9 %collective-permute-start.5 = (f32[2,384,768]{2,1,0:T(8,128)S(1)}, f32[2,384,768]{2,1,0:T(8,128)S(1)}, u32[]{:S(2)}, u32[]{:S(2)}) collective-permute-start(f32[2,384,768]{2,1,0:T(8,128)S(1)} %bitcast.58), channel_id=1, source_target_pairs={{0,2},{1,7},{2,4},{3,1},{4,6},{5,3},{6,0},{7,5},{8,10},{9,15},{10,... | collective-permute-start | bytes 7077896 | tf_op jit(solution)/shard_map/p1z/ppermute | solution.py:25
  9.4 8.8 %collective-permute-done = f32[384,384]{1,0:T(8,128)S(1)} collective-permute-done((f32[384,384]{1,0:T(8,128)S(1)}, f32[384,384]{1,0:T(8,128)S(1)}, u32[]{:S(2)}, u32[]{:S(2)}) %collective-permute-start) | collective-permute-done | bytes 589856 | tf_op jit(solution)/shard_map/p1/ppermute | solution.py:25
  18.3 1.7 collective-permute-done.1
  20.0 2.3 %collective-permute-start.7 = (f32[384,384]{1,0:T(8,128)S(1)}, f32[384,384]{1,0:T(8,128)S(1)}, u32[]{:S(2)}, u32[]{:S(2)}) collective-permute-start(f32[384,384]{1,0:T(8,128)S(1)} %collective-permute-done.1), channel_id=1, source_target_pairs={{0,8},{1,25},{2,10},{3,27},{4,12},{5,29},{6,14},{7,31},{8,16},{9,1... | collective-permute-start | bytes 1769480 | tf_op jit(solution)/shard_map/p2/ppermute | solution.py:25
  22.9 2.6 %maximum_maximum_fusion.1 = (f32[4,384,384]{2,1,0:T(8,128)}, f32[4,384,384]{2,1,0:T(8,128)}) fusion(f32[1,384,384]{2,1,0:T(8,128)S(1)} %bitcast.63, f32[1,384,384]{2,1,0:T(8,128)S(1)} %bitcast.62, f32[1,384,384]{2,1,0:T(8,128)S(1)} %get-tuple-element.77, f32[4]{0:T(128)S(1)} %pad.19.clone, f32[1,384,384]{2,1,0:T(8,128)S(1)} %bitcast.61, ...), kind=kLoop, calls=%fused_computation.2 | loop fusion | flops 3538944 | bytes 8257552 | tf_op jit(solution)/shard_map/concatenate | solution.py:328
  25.5 4.4 %collective-permute-done.7 = f32[384,384]{1,0:T(8,128)S(1)} collective-permute-done((f32[384,384]{1,0:T(8,128)S(1)}, f32[384,384]{1,0:T(8,128)S(1)}, u32[]{:S(2)}, u32[]{:S(2)}) %collective-permute-start.7) | collective-permute-done | bytes 589856 | tf_op jit(solution)/shard_map/p2/ppermute | solution.py:25
  29.9 0.9 bitcast_dynamic-update-slice_fusion.rest_2_
  30.7 2.8 %collective-permute-done.6 = f32[384,384]{1,0:T(8,128)S(1)} collective-permute-done((f32[384,384]{1,0:T(8,128)S(1)}, f32[384,384]{1,0:T(8,128)S(1)}, u32[]{:S(2)}, u32[]{:S(2)}) %collective-permute-start.6) | collective-permute-done | bytes 589856 | tf_op jit(solution)/shard_map/p2/ppermute | solution.py:25
  33.5 0.9 bitcast_dynamic-update-slice_fusion.1.rest_0_
  34.3 4.0 %collective-permute-done.5.rest_6_.rest_2_ = f32[2,384,768]{2,1,0:T(8,128)S(1)} collective-permute-done((f32[2,384,768]{2,1,0:T(8,128)S(1)}, f32[2,384,768]{2,1,0:T(8,128)S(1)}, u32[]{:S(2)}, u32[]{:S(2)}) %collective-permute-start.5) | collective-permute-done | bytes 2359328 | tf_op jit(solution)/shard_map/p1z/ppermute | solution.py:25
  38.7 1.3 collective-permute-start.9
  42.4 26.4 %collective-permute-done.10.rest_3_ = f32[4,384,384]{2,1,0:T(8,128)} collective-permute-done((f32[4,384,384]{2,1,0:T(8,128)}, f32[4,384,384]{2,1,0:T(8,128)}, u32[]{:S(2)}, u32[]{:S(2)}) %collective-permute-start.10) | collective-permute-done | bytes 2359328 | tf_op jit(solution)/shard_map/p3/ppermute | solution.py:25
  68.8 1.6 collective-permute-done.8.rest_7_.rest_3_
  70.8 3.0 %collective-permute-start.13 = (f32[4,384,384]{2,1,0:T(8,128)}, f32[4,384,384]{2,1,0:T(8,128)}, u32[]{:S(2)}, u32[]{:S(2)}) collective-permute-start(f32[4,384,384]{2,1,0:T(8,128)} %bitcast_dynamic-update-slice_fusion.rest_2_), channel_id=1, source_target_pairs={{0,96},{1,33},{2,98},{3,35},{4,100},{5,37},{6,102},{7,39},{8,104},... | collective-permute-start | bytes 7077896 | tf_op jit(solution)/shard_map/p4/ppermute | solution.py:25
  73.8 0.7 collective-permute-start.12
  74.5 3.9 %collective-permute-done.14.rest_8_.rest_6_ = f32[2,384,768]{2,1,0:T(8,128)S(1)} collective-permute-done((f32[2,384,768]{2,1,0:T(8,128)}, f32[2,384,768]{2,1,0:T(8,128)S(1)}, u32[]{:S(2)}, u32[]{:S(2)}) %collective-permute-start.14) | collective-permute-done | bytes 2359328 | tf_op jit(solution)/shard_map/p4s/ppermute | solution.py:25
  78.4 1.4 copy-done.2
  79.8 1.4 copy-done.3
  81.2 15.7 %early_products.1.rest_14_ = f32[2,384,768]{2,1,0:T(8,128)} custom-call(s32[8]{0:T(128)} %concatenate.16.where_ref, s32[24]{0:T(128)} %bitcast.70, s32[3,32]{1,0:T(4,128)} %pad_add_fusion.table_ref, f32[4,384,384]{2,1,0:T(8,128)} %bitcast_dynamic-update-slice_fusion.1.rest_0_, f32[4,384,384]{2,1,0:T(8,128)} %collective-permute-done.9.rest_1_, ...), custom_call_target="tpu_custom_call" | custom-call | flops 8400000000 | bytes 21600000 | tf_op jit(solution)/shard_map/early_products/pallas_call | solution.py:184
  96.9 3.5 %collective-permute-done.13.rest_11_ = f32[4,384,384]{2,1,0:T(8,128)} collective-permute-done((f32[4,384,384]{2,1,0:T(8,128)}, f32[4,384,384]{2,1,0:T(8,128)}, u32[]{:S(2)}, u32[]{:S(2)}) %collective-permute-start.13) | collective-permute-done | bytes 2359328 | tf_op jit(solution)/shard_map/p4/ppermute | solution.py:25
  100.5 2.5 %collective-permute-done.12.rest_10_ = f32[4,384,384]{2,1,0:T(8,128)} collective-permute-done((f32[4,384,384]{2,1,0:T(8,128)}, f32[4,384,384]{2,1,0:T(8,128)}, u32[]{:S(2)}, u32[]{:S(2)}) %collective-permute-start.12) | collective-permute-done | bytes 2359328 | tf_op jit(solution)/shard_map/p4/ppermute | solution.py:25
  103.0 1.7 collective-permute-done.11.rest_12_.rest_4_
  104.7 1.3 collective-permute-start.17
  106.0 3.5 %collective-permute-done.16.rest_13_.rest_5_ = f32[2,384,768]{2,1,0:T(8,128)S(1)} collective-permute-done((f32[2,384,768]{2,1,0:T(8,128)}, f32[2,384,768]{2,1,0:T(8,128)S(1)}, u32[]{:S(2)}, u32[]{:S(2)}) %collective-permute-start.16) | collective-permute-done | bytes 2359328 | tf_op jit(solution)/shard_map/p5s/ppermute | solution.py:25
  109.4 1.4 copy-done.4
  110.9 15.0 %middle_products.1 = (f32[2,384,768]{2,1,0:T(8,128)}, bf16[768,768]{1,0:T(8,128)(2,1)}, bf16[768,768]{1,0:T(8,128)(2,1)}) custom-call(s32[8]{0:T(128)} %concatenate.16.where_ref, s32[24]{0:T(128)} %bitcast.71, s32[3,32]{1,0:T(4,128)} %pad_add_fusion.table_ref, f32[4,384,384]{2,1,0:T(8,128)} %bitcast_dynamic-update-slice_fusion.1.rest_0_, ...), custom_call_target="tpu_custom_call" | custom-call | flops 8400000000 | bytes 21600000 | tf_op jit(solution)/shard_map/middle_products/pallas_call | solution.py:219
  125.9 9.2 %collective-permute-done.18.rest_9_ = f32[4,384,384]{2,1,0:T(8,128)} collective-permute-done((f32[4,384,384]{2,1,0:T(8,128)}, f32[4,384,384]{2,1,0:T(8,128)}, u32[]{:S(2)}, u32[]{:S(2)}) %collective-permute-start.18) | collective-permute-done | bytes 2359328 | tf_op jit(solution)/shard_map/p5/ppermute | solution.py:25
  135.1 16.0 %last_products.1 = (f32[768,768]{1,0:T(8,128)}, f32[1,768]{1,0:T(1,128)}, f32[4,96,768]{2,1,0:T(8,128)}, f32[4,96,768]{2,1,0:T(8,128)}) custom-call(s32[8]{0:T(128)} %concatenate.16.where_ref, s32[24]{0:T(128)} %bitcast.72, s32[3,32]{1,0:T(4,128)} %pad_add_fusion.table_ref, f32[2,384,768]{2,1,0:T(8,128)} %bitcast.57, ...), custom_call_target="tpu_custom_call" | custom-call | flops 8400000000 | bytes 21600000 | tf_op jit(solution)/shard_map/last_products/pallas_call | solution.py:277
  151.7 2.5 %collective-permute-done.23 = f32[1,768]{1,0:T(1,128)S(1)} collective-permute-done((f32[1,768]{1,0:T(1,128)}, f32[1,768]{1,0:T(1,128)S(1)}, u32[]{:S(2)}, u32[]{:S(2)}) %collective-permute-start.23) | collective-permute-done | bytes 3104 | tf_op jit(solution)/shard_map/swap/ppermute | solution.py:25
  154.2 0.7 add.372
  154.9 3.2 %collective-permute-start.25 = (f32[1,768]{1,0:T(1,128)S(1)}, f32[1,768]{1,0:T(1,128)S(1)}, u32[]{:S(2)}, u32[]{:S(2)}) collective-permute-start(f32[1,768]{1,0:T(1,128)S(1)} %add.372), channel_id=1, source_target_pairs={{0,6},{1,7},{2,0},{3,1},{4,2},{5,3},{6,4},{7,5},{8,14},{9,15},{10,... | collective-permute-start | bytes 9224 | tf_op jit(solution)/shard_map/ppermute | solution.py:25
  158.1 1.6 collective-permute-done.24
  159.7 3.5 %collective-permute-done.26 = f32[1,768]{1,0:T(1,128)S(1)} collective-permute-done((f32[1,768]{1,0:T(1,128)S(1)}, f32[1,768]{1,0:T(1,128)S(1)}, u32[]{:S(2)}, u32[]{:S(2)}) %collective-permute-start.26) | collective-permute-done | bytes 3104 | tf_op jit(solution)/shard_map/ppermute | solution.py:25
  163.3 1.4 add.356
  165.2 2.9 %collective-permute-start.28 = (f32[1,768]{1,0:T(1,128)S(1)}, f32[1,768]{1,0:T(1,128)S(1)}, u32[]{:S(2)}, u32[]{:S(2)}) collective-permute-start(f32[1,768]{1,0:T(1,128)S(1)} %add_add_fusion), channel_id=1, source_target_pairs={{0,16},{1,17},{2,18},{3,19},{4,20},{5,21},{6,22},{7,23},{8,24},{9,... | collective-permute-start | bytes 9224 | tf_op jit(solution)/shard_map/ppermute | solution.py:25
  168.1 2.1 %collective-permute-start.29 = (f32[1,768]{1,0:T(1,128)S(1)}, f32[1,768]{1,0:T(1,128)S(1)}, u32[]{:S(2)}, u32[]{:S(2)}) collective-permute-start(f32[1,768]{1,0:T(1,128)S(1)} %add_add_fusion), channel_id=1, source_target_pairs={{0,8},{1,9},{2,10},{3,11},{4,12},{5,13},{6,14},{7,15},{8,16},{9,17... | collective-permute-start | bytes 9224 | tf_op jit(solution)/shard_map/ppermute | solution.py:25
  170.3 3.2 %collective-permute-start.21 = (f32[96,768]{1,0:T(8,128)S(1)}, f32[96,768]{1,0:T(8,128)S(1)}, u32[]{:S(2)}, u32[]{:S(2)}) collective-permute-start(f32[96,768]{1,0:T(8,128)S(1)} %get-tuple-element.76), channel_id=1, source_target_pairs={{0,6},{1,7},{2,0},{3,1},{4,2},{5,3},{6,4},{7,5},{8,14},{9,15},{10,... | collective-permute-start | bytes 884744 | tf_op jit(solution)/shard_map/ppermute | solution.py:25
  173.6 3.0 %collective-permute-start.30 = (f32[4,768]{1,0:T(4,128)S(1)}, f32[4,768]{1,0:T(4,128)S(1)}, u32[]{:S(2)}, u32[]{:S(2)}) collective-permute-start(f32[4,768]{1,0:T(4,128)S(1)} %get-tuple-element.82), channel_id=1, source_target_pairs={{0,96},{1,97},{2,98},{3,99},{4,100},{5,101},{6,102},{7,103},{8,104... | collective-permute-start | bytes 36872 | tf_op jit(solution)/shard_map/ppermute | solution.py:25
  176.5 1.4 collective-permute-done.30
  178.0 3.8 %collective-permute-done.31 = f32[4,768]{1,0:T(4,128)S(1)} collective-permute-done((f32[4,768]{1,0:T(4,128)S(1)}, f32[4,768]{1,0:T(4,128)S(1)}, u32[]{:S(2)}, u32[]{:S(2)}) %collective-permute-start.31) | collective-permute-done | bytes 12320 | tf_op jit(solution)/shard_map/ppermute | solution.py:25
  181.7 1.4 collective-permute-done.32
  183.2 1.7 gather_fusion
  185.5 0.8 fusion.3
  (64 shorter events, 5.7 us)
Async XLA Ops:
  0.6 6.9 %copy-start = (f32[1,768,768]{2,1,0:T(8,128)S(1)}, f32[1,768,768]{2,1,0:T(8,128)}, u32[]{:S(2)}) copy-start(f32[1,768,768]{2,1,0:T(8,128)} %param.11) | copy-start | bytes 7077892
  2.2 16.1 %collective-permute-start = (f32[384,384]{1,0:T(8,128)S(1)}, f32[384,384]{1,0:T(8,128)S(1)}, u32[]{:S(2)}, u32[]{:S(2)}) collective-permute-start(f32[384,384]{1,0:T(8,128)S(1)} %get-tuple-element.80), channel_id=1, source_target_pairs={{0,32},{1,97},{2,34},{3,99},{4,36},{5,101},{6,38},{7,103},{8,40},{... | collective-permute-start | bytes 1769480 | tf_op jit(solution)/shard_map/p1/ppermute | solution.py:25
  3.8 14.5 %collective-permute-start.2 = (f32[384,384]{1,0:T(8,128)S(1)}, f32[384,384]{1,0:T(8,128)S(1)}, u32[]{:S(2)}, u32[]{:S(2)}) collective-permute-start(f32[384,384]{1,0:T(8,128)S(1)} %get-tuple-element.80), channel_id=1, source_target_pairs={{0,96},{1,33},{2,98},{3,35},{4,100},{5,37},{6,102},{7,39},{8,104},... | collective-permute-start | bytes 1769480 | tf_op jit(solution)/shard_map/p1/ppermute | solution.py:25
  5.5 14.5 %collective-permute-start.1 = (f32[384,384]{1,0:T(8,128)S(1)}, f32[384,384]{1,0:T(8,128)S(1)}, u32[]{:S(2)}, u32[]{:S(2)}) collective-permute-start(f32[384,384]{1,0:T(8,128)S(1)} %get-tuple-element.79), channel_id=1, source_target_pairs={{0,8},{1,25},{2,10},{3,27},{4,12},{5,29},{6,14},{7,31},{8,16},{9,1... | collective-permute-start | bytes 1769480 | tf_op jit(solution)/shard_map/p1/ppermute | solution.py:25
  6.8 13.2 %collective-permute-start.3 = (f32[384,384]{1,0:T(8,128)S(1)}, f32[384,384]{1,0:T(8,128)S(1)}, u32[]{:S(2)}, u32[]{:S(2)}) collective-permute-start(f32[384,384]{1,0:T(8,128)S(1)} %get-tuple-element.79), channel_id=1, source_target_pairs={{0,24},{1,9},{2,26},{3,11},{4,28},{5,13},{6,30},{7,15},{8,0},{9,17... | collective-permute-start | bytes 1769480 | tf_op jit(solution)/shard_map/p1/ppermute | solution.py:25
  7.5 30.9 %collective-permute-start.5 = (f32[2,384,768]{2,1,0:T(8,128)S(1)}, f32[2,384,768]{2,1,0:T(8,128)S(1)}, u32[]{:S(2)}, u32[]{:S(2)}) collective-permute-start(f32[2,384,768]{2,1,0:T(8,128)S(1)} %bitcast.58), channel_id=1, source_target_pairs={{0,2},{1,7},{2,4},{3,1},{4,6},{5,3},{6,0},{7,5},{8,10},{9,15},{10,... | collective-permute-start | bytes 7077896 | tf_op jit(solution)/shard_map/p1z/ppermute | solution.py:25
  20.0 18.4 %collective-permute-start.4 = (f32[2,384,768]{2,1,0:T(8,128)S(1)}, f32[2,384,768]{2,1,0:T(8,128)}, u32[]{:S(2)}, u32[]{:S(2)}) collective-permute-start(f32[2,384,768]{2,1,0:T(8,128)S(1)} %bitcast.59), channel_id=1, source_target_pairs={{0,1},{1,0},{2,3},{3,2},{4,5},{5,4},{6,7},{7,6},{8,9},{9,8},{10,11... | collective-permute-start | bytes 7077896 | tf_op jit(solution)/shard_map/p2s/ppermute | solution.py:25
  20.0 9.9 %collective-permute-start.7 = (f32[384,384]{1,0:T(8,128)S(1)}, f32[384,384]{1,0:T(8,128)S(1)}, u32[]{:S(2)}, u32[]{:S(2)}) collective-permute-start(f32[384,384]{1,0:T(8,128)S(1)} %collective-permute-done.1), channel_id=1, source_target_pairs={{0,8},{1,25},{2,10},{3,27},{4,12},{5,29},{6,14},{7,31},{8,16},{9,1... | collective-permute-start | bytes 1769480 | tf_op jit(solution)/shard_map/p2/ppermute | solution.py:25
  22.4 11.1 %collective-permute-start.6 = (f32[384,384]{1,0:T(8,128)S(1)}, f32[384,384]{1,0:T(8,128)S(1)}, u32[]{:S(2)}, u32[]{:S(2)}) collective-permute-start(f32[384,384]{1,0:T(8,128)S(1)} %collective-permute-done), channel_id=1, source_target_pairs={{0,32},{1,97},{2,34},{3,99},{4,36},{5,101},{6,38},{7,103},{8,40},{... | collective-permute-start | bytes 1769480 | tf_op jit(solution)/shard_map/p2/ppermute | solution.py:25
  25.5 14.5 %copy-start.5 = (f32[1,96,768]{2,1,0:T(8,128)S(1)}, f32[1,96,768]{2,1,0:T(8,128)}, u32[]{:S(2)}) copy-start(f32[1,96,768]{2,1,0:T(8,128)} %param.12) | copy-start | bytes 884740
  25.5 16.9 %copy-start.6 = (s32[256]{0:T(256)S(1)}, s32[256]{0:T(256)}, u32[]{:S(2)}) copy-start(s32[256]{0:T(256)} %param.14) | copy-start | bytes 3076
  38.4 42.8 %copy-start.1 = (f32[2,384,768]{2,1,0:T(8,128)}, f32[2,384,768]{2,1,0:T(8,128)S(1)}, u32[]{:S(2)}) copy-start(f32[2,384,768]{2,1,0:T(8,128)S(1)} %collective-permute-done.5.rest_6_.rest_2_) | copy-start | bytes 7077892
  38.4 30.4 %collective-permute-start.10 = (f32[4,384,384]{2,1,0:T(8,128)}, f32[4,384,384]{2,1,0:T(8,128)}, u32[]{:S(2)}, u32[]{:S(2)}) collective-permute-start(f32[4,384,384]{2,1,0:T(8,128)} %bitcast_dynamic-update-slice_fusion.rest_2_), channel_id=1, source_target_pairs={{0,32},{1,97},{2,34},{3,99},{4,36},{5,101},{6,38},{7,103},{8,40},{... | collective-permute-start | bytes 7077896 | tf_op jit(solution)/shard_map/p3/ppermute | solution.py:25
  38.7 30.1 %collective-permute-start.9 = (f32[4,384,384]{2,1,0:T(8,128)}, f32[4,384,384]{2,1,0:T(8,128)}, u32[]{:S(2)}, u32[]{:S(2)}) collective-permute-start(f32[4,384,384]{2,1,0:T(8,128)} %bitcast_dynamic-update-slice_fusion.1.rest_0_), channel_id=1, source_target_pairs={{0,8},{1,25},{2,10},{3,27},{4,12},{5,29},{6,14},{7,31},{8,16},{9,1... | collective-permute-start | bytes 7077896 | tf_op jit(solution)/shard_map/p3/ppermute | solution.py:25
  40.0 30.4 %collective-permute-start.8 = (f32[2,384,768]{2,1,0:T(8,128)}, f32[2,384,768]{2,1,0:T(8,128)}, u32[]{:S(2)}, u32[]{:S(2)}) collective-permute-start(f32[2,384,768]{2,1,0:T(8,128)} %collective-permute-done.4.rest_5_.rest_1_), channel_id=1, source_target_pairs={{0,2},{1,7},{2,4},{3,1},{4,6},{5,3},{6,0},{7,5},{8,10},{9,15},{10,... | collective-permute-start | bytes 7077896 | tf_op jit(solution)/shard_map/p3z/ppermute | solution.py:25
  70.3 8.1 %collective-permute-start.14 = (f32[2,384,768]{2,1,0:T(8,128)}, f32[2,384,768]{2,1,0:T(8,128)S(1)}, u32[]{:S(2)}, u32[]{:S(2)}) collective-permute-start(f32[2,384,768]{2,1,0:T(8,128)} %collective-permute-done.8.rest_7_.rest_3_), channel_id=1, source_target_pairs={{0,1},{1,0},{2,3},{3,2},{4,5},{5,4},{6,7},{7,6},{8,9},{9,8},{10,11... | collective-permute-start | bytes 7077896 | tf_op jit(solution)/shard_map/p4s/ppermute | solution.py:25
  70.3 8.1 %collective-permute-start.15 = (f32[2,384,768]{2,1,0:T(8,128)S(1)}, f32[2,384,768]{2,1,0:T(8,128)S(1)}, u32[]{:S(2)}, u32[]{:S(2)}) collective-permute-start(f32[2,384,768]{2,1,0:T(8,128)S(1)} %collective-permute-done.5.rest_6_.rest_2_), channel_id=1, source_target_pairs={{0,1},{1,0},{2,3},{3,2},{4,5},{5,4},{6,7},{7,6},{8,9},{9,8},{10,11... | collective-permute-start | bytes 7077896 | tf_op jit(solution)/shard_map/p4s/ppermute | solution.py:25
  70.8 29.6 %collective-permute-start.13 = (f32[4,384,384]{2,1,0:T(8,128)}, f32[4,384,384]{2,1,0:T(8,128)}, u32[]{:S(2)}, u32[]{:S(2)}) collective-permute-start(f32[4,384,384]{2,1,0:T(8,128)} %bitcast_dynamic-update-slice_fusion.rest_2_), channel_id=1, source_target_pairs={{0,96},{1,33},{2,98},{3,35},{4,100},{5,37},{6,102},{7,39},{8,104},... | collective-permute-start | bytes 7077896 | tf_op jit(solution)/shard_map/p4/ppermute | solution.py:25
  73.8 29.2 %collective-permute-start.12 = (f32[4,384,384]{2,1,0:T(8,128)}, f32[4,384,384]{2,1,0:T(8,128)}, u32[]{:S(2)}, u32[]{:S(2)}) collective-permute-start(f32[4,384,384]{2,1,0:T(8,128)} %bitcast_dynamic-update-slice_fusion.1.rest_0_), channel_id=1, source_target_pairs={{0,24},{1,9},{2,26},{3,11},{4,28},{5,13},{6,30},{7,15},{8,0},{9,17... | collective-permute-start | bytes 7077896 | tf_op jit(solution)/shard_map/p4/ppermute | solution.py:25
  74.5 30.2 %collective-permute-start.11 = (f32[2,384,768]{2,1,0:T(8,128)S(1)}, f32[2,384,768]{2,1,0:T(8,128)}, u32[]{:S(2)}, u32[]{:S(2)}) collective-permute-start(f32[2,384,768]{2,1,0:T(8,128)S(1)} %collective-permute-done.5.rest_6_.rest_2_), channel_id=1, source_target_pairs={{0,2},{1,7},{2,4},{3,1},{4,6},{5,3},{6,0},{7,5},{8,10},{9,15},{10,... | collective-permute-start | bytes 7077896 | tf_op jit(solution)/shard_map/p4z/ppermute | solution.py:25
  78.4 1.4 copy-start.2
  79.8 1.4 copy-start.3
  104.7 4.7 %collective-permute-start.16 = (f32[2,384,768]{2,1,0:T(8,128)}, f32[2,384,768]{2,1,0:T(8,128)S(1)}, u32[]{:S(2)}, u32[]{:S(2)}) collective-permute-start(f32[2,384,768]{2,1,0:T(8,128)} %collective-permute-done.11.rest_12_.rest_4_), channel_id=1, source_target_pairs={{0,1},{1,0},{2,3},{3,2},{4,5},{5,4},{6,7},{7,6},{8,9},{9,8},{10,11... | collective-permute-start | bytes 7077896 | tf_op jit(solution)/shard_map/p5s/ppermute | solution.py:25
  104.7 30.4 %collective-permute-start.18 = (f32[4,384,384]{2,1,0:T(8,128)}, f32[4,384,384]{2,1,0:T(8,128)}, u32[]{:S(2)}, u32[]{:S(2)}) collective-permute-start(f32[4,384,384]{2,1,0:T(8,128)} %collective-permute-done.10.rest_3_), channel_id=1, source_target_pairs={{0,32},{1,97},{2,34},{3,99},{4,36},{5,101},{6,38},{7,103},{8,40},{... | collective-permute-start | bytes 7077896 | tf_op jit(solution)/shard_map/p5/ppermute | solution.py:25
  104.7 30.4 %collective-permute-start.17 = (f32[4,384,384]{2,1,0:T(8,128)}, f32[4,384,384]{2,1,0:T(8,128)}, u32[]{:S(2)}, u32[]{:S(2)}) collective-permute-start(f32[4,384,384]{2,1,0:T(8,128)} %collective-permute-done.9.rest_1_), channel_id=1, source_target_pairs={{0,8},{1,25},{2,10},{3,27},{4,12},{5,29},{6,14},{7,31},{8,16},{9,1... | collective-permute-start | bytes 7077896 | tf_op jit(solution)/shard_map/p5/ppermute | solution.py:25
  109.4 1.4 copy-start.4
  151.1 12.2 %collective-permute-start.19 = (f32[4,96,768]{2,1,0:T(8,128)}, f32[4,96,768]{2,1,0:T(8,128)S(1)}, u32[]{:S(2)}, u32[]{:S(2)}) collective-permute-start(f32[4,96,768]{2,1,0:T(8,128)} %get-tuple-element.66), channel_id=1, source_target_pairs={{0,1},{1,0},{2,3},{3,2},{4,5},{5,4},{6,7},{7,6},{8,9},{9,8},{10,11... | collective-permute-start | bytes 3538952 | tf_op jit(solution)/shard_map/swap/ppermute | solution.py:25
  151.2 3.0 %collective-permute-start.23 = (f32[1,768]{1,0:T(1,128)}, f32[1,768]{1,0:T(1,128)S(1)}, u32[]{:S(2)}, u32[]{:S(2)}) collective-permute-start(f32[1,768]{1,0:T(1,128)} %get-tuple-element.67), channel_id=1, source_target_pairs={{0,1},{1,0},{2,3},{3,2},{4,5},{5,4},{6,7},{7,6},{8,9},{9,8},{10,11... | collective-permute-start | bytes 9224 | tf_op jit(solution)/shard_map/swap/ppermute | solution.py:25
  154.9 4.8 %collective-permute-start.24 = (f32[1,768]{1,0:T(1,128)S(1)}, f32[1,768]{1,0:T(1,128)S(1)}, u32[]{:S(2)}, u32[]{:S(2)}) collective-permute-start(f32[1,768]{1,0:T(1,128)S(1)} %add.372), channel_id=1, source_target_pairs={{0,2},{1,3},{2,4},{3,5},{4,6},{5,7},{6,0},{7,1},{8,10},{9,11},{10,... | collective-permute-start | bytes 9224 | tf_op jit(solution)/shard_map/ppermute | solution.py:25
  154.9 4.8 %collective-permute-start.25 = (f32[1,768]{1,0:T(1,128)S(1)}, f32[1,768]{1,0:T(1,128)S(1)}, u32[]{:S(2)}, u32[]{:S(2)}) collective-permute-start(f32[1,768]{1,0:T(1,128)S(1)} %add.372), channel_id=1, source_target_pairs={{0,6},{1,7},{2,0},{3,1},{4,2},{5,3},{6,4},{7,5},{8,14},{9,15},{10,... | collective-permute-start | bytes 9224 | tf_op jit(solution)/shard_map/ppermute | solution.py:25
  158.1 5.1 %collective-permute-start.26 = (f32[1,768]{1,0:T(1,128)S(1)}, f32[1,768]{1,0:T(1,128)S(1)}, u32[]{:S(2)}, u32[]{:S(2)}) collective-permute-start(f32[1,768]{1,0:T(1,128)S(1)} %add.372), channel_id=1, source_target_pairs={{0,4},{1,5},{2,6},{3,7},{4,0},{5,1},{6,2},{7,3},{8,12},{9,13},{10,... | collective-permute-start | bytes 9224 | tf_op jit(solution)/shard_map/ppermute | solution.py:25
  164.7 20.2 %copy-start.7 = (f32[256]{0:T(256)S(1)}, f32[256]{0:T(256)}, u32[]{:S(2)}) copy-start(f32[256]{0:T(256)} %param.15) | copy-start | bytes 3076
  164.7 8.9 %collective-permute-start.27 = (f32[1,768]{1,0:T(1,128)S(1)}, f32[1,768]{1,0:T(1,128)S(1)}, u32[]{:S(2)}, u32[]{:S(2)}) collective-permute-start(f32[1,768]{1,0:T(1,128)S(1)} %add_add_fusion), channel_id=1, source_target_pairs={{0,24},{1,25},{2,26},{3,27},{4,28},{5,29},{6,30},{7,31},{8,0},{9,1... | collective-permute-start | bytes 9224 | tf_op jit(solution)/shard_map/ppermute | solution.py:25
  165.2 8.3 %collective-permute-start.28 = (f32[1,768]{1,0:T(1,128)S(1)}, f32[1,768]{1,0:T(1,128)S(1)}, u32[]{:S(2)}, u32[]{:S(2)}) collective-permute-start(f32[1,768]{1,0:T(1,128)S(1)} %add_add_fusion), channel_id=1, source_target_pairs={{0,16},{1,17},{2,18},{3,19},{4,20},{5,21},{6,22},{7,23},{8,24},{9,... | collective-permute-start | bytes 9224 | tf_op jit(solution)/shard_map/ppermute | solution.py:25
  168.1 5.5 %collective-permute-start.29 = (f32[1,768]{1,0:T(1,128)S(1)}, f32[1,768]{1,0:T(1,128)S(1)}, u32[]{:S(2)}, u32[]{:S(2)}) collective-permute-start(f32[1,768]{1,0:T(1,128)S(1)} %add_add_fusion), channel_id=1, source_target_pairs={{0,8},{1,9},{2,10},{3,11},{4,12},{5,13},{6,14},{7,15},{8,16},{9,17... | collective-permute-start | bytes 9224 | tf_op jit(solution)/shard_map/ppermute | solution.py:25
  170.2 15.2 %collective-permute-start.20 = (f32[96,768]{1,0:T(8,128)S(1)}, f32[96,768]{1,0:T(8,128)S(1)}, u32[]{:S(2)}, u32[]{:S(2)}) collective-permute-start(f32[96,768]{1,0:T(8,128)S(1)} %get-tuple-element.74), channel_id=1, source_target_pairs={{0,2},{1,3},{2,4},{3,5},{4,6},{5,7},{6,0},{7,1},{8,10},{9,11},{10,... | collective-permute-start | bytes 884744 | tf_op jit(solution)/shard_map/ppermute | solution.py:25
  170.3 15.2 %collective-permute-start.21 = (f32[96,768]{1,0:T(8,128)S(1)}, f32[96,768]{1,0:T(8,128)S(1)}, u32[]{:S(2)}, u32[]{:S(2)}) collective-permute-start(f32[96,768]{1,0:T(8,128)S(1)} %get-tuple-element.76), channel_id=1, source_target_pairs={{0,6},{1,7},{2,0},{3,1},{4,2},{5,3},{6,4},{7,5},{8,14},{9,15},{10,... | collective-permute-start | bytes 884744 | tf_op jit(solution)/shard_map/ppermute | solution.py:25
  173.5 11.9 %collective-permute-start.22 = (f32[96,768]{1,0:T(8,128)S(1)}, f32[96,768]{1,0:T(8,128)S(1)}, u32[]{:S(2)}, u32[]{:S(2)}) collective-permute-start(f32[96,768]{1,0:T(8,128)S(1)} %get-tuple-element.75), channel_id=1, source_target_pairs={{0,4},{1,5},{2,6},{3,7},{4,0},{5,1},{6,2},{7,3},{8,12},{9,13},{10,... | collective-permute-start | bytes 884744 | tf_op jit(solution)/shard_map/ppermute | solution.py:25
  173.6 4.4 %collective-permute-start.30 = (f32[4,768]{1,0:T(4,128)S(1)}, f32[4,768]{1,0:T(4,128)S(1)}, u32[]{:S(2)}, u32[]{:S(2)}) collective-permute-start(f32[4,768]{1,0:T(4,128)S(1)} %get-tuple-element.82), channel_id=1, source_target_pairs={{0,96},{1,97},{2,98},{3,99},{4,100},{5,101},{6,102},{7,103},{8,104... | collective-permute-start | bytes 36872 | tf_op jit(solution)/shard_map/ppermute | solution.py:25
  176.5 5.2 %collective-permute-start.31 = (f32[4,768]{1,0:T(4,128)S(1)}, f32[4,768]{1,0:T(4,128)S(1)}, u32[]{:S(2)}, u32[]{:S(2)}) collective-permute-start(f32[4,768]{1,0:T(4,128)S(1)} %get-tuple-element.82), channel_id=1, source_target_pairs={{0,64},{1,65},{2,66},{3,67},{4,68},{5,69},{6,70},{7,71},{8,72},{9,... | collective-permute-start | bytes 36872 | tf_op jit(solution)/shard_map/ppermute | solution.py:25
  177.9 5.2 %collective-permute-start.32 = (f32[4,768]{1,0:T(4,128)S(1)}, f32[4,768]{1,0:T(4,128)S(1)}, u32[]{:S(2)}, u32[]{:S(2)}) collective-permute-start(f32[4,768]{1,0:T(4,128)S(1)} %get-tuple-element.82), channel_id=1, source_target_pairs={{0,32},{1,33},{2,34},{3,35},{4,36},{5,37},{6,38},{7,39},{8,40},{9,... | collective-permute-start | bytes 36872 | tf_op jit(solution)/shard_map/ppermute | solution.py:25

commit v5 on v4

--- a/solution.py
+++ b/solution.py
@@ -347,9 +347,11 @@
     final = {name: pieces[name] for name in BLOCKS + ("a3", "b3")}
     sep, part_var, mine, other = last_products(where, mask, table, final, sums, own_high, own_low, diag_here)
 
-    part = part_var + swap(part_var)
-    half_sum = mine + swap(other)
-    part = part + send(part, dz=1) + send(part, dz=-1) + send(part, dz=2)
+    arrived = swap(other)
+    part = after(part_var + swap(part_var), arrived)
+    half_sum = mine + arrived
+    along_z = send(part, dz=1), send(part, dz=-1), send(part, dz=2)
+    part = part + along_z[0] + along_z[1] + along_z[2]
     toward = lambda dz: lax.dynamic_index_in_dim(half_sum, (z + dz) % 4, 0, False)
     block_here = inverse + (toward(0) + send(toward(1), dz=1) + send(toward(-1), dz=-1) + send(toward(2), dz=2))
     part = after(part, half_sum)

time: 187 us -> 185 us (0.989)
  transfers between devices with their start and end apart: 33 -> 33, of which waited for: 19 -> 19; matrix products, arithmetic and copies ran while one was open for 5% -> 6% of each run, Pallas kernels for 16% -> 17%
where the time goes in v5:
time: 185 us
  waiting for transfers between devices  86.7 us (47%)
  Pallas kernels  46.7 us (25%)
  starting transfers between devices  32.7 us (18%)
  local copies, waits for them, and re-layouts  10.6 us (6%)
  other arithmetic  7.37 us (4%)
    ppermute x33, waiting for transfers between devices, send(): return lax.ppermute(value, AXES, pairs)  86.7 us
    ppermute x33, starting transfers between devices, send(): return lax.ppermute(value, AXES, pairs)  32.7 us
    pallas_call x1, Pallas kernels, last_products(): pl.pallas_call(body, out_shape=(shape(768, 768), shape(1, 768), shape(4,...  16 us
    pallas_call x1, Pallas kernels, early_products(): pl.pallas_call(body, out_shape=shape(2, 384, 768), in_specs=[SMEM, SMEM,...  15.7 us
    pallas_call x1, Pallas kernels, middle_products(): pl.pallas_call(body, out_shape=(shape(2, 384, 768), half, half), in_specs...  15 us
    unnamed x16, local copies, waits for them, and re-layouts  4.24 us
  transfers between devices with their start and end apart: 33, of which 19 were waited for; matrix products, arithmetic and copies ran while one was open for 6% of the time, Pallas kernels for 17%

profile of v5, /device:TPU:16, one launch (start us, length us, event | category | flops | bytes accessed | tf_op | source)
XLA Modules:
  0.0 184.8 jit_solution(4107575773314150363)
XLA Ops:
  0.6 1.5 slice_bitcast_fusion
  2.2 1.6 collective-permute-start
  3.8 1.7 collective-permute-start.2
  5.5 1.3 collective-permute-start.1
  6.8 0.7 collective-permute-start.3
  7.5 1.9 %collective-permute-start.5 = (f32[2,384,768]{2,1,0:T(8,128)S(1)}, f32[2,384,768]{2,1,0:T(8,128)S(1)}, u32[]{:S(2)}, u32[]{:S(2)}) collective-permute-start(f32[2,384,768]{2,1,0:T(8,128)S(1)} %bitcast.58), channel_id=1, source_target_pairs={{0,2},{1,7},{2,4},{3,1},{4,6},{5,3},{6,0},{7,5},{8,10},{9,15},{10,... | collective-permute-start | bytes 7077896 | tf_op jit(solution)/shard_map/p1z/ppermute | solution.py:25
  9.4 8.8 %collective-permute-done = f32[384,384]{1,0:T(8,128)S(1)} collective-permute-done((f32[384,384]{1,0:T(8,128)S(1)}, f32[384,384]{1,0:T(8,128)S(1)}, u32[]{:S(2)}, u32[]{:S(2)}) %collective-permute-start) | collective-permute-done | bytes 589856 | tf_op jit(solution)/shard_map/p1/ppermute | solution.py:25
  18.3 1.7 collective-permute-done.1
  20.0 2.3 %collective-permute-start.7 = (f32[384,384]{1,0:T(8,128)S(1)}, f32[384,384]{1,0:T(8,128)S(1)}, u32[]{:S(2)}, u32[]{:S(2)}) collective-permute-start(f32[384,384]{1,0:T(8,128)S(1)} %collective-permute-done.1), channel_id=1, source_target_pairs={{0,8},{1,25},{2,10},{3,27},{4,12},{5,29},{6,14},{7,31},{8,16},{9,1... | collective-permute-start | bytes 1769480 | tf_op jit(solution)/shard_map/p2/ppermute | solution.py:25
  22.9 2.6 %maximum_maximum_fusion.1 = (f32[4,384,384]{2,1,0:T(8,128)}, f32[4,384,384]{2,1,0:T(8,128)}) fusion(f32[1,384,384]{2,1,0:T(8,128)S(1)} %bitcast.63, f32[1,384,384]{2,1,0:T(8,128)S(1)} %bitcast.62, f32[1,384,384]{2,1,0:T(8,128)S(1)} %get-tuple-element.79, f32[4]{0:T(128)S(1)} %pad.19.clone, f32[1,384,384]{2,1,0:T(8,128)S(1)} %bitcast.61, ...), kind=kLoop, calls=%fused_computation.2 | loop fusion | flops 3538944 | bytes 8257552 | tf_op jit(solution)/shard_map/concatenate | solution.py:328
  25.5 4.4 %collective-permute-done.7 = f32[384,384]{1,0:T(8,128)S(1)} collective-permute-done((f32[384,384]{1,0:T(8,128)S(1)}, f32[384,384]{1,0:T(8,128)S(1)}, u32[]{:S(2)}, u32[]{:S(2)}) %collective-permute-start.7) | collective-permute-done | bytes 589856 | tf_op jit(solution)/shard_map/p2/ppermute | solution.py:25
  29.9 0.9 bitcast_dynamic-update-slice_fusion.rest_2_
  30.7 2.8 %collective-permute-done.6 = f32[384,384]{1,0:T(8,128)S(1)} collective-permute-done((f32[384,384]{1,0:T(8,128)S(1)}, f32[384,384]{1,0:T(8,128)S(1)}, u32[]{:S(2)}, u32[]{:S(2)}) %collective-permute-start.6) | collective-permute-done | bytes 589856 | tf_op jit(solution)/shard_map/p2/ppermute | solution.py:25
  33.5 0.9 bitcast_dynamic-update-slice_fusion.1.rest_0_
  34.3 4.0 %collective-permute-done.5.rest_6_.rest_2_ = f32[2,384,768]{2,1,0:T(8,128)S(1)} collective-permute-done((f32[2,384,768]{2,1,0:T(8,128)S(1)}, f32[2,384,768]{2,1,0:T(8,128)S(1)}, u32[]{:S(2)}, u32[]{:S(2)}) %collective-permute-start.5) | collective-permute-done | bytes 2359328 | tf_op jit(solution)/shard_map/p1z/ppermute | solution.py:25
  38.7 1.3 collective-permute-start.9
  41.8 0.6 pad_add_fusion.table_ref
  42.4 26.4 %collective-permute-done.10.rest_3_ = f32[4,384,384]{2,1,0:T(8,128)} collective-permute-done((f32[4,384,384]{2,1,0:T(8,128)}, f32[4,384,384]{2,1,0:T(8,128)}, u32[]{:S(2)}, u32[]{:S(2)}) %collective-permute-start.10) | collective-permute-done | bytes 2359328 | tf_op jit(solution)/shard_map/p3/ppermute | solution.py:25
  68.8 1.6 collective-permute-done.8.rest_7_.rest_3_
  70.8 3.0 %collective-permute-start.13 = (f32[4,384,384]{2,1,0:T(8,128)}, f32[4,384,384]{2,1,0:T(8,128)}, u32[]{:S(2)}, u32[]{:S(2)}) collective-permute-start(f32[4,384,384]{2,1,0:T(8,128)} %bitcast_dynamic-update-slice_fusion.rest_2_), channel_id=1, source_target_pairs={{0,96},{1,33},{2,98},{3,35},{4,100},{5,37},{6,102},{7,39},{8,104},... | collective-permute-start | bytes 7077896 | tf_op jit(solution)/shard_map/p4/ppermute | solution.py:25
  73.8 0.7 collective-permute-start.12
  74.5 3.9 %collective-permute-done.14.rest_8_.rest_6_ = f32[2,384,768]{2,1,0:T(8,128)S(1)} collective-permute-done((f32[2,384,768]{2,1,0:T(8,128)}, f32[2,384,768]{2,1,0:T(8,128)S(1)}, u32[]{:S(2)}, u32[]{:S(2)}) %collective-permute-start.14) | collective-permute-done | bytes 2359328 | tf_op jit(solution)/shard_map/p4s/ppermute | solution.py:25
  78.4 1.4 copy-done.2
  79.8 1.4 copy-done.3
  81.2 15.7 %early_products.1.rest_14_ = f32[2,384,768]{2,1,0:T(8,128)} custom-call(s32[8]{0:T(128)} %concatenate.16.where_ref, s32[24]{0:T(128)} %bitcast.70, s32[3,32]{1,0:T(4,128)} %pad_add_fusion.table_ref, f32[4,384,384]{2,1,0:T(8,128)} %bitcast_dynamic-update-slice_fusion.1.rest_0_, f32[4,384,384]{2,1,0:T(8,128)} %collective-permute-done.9.rest_1_, ...), custom_call_target="tpu_custom_call" | custom-call | flops 8400000000 | bytes 21600000 | tf_op jit(solution)/shard_map/early_products/pallas_call | solution.py:184
  96.9 3.5 %collective-permute-done.13.rest_11_ = f32[4,384,384]{2,1,0:T(8,128)} collective-permute-done((f32[4,384,384]{2,1,0:T(8,128)}, f32[4,384,384]{2,1,0:T(8,128)}, u32[]{:S(2)}, u32[]{:S(2)}) %collective-permute-start.13) | collective-permute-done | bytes 2359328 | tf_op jit(solution)/shard_map/p4/ppermute | solution.py:25
  100.5 2.5 %collective-permute-done.12.rest_10_ = f32[4,384,384]{2,1,0:T(8,128)} collective-permute-done((f32[4,384,384]{2,1,0:T(8,128)}, f32[4,384,384]{2,1,0:T(8,128)}, u32[]{:S(2)}, u32[]{:S(2)}) %collective-permute-start.12) | collective-permute-done | bytes 2359328 | tf_op jit(solution)/shard_map/p4/ppermute | solution.py:25
  103.0 1.7 collective-permute-done.11.rest_12_.rest_4_
  104.7 1.3 collective-permute-start.17
  106.0 3.5 %collective-permute-done.16.rest_13_.rest_5_ = f32[2,384,768]{2,1,0:T(8,128)S(1)} collective-permute-done((f32[2,384,768]{2,1,0:T(8,128)}, f32[2,384,768]{2,1,0:T(8,128)S(1)}, u32[]{:S(2)}, u32[]{:S(2)}) %collective-permute-start.16) | collective-permute-done | bytes 2359328 | tf_op jit(solution)/shard_map/p5s/ppermute | solution.py:25
  109.4 1.4 copy-done.4
  110.9 15.0 %middle_products.1 = (f32[2,384,768]{2,1,0:T(8,128)}, bf16[768,768]{1,0:T(8,128)(2,1)}, bf16[768,768]{1,0:T(8,128)(2,1)}) custom-call(s32[8]{0:T(128)} %concatenate.16.where_ref, s32[24]{0:T(128)} %bitcast.71, s32[3,32]{1,0:T(4,128)} %pad_add_fusion.table_ref, f32[4,384,384]{2,1,0:T(8,128)} %bitcast_dynamic-update-slice_fusion.1.rest_0_, ...), custom_call_target="tpu_custom_call" | custom-call | flops 8400000000 | bytes 21600000 | tf_op jit(solution)/shard_map/middle_products/pallas_call | solution.py:219
  125.9 9.2 %collective-permute-done.18.rest_9_ = f32[4,384,384]{2,1,0:T(8,128)} collective-permute-done((f32[4,384,384]{2,1,0:T(8,128)}, f32[4,384,384]{2,1,0:T(8,128)}, u32[]{:S(2)}, u32[]{:S(2)}) %collective-permute-start.18) | collective-permute-done | bytes 2359328 | tf_op jit(solution)/shard_map/p5/ppermute | solution.py:25
  135.1 16.0 %last_products.1 = (f32[768,768]{1,0:T(8,128)}, f32[1,768]{1,0:T(1,128)}, f32[4,96,768]{2,1,0:T(8,128)}, f32[4,96,768]{2,1,0:T(8,128)}) custom-call(s32[8]{0:T(128)} %concatenate.16.where_ref, s32[24]{0:T(128)} %bitcast.72, s32[3,32]{1,0:T(4,128)} %pad_add_fusion.table_ref, f32[2,384,768]{2,1,0:T(8,128)} %bitcast.57, ...), custom_call_target="tpu_custom_call" | custom-call | flops 8400000000 | bytes 21600000 | tf_op jit(solution)/shard_map/last_products/pallas_call | solution.py:277
  151.7 2.5 %collective-permute-done.23 = f32[1,768]{1,0:T(1,128)S(1)} collective-permute-done((f32[1,768]{1,0:T(1,128)}, f32[1,768]{1,0:T(1,128)S(1)}, u32[]{:S(2)}, u32[]{:S(2)}) %collective-permute-start.23) | collective-permute-done | bytes 3104 | tf_op jit(solution)/shard_map/swap/ppermute | solution.py:25
  154.2 0.7 add.372
  154.9 3.2 %collective-permute-start.25 = (f32[1,768]{1,0:T(1,128)S(1)}, f32[1,768]{1,0:T(1,128)S(1)}, u32[]{:S(2)}, u32[]{:S(2)}) collective-permute-start(f32[1,768]{1,0:T(1,128)S(1)} %add.372), channel_id=1, source_target_pairs={{0,6},{1,7},{2,0},{3,1},{4,2},{5,3},{6,4},{7,5},{8,14},{9,15},{10,... | collective-permute-start | bytes 9224 | tf_op jit(solution)/shard_map/ppermute | solution.py:25
  158.1 1.4 add.356
  159.7 3.5 %collective-permute-done.26 = f32[1,768]{1,0:T(1,128)S(1)} collective-permute-done((f32[1,768]{1,0:T(1,128)S(1)}, f32[1,768]{1,0:T(1,128)S(1)}, u32[]{:S(2)}, u32[]{:S(2)}) %collective-permute-start.26) | collective-permute-done | bytes 3104 | tf_op jit(solution)/shard_map/ppermute | solution.py:25
  163.8 2.9 %collective-permute-start.28 = (f32[1,768]{1,0:T(1,128)S(1)}, f32[1,768]{1,0:T(1,128)S(1)}, u32[]{:S(2)}, u32[]{:S(2)}) collective-permute-start(f32[1,768]{1,0:T(1,128)S(1)} %add_add_fusion), channel_id=1, source_target_pairs={{0,16},{1,17},{2,18},{3,19},{4,20},{5,21},{6,22},{7,23},{8,24},{9,... | collective-permute-start | bytes 9224 | tf_op jit(solution)/shard_map/ppermute | solution.py:25
  166.7 2.1 %collective-permute-start.29 = (f32[1,768]{1,0:T(1,128)S(1)}, f32[1,768]{1,0:T(1,128)S(1)}, u32[]{:S(2)}, u32[]{:S(2)}) collective-permute-start(f32[1,768]{1,0:T(1,128)S(1)} %add_add_fusion), channel_id=1, source_target_pairs={{0,8},{1,9},{2,10},{3,11},{4,12},{5,13},{6,14},{7,15},{8,16},{9,17... | collective-permute-start | bytes 9224 | tf_op jit(solution)/shard_map/ppermute | solution.py:25
  168.9 3.2 %collective-permute-start.21 = (f32[96,768]{1,0:T(8,128)S(1)}, f32[96,768]{1,0:T(8,128)S(1)}, u32[]{:S(2)}, u32[]{:S(2)}) collective-permute-start(f32[96,768]{1,0:T(8,128)S(1)} %get-tuple-element.78), channel_id=1, source_target_pairs={{0,6},{1,7},{2,0},{3,1},{4,2},{5,3},{6,4},{7,5},{8,14},{9,15},{10,... | collective-permute-start | bytes 884744 | tf_op jit(solution)/shard_map/ppermute | solution.py:25
  172.2 3.0 %collective-permute-start.30 = (f32[4,768]{1,0:T(4,128)S(1)}, f32[4,768]{1,0:T(4,128)S(1)}, u32[]{:S(2)}, u32[]{:S(2)}) collective-permute-start(f32[4,768]{1,0:T(4,128)S(1)} %get-tuple-element.84), channel_id=1, source_target_pairs={{0,96},{1,97},{2,98},{3,99},{4,100},{5,101},{6,102},{7,103},{8,104... | collective-permute-start | bytes 36872 | tf_op jit(solution)/shard_map/ppermute | solution.py:25
  175.1 1.4 collective-permute-done.30
  176.5 3.8 %collective-permute-done.31 = f32[4,768]{1,0:T(4,128)S(1)} collective-permute-done((f32[4,768]{1,0:T(4,128)S(1)}, f32[4,768]{1,0:T(4,128)S(1)}, u32[]{:S(2)}, u32[]{:S(2)}) %collective-permute-start.31) | collective-permute-done | bytes 12320 | tf_op jit(solution)/shard_map/ppermute | solution.py:25
  180.3 1.4 collective-permute-done.32
  181.7 1.7 gather_fusion
  184.0 0.8 fusion.3
  (64 shorter events, 5.3 us)
Async XLA Ops:
  0.6 6.9 %copy-start = (f32[1,768,768]{2,1,0:T(8,128)S(1)}, f32[1,768,768]{2,1,0:T(8,128)}, u32[]{:S(2)}) copy-start(f32[1,768,768]{2,1,0:T(8,128)} %param.11) | copy-start | bytes 7077892
  2.2 16.1 %collective-permute-start = (f32[384,384]{1,0:T(8,128)S(1)}, f32[384,384]{1,0:T(8,128)S(1)}, u32[]{:S(2)}, u32[]{:S(2)}) collective-permute-start(f32[384,384]{1,0:T(8,128)S(1)} %get-tuple-element.82), channel_id=1, source_target_pairs={{0,32},{1,97},{2,34},{3,99},{4,36},{5,101},{6,38},{7,103},{8,40},{... | collective-permute-start | bytes 1769480 | tf_op jit(solution)/shard_map/p1/ppermute | solution.py:25
  3.8 14.5 %collective-permute-start.2 = (f32[384,384]{1,0:T(8,128)S(1)}, f32[384,384]{1,0:T(8,128)S(1)}, u32[]{:S(2)}, u32[]{:S(2)}) collective-permute-start(f32[384,384]{1,0:T(8,128)S(1)} %get-tuple-element.82), channel_id=1, source_target_pairs={{0,96},{1,33},{2,98},{3,35},{4,100},{5,37},{6,102},{7,39},{8,104},... | collective-permute-start | bytes 1769480 | tf_op jit(solution)/shard_map/p1/ppermute | solution.py:25
  5.5 14.5 %collective-permute-start.1 = (f32[384,384]{1,0:T(8,128)S(1)}, f32[384,384]{1,0:T(8,128)S(1)}, u32[]{:S(2)}, u32[]{:S(2)}) collective-permute-start(f32[384,384]{1,0:T(8,128)S(1)} %get-tuple-element.81), channel_id=1, source_target_pairs={{0,8},{1,25},{2,10},{3,27},{4,12},{5,29},{6,14},{7,31},{8,16},{9,1... | collective-permute-start | bytes 1769480 | tf_op jit(solution)/shard_map/p1/ppermute | solution.py:25
  6.8 13.2 %collective-permute-start.3 = (f32[384,384]{1,0:T(8,128)S(1)}, f32[384,384]{1,0:T(8,128)S(1)}, u32[]{:S(2)}, u32[]{:S(2)}) collective-permute-start(f32[384,384]{1,0:T(8,128)S(1)} %get-tuple-element.81), channel_id=1, source_target_pairs={{0,24},{1,9},{2,26},{3,11},{4,28},{5,13},{6,30},{7,15},{8,0},{9,17... | collective-permute-start | bytes 1769480 | tf_op jit(solution)/shard_map/p1/ppermute | solution.py:25
  7.5 30.9 %collective-permute-start.5 = (f32[2,384,768]{2,1,0:T(8,128)S(1)}, f32[2,384,768]{2,1,0:T(8,128)S(1)}, u32[]{:S(2)}, u32[]{:S(2)}) collective-permute-start(f32[2,384,768]{2,1,0:T(8,128)S(1)} %bitcast.58), channel_id=1, source_target_pairs={{0,2},{1,7},{2,4},{3,1},{4,6},{5,3},{6,0},{7,5},{8,10},{9,15},{10,... | collective-permute-start | bytes 7077896 | tf_op jit(solution)/shard_map/p1z/ppermute | solution.py:25
  20.0 18.4 %collective-permute-start.4 = (f32[2,384,768]{2,1,0:T(8,128)S(1)}, f32[2,384,768]{2,1,0:T(8,128)}, u32[]{:S(2)}, u32[]{:S(2)}) collective-permute-start(f32[2,384,768]{2,1,0:T(8,128)S(1)} %bitcast.59), channel_id=1, source_target_pairs={{0,1},{1,0},{2,3},{3,2},{4,5},{5,4},{6,7},{7,6},{8,9},{9,8},{10,11... | collective-permute-start | bytes 7077896 | tf_op jit(solution)/shard_map/p2s/ppermute | solution.py:25
  20.0 9.9 %collective-permute-start.7 = (f32[384,384]{1,0:T(8,128)S(1)}, f32[384,384]{1,0:T(8,128)S(1)}, u32[]{:S(2)}, u32[]{:S(2)}) collective-permute-start(f32[384,384]{1,0:T(8,128)S(1)} %collective-permute-done.1), channel_id=1, source_target_pairs={{0,8},{1,25},{2,10},{3,27},{4,12},{5,29},{6,14},{7,31},{8,16},{9,1... | collective-permute-start | bytes 1769480 | tf_op jit(solution)/shard_map/p2/ppermute | solution.py:25
  22.4 11.1 %collective-permute-start.6 = (f32[384,384]{1,0:T(8,128)S(1)}, f32[384,384]{1,0:T(8,128)S(1)}, u32[]{:S(2)}, u32[]{:S(2)}) collective-permute-start(f32[384,384]{1,0:T(8,128)S(1)} %collective-permute-done), channel_id=1, source_target_pairs={{0,32},{1,97},{2,34},{3,99},{4,36},{5,101},{6,38},{7,103},{8,40},{... | collective-permute-start | bytes 1769480 | tf_op jit(solution)/shard_map/p2/ppermute | solution.py:25
  25.5 14.5 %copy-start.5 = (f32[1,96,768]{2,1,0:T(8,128)S(1)}, f32[1,96,768]{2,1,0:T(8,128)}, u32[]{:S(2)}) copy-start(f32[1,96,768]{2,1,0:T(8,128)} %param.12) | copy-start | bytes 884740
  25.5 16.9 %copy-start.6 = (s32[256]{0:T(256)S(1)}, s32[256]{0:T(256)}, u32[]{:S(2)}) copy-start(s32[256]{0:T(256)} %param.14) | copy-start | bytes 3076
  38.4 42.8 %copy-start.1 = (f32[2,384,768]{2,1,0:T(8,128)}, f32[2,384,768]{2,1,0:T(8,128)S(1)}, u32[]{:S(2)}) copy-start(f32[2,384,768]{2,1,0:T(8,128)S(1)} %collective-permute-done.5.rest_6_.rest_2_) | copy-start | bytes 7077892
  38.4 30.4 %collective-permute-start.10 = (f32[4,384,384]{2,1,0:T(8,128)}, f32[4,384,384]{2,1,0:T(8,128)}, u32[]{:S(2)}, u32[]{:S(2)}) collective-permute-start(f32[4,384,384]{2,1,0:T(8,128)} %bitcast_dynamic-update-slice_fusion.rest_2_), channel_id=1, source_target_pairs={{0,32},{1,97},{2,34},{3,99},{4,36},{5,101},{6,38},{7,103},{8,40},{... | collective-permute-start | bytes 7077896 | tf_op jit(solution)/shard_map/p3/ppermute | solution.py:25
  38.7 30.1 %collective-permute-start.9 = (f32[4,384,384]{2,1,0:T(8,128)}, f32[4,384,384]{2,1,0:T(8,128)}, u32[]{:S(2)}, u32[]{:S(2)}) collective-permute-start(f32[4,384,384]{2,1,0:T(8,128)} %bitcast_dynamic-update-slice_fusion.1.rest_0_), channel_id=1, source_target_pairs={{0,8},{1,25},{2,10},{3,27},{4,12},{5,29},{6,14},{7,31},{8,16},{9,1... | collective-permute-start | bytes 7077896 | tf_op jit(solution)/shard_map/p3/ppermute | solution.py:25
  40.0 30.4 %collective-permute-start.8 = (f32[2,384,768]{2,1,0:T(8,128)}, f32[2,384,768]{2,1,0:T(8,128)}, u32[]{:S(2)}, u32[]{:S(2)}) collective-permute-start(f32[2,384,768]{2,1,0:T(8,128)} %collective-permute-done.4.rest_5_.rest_1_), channel_id=1, source_target_pairs={{0,2},{1,7},{2,4},{3,1},{4,6},{5,3},{6,0},{7,5},{8,10},{9,15},{10,... | collective-permute-start | bytes 7077896 | tf_op jit(solution)/shard_map/p3z/ppermute | solution.py:25
  70.3 8.1 %collective-permute-start.14 = (f32[2,384,768]{2,1,0:T(8,128)}, f32[2,384,768]{2,1,0:T(8,128)S(1)}, u32[]{:S(2)}, u32[]{:S(2)}) collective-permute-start(f32[2,384,768]{2,1,0:T(8,128)} %collective-permute-done.8.rest_7_.rest_3_), channel_id=1, source_target_pairs={{0,1},{1,0},{2,3},{3,2},{4,5},{5,4},{6,7},{7,6},{8,9},{9,8},{10,11... | collective-permute-start | bytes 7077896 | tf_op jit(solution)/shard_map/p4s/ppermute | solution.py:25
  70.3 8.1 %collective-permute-start.15 = (f32[2,384,768]{2,1,0:T(8,128)S(1)}, f32[2,384,768]{2,1,0:T(8,128)S(1)}, u32[]{:S(2)}, u32[]{:S(2)}) collective-permute-start(f32[2,384,768]{2,1,0:T(8,128)S(1)} %collective-permute-done.5.rest_6_.rest_2_), channel_id=1, source_target_pairs={{0,1},{1,0},{2,3},{3,2},{4,5},{5,4},{6,7},{7,6},{8,9},{9,8},{10,11... | collective-permute-start | bytes 7077896 | tf_op jit(solution)/shard_map/p4s/ppermute | solution.py:25
  70.8 29.6 %collective-permute-start.13 = (f32[4,384,384]{2,1,0:T(8,128)}, f32[4,384,384]{2,1,0:T(8,128)}, u32[]{:S(2)}, u32[]{:S(2)}) collective-permute-start(f32[4,384,384]{2,1,0:T(8,128)} %bitcast_dynamic-update-slice_fusion.rest_2_), channel_id=1, source_target_pairs={{0,96},{1,33},{2,98},{3,35},{4,100},{5,37},{6,102},{7,39},{8,104},... | collective-permute-start | bytes 7077896 | tf_op jit(solution)/shard_map/p4/ppermute | solution.py:25
  73.8 29.2 %collective-permute-start.12 = (f32[4,384,384]{2,1,0:T(8,128)}, f32[4,384,384]{2,1,0:T(8,128)}, u32[]{:S(2)}, u32[]{:S(2)}) collective-permute-start(f32[4,384,384]{2,1,0:T(8,128)} %bitcast_dynamic-update-slice_fusion.1.rest_0_), channel_id=1, source_target_pairs={{0,24},{1,9},{2,26},{3,11},{4,28},{5,13},{6,30},{7,15},{8,0},{9,17... | collective-permute-start | bytes 7077896 | tf_op jit(solution)/shard_map/p4/ppermute | solution.py:25
  74.5 30.2 %collective-permute-start.11 = (f32[2,384,768]{2,1,0:T(8,128)S(1)}, f32[2,384,768]{2,1,0:T(8,128)}, u32[]{:S(2)}, u32[]{:S(2)}) collective-permute-start(f32[2,384,768]{2,1,0:T(8,128)S(1)} %collective-permute-done.5.rest_6_.rest_2_), channel_id=1, source_target_pairs={{0,2},{1,7},{2,4},{3,1},{4,6},{5,3},{6,0},{7,5},{8,10},{9,15},{10,... | collective-permute-start | bytes 7077896 | tf_op jit(solution)/shard_map/p4z/ppermute | solution.py:25
  78.4 1.4 copy-start.2
  79.8 1.4 copy-start.3
  104.7 4.7 %collective-permute-start.16 = (f32[2,384,768]{2,1,0:T(8,128)}, f32[2,384,768]{2,1,0:T(8,128)S(1)}, u32[]{:S(2)}, u32[]{:S(2)}) collective-permute-start(f32[2,384,768]{2,1,0:T(8,128)} %collective-permute-done.11.rest_12_.rest_4_), channel_id=1, source_target_pairs={{0,1},{1,0},{2,3},{3,2},{4,5},{5,4},{6,7},{7,6},{8,9},{9,8},{10,11... | collective-permute-start | bytes 7077896 | tf_op jit(solution)/shard_map/p5s/ppermute | solution.py:25
  104.7 30.4 %collective-permute-start.18 = (f32[4,384,384]{2,1,0:T(8,128)}, f32[4,384,384]{2,1,0:T(8,128)}, u32[]{:S(2)}, u32[]{:S(2)}) collective-permute-start(f32[4,384,384]{2,1,0:T(8,128)} %collective-permute-done.10.rest_3_), channel_id=1, source_target_pairs={{0,32},{1,97},{2,34},{3,99},{4,36},{5,101},{6,38},{7,103},{8,40},{... | collective-permute-start | bytes 7077896 | tf_op jit(solution)/shard_map/p5/ppermute | solution.py:25
  104.7 30.4 %collective-permute-start.17 = (f32[4,384,384]{2,1,0:T(8,128)}, f32[4,384,384]{2,1,0:T(8,128)}, u32[]{:S(2)}, u32[]{:S(2)}) collective-permute-start(f32[4,384,384]{2,1,0:T(8,128)} %collective-permute-done.9.rest_1_), channel_id=1, source_target_pairs={{0,8},{1,25},{2,10},{3,27},{4,12},{5,29},{6,14},{7,31},{8,16},{9,1... | collective-permute-start | bytes 7077896 | tf_op jit(solution)/shard_map/p5/ppermute | solution.py:25
  109.4 1.4 copy-start.4
  151.1 3.8 %collective-permute-start.19 = (f32[4,96,768]{2,1,0:T(8,128)}, f32[4,96,768]{2,1,0:T(8,128)S(1)}, u32[]{:S(2)}, u32[]{:S(2)}) collective-permute-start(f32[4,96,768]{2,1,0:T(8,128)} %get-tuple-element.67), channel_id=1, source_target_pairs={{0,1},{1,0},{2,3},{3,2},{4,5},{5,4},{6,7},{7,6},{8,9},{9,8},{10,11... | collective-permute-start | bytes 3538952 | tf_op jit(solution)/shard_map/swap/ppermute | solution.py:25
  151.2 3.0 %collective-permute-start.23 = (f32[1,768]{1,0:T(1,128)}, f32[1,768]{1,0:T(1,128)S(1)}, u32[]{:S(2)}, u32[]{:S(2)}) collective-permute-start(f32[1,768]{1,0:T(1,128)} %get-tuple-element.68), channel_id=1, source_target_pairs={{0,1},{1,0},{2,3},{3,2},{4,5},{5,4},{6,7},{7,6},{8,9},{9,8},{10,11... | collective-permute-start | bytes 9224 | tf_op jit(solution)/shard_map/swap/ppermute | solution.py:25
  154.9 4.8 %collective-permute-start.24 = (f32[1,768]{1,0:T(1,128)S(1)}, f32[1,768]{1,0:T(1,128)S(1)}, u32[]{:S(2)}, u32[]{:S(2)}) collective-permute-start(f32[1,768]{1,0:T(1,128)S(1)} %add.372), channel_id=1, source_target_pairs={{0,2},{1,3},{2,4},{3,5},{4,6},{5,7},{6,0},{7,1},{8,10},{9,11},{10,... | collective-permute-start | bytes 9224 | tf_op jit(solution)/shard_map/ppermute | solution.py:25
  154.9 4.8 %collective-permute-start.25 = (f32[1,768]{1,0:T(1,128)S(1)}, f32[1,768]{1,0:T(1,128)S(1)}, u32[]{:S(2)}, u32[]{:S(2)}) collective-permute-start(f32[1,768]{1,0:T(1,128)S(1)} %add.372), channel_id=1, source_target_pairs={{0,6},{1,7},{2,0},{3,1},{4,2},{5,3},{6,4},{7,5},{8,14},{9,15},{10,... | collective-permute-start | bytes 9224 | tf_op jit(solution)/shard_map/ppermute | solution.py:25
  158.1 5.1 %collective-permute-start.26 = (f32[1,768]{1,0:T(1,128)S(1)}, f32[1,768]{1,0:T(1,128)S(1)}, u32[]{:S(2)}, u32[]{:S(2)}) collective-permute-start(f32[1,768]{1,0:T(1,128)S(1)} %add.372), channel_id=1, source_target_pairs={{0,4},{1,5},{2,6},{3,7},{4,0},{5,1},{6,2},{7,3},{8,12},{9,13},{10,... | collective-permute-start | bytes 9224 | tf_op jit(solution)/shard_map/ppermute | solution.py:25
  159.6 23.9 %copy-start.7 = (f32[256]{0:T(256)S(1)}, f32[256]{0:T(256)}, u32[]{:S(2)}) copy-start(f32[256]{0:T(256)} %param.15) | copy-start | bytes 3076
  163.2 8.9 %collective-permute-start.27 = (f32[1,768]{1,0:T(1,128)S(1)}, f32[1,768]{1,0:T(1,128)S(1)}, u32[]{:S(2)}, u32[]{:S(2)}) collective-permute-start(f32[1,768]{1,0:T(1,128)S(1)} %add_add_fusion), channel_id=1, source_target_pairs={{0,24},{1,25},{2,26},{3,27},{4,28},{5,29},{6,30},{7,31},{8,0},{9,1... | collective-permute-start | bytes 9224 | tf_op jit(solution)/shard_map/ppermute | solution.py:25
  163.8 8.3 %collective-permute-start.28 = (f32[1,768]{1,0:T(1,128)S(1)}, f32[1,768]{1,0:T(1,128)S(1)}, u32[]{:S(2)}, u32[]{:S(2)}) collective-permute-start(f32[1,768]{1,0:T(1,128)S(1)} %add_add_fusion), channel_id=1, source_target_pairs={{0,16},{1,17},{2,18},{3,19},{4,20},{5,21},{6,22},{7,23},{8,24},{9,... | collective-permute-start | bytes 9224 | tf_op jit(solution)/shard_map/ppermute | solution.py:25
  166.7 5.5 %collective-permute-start.29 = (f32[1,768]{1,0:T(1,128)S(1)}, f32[1,768]{1,0:T(1,128)S(1)}, u32[]{:S(2)}, u32[]{:S(2)}) collective-permute-start(f32[1,768]{1,0:T(1,128)S(1)} %add_add_fusion), channel_id=1, source_target_pairs={{0,8},{1,9},{2,10},{3,11},{4,12},{5,13},{6,14},{7,15},{8,16},{9,17... | collective-permute-start | bytes 9224 | tf_op jit(solution)/shard_map/ppermute | solution.py:25
  168.8 15.2 %collective-permute-start.20 = (f32[96,768]{1,0:T(8,128)S(1)}, f32[96,768]{1,0:T(8,128)S(1)}, u32[]{:S(2)}, u32[]{:S(2)}) collective-permute-start(f32[96,768]{1,0:T(8,128)S(1)} %get-tuple-element.76), channel_id=1, source_target_pairs={{0,2},{1,3},{2,4},{3,5},{4,6},{5,7},{6,0},{7,1},{8,10},{9,11},{10,... | collective-permute-start | bytes 884744 | tf_op jit(solution)/shard_map/ppermute | solution.py:25
  168.9 15.2 %collective-permute-start.21 = (f32[96,768]{1,0:T(8,128)S(1)}, f32[96,768]{1,0:T(8,128)S(1)}, u32[]{:S(2)}, u32[]{:S(2)}) collective-permute-start(f32[96,768]{1,0:T(8,128)S(1)} %get-tuple-element.78), channel_id=1, source_target_pairs={{0,6},{1,7},{2,0},{3,1},{4,2},{5,3},{6,4},{7,5},{8,14},{9,15},{10,... | collective-permute-start | bytes 884744 | tf_op jit(solution)/shard_map/ppermute | solution.py:25
  172.1 11.9 %collective-permute-start.22 = (f32[96,768]{1,0:T(8,128)S(1)}, f32[96,768]{1,0:T(8,128)S(1)}, u32[]{:S(2)}, u32[]{:S(2)}) collective-permute-start(f32[96,768]{1,0:T(8,128)S(1)} %get-tuple-element.77), channel_id=1, source_target_pairs={{0,4},{1,5},{2,6},{3,7},{4,0},{5,1},{6,2},{7,3},{8,12},{9,13},{10,... | collective-permute-start | bytes 884744 | tf_op jit(solution)/shard_map/ppermute | solution.py:25
  172.2 4.4 %collective-permute-start.30 = (f32[4,768]{1,0:T(4,128)S(1)}, f32[4,768]{1,0:T(4,128)S(1)}, u32[]{:S(2)}, u32[]{:S(2)}) collective-permute-start(f32[4,768]{1,0:T(4,128)S(1)} %get-tuple-element.84), channel_id=1, source_target_pairs={{0,96},{1,97},{2,98},{3,99},{4,100},{5,101},{6,102},{7,103},{8,104... | collective-permute-start | bytes 36872 | tf_op jit(solution)/shard_map/ppermute | solution.py:25
  175.1 5.2 %collective-permute-start.31 = (f32[4,768]{1,0:T(4,128)S(1)}, f32[4,768]{1,0:T(4,128)S(1)}, u32[]{:S(2)}, u32[]{:S(2)}) collective-permute-start(f32[4,768]{1,0:T(4,128)S(1)} %get-tuple-element.84), channel_id=1, source_target_pairs={{0,64},{1,65},{2,66},{3,67},{4,68},{5,69},{6,70},{7,71},{8,72},{9,... | collective-permute-start | bytes 36872 | tf_op jit(solution)/shard_map/ppermute | solution.py:25
  176.5 5.2 %collective-permute-start.32 = (f32[4,768]{1,0:T(4,128)S(1)}, f32[4,768]{1,0:T(4,128)S(1)}, u32[]{:S(2)}, u32[]{:S(2)}) collective-permute-start(f32[4,768]{1,0:T(4,128)S(1)} %get-tuple-element.84), channel_id=1, source_target_pairs={{0,32},{1,33},{2,34},{3,35},{4,36},{5,37},{6,38},{7,39},{8,40},{9,... | collective-permute-start | bytes 36872 | tf_op jit(solution)/shard_map/ppermute | solution.py:25

commit v6 on v5

--- a/solution.py
+++ b/solution.py
@@ -53,7 +53,6 @@
 
 
 ROWS = ((1,), (0,))
-SLOTS = 3
 
 LINES = ("a0", "a1", "a2", "a3", "b0", "b1", "b2", "b3")
 BLOCKS = ("own", "sib", "za", "zb", "zc", "zu", "zs", "zt")
@@ -79,6 +78,7 @@
 
 
 def pair_loop(begin, end, refs, table, mask, sums, meanwhile, s_buf, m_buf, spot, s_sem, m_sem):
+    slots = s_buf.shape[0]
     first_group = end[0] - begin[0]
     count = first_group + end[1] - begin[1]
 
@@ -123,7 +123,7 @@
         group = spot[slot, 2]
         sums[group] = sums[group] + part_sum
 
-    for ahead in range(SLOTS - 1):
+    for ahead in range(slots - 1):
 
         @pl.when(ahead < count)
         def _():
@@ -133,13 +133,13 @@
         meanwhile()
 
     def step(p, carry):
-        later = p + SLOTS - 1
+        later = p + slots - 1
 
         @pl.when(later < count)
         def _():
-            start(later, lax.rem(later, SLOTS))
-
-        finish(lax.rem(p, SLOTS))
+            start(later, lax.rem(later, slots))
+
+        finish(lax.rem(p, slots))
         return carry
 
     lax.fori_loop(0, count, step, 0)
@@ -150,13 +150,13 @@
 VMEM = pl.BlockSpec(memory_space=pltpu.VMEM)
 
 
-def buffers():
+def buffers(slots=3):
     return [
-        pltpu.VMEM((SLOTS, 384, 768), FULL),
-        pltpu.VMEM((SLOTS, 768, 768), FULL),
-        pltpu.SMEM((SLOTS, 3), jnp.int32),
-        pltpu.SemaphoreType.DMA((SLOTS, 2)),
-        pltpu.SemaphoreType.DMA((SLOTS, 2)),
+        pltpu.VMEM((slots, 384, 768), FULL),
+        pltpu.VMEM((slots, 768, 768), FULL),
+        pltpu.SMEM((slots, 3), jnp.int32),
+        pltpu.SemaphoreType.DMA((slots, 2)),
+        pltpu.SemaphoreType.DMA((slots, 2)),
     ]
 
 
@@ -286,7 +286,7 @@
             pltpu.VMEM((768, 768), SHORT),
             pltpu.SemaphoreType.DMA((4,)),
         ]
-        + buffers(),
+        + buffers(2),
         compiler_params=pltpu.CompilerParams(vmem_limit_bytes=60 << 20),
         cost_estimate=cost(6),
         name="last_products",

time: 185 us -> 185 us (level)
  no operation moved by 1% of the time
where the time goes in v6:
time: 185 us
  waiting for transfers between devices  86.7 us (47%)
  Pallas kernels  46.4 us (25%)
  starting transfers between devices  33 us (18%)
  local copies, waits for them, and re-layouts  10.6 us (6%)
  other arithmetic  7.37 us (4%)
    ppermute x33, waiting for transfers between devices, send(): return lax.ppermute(value, AXES, pairs)  86.7 us
    ppermute x33, starting transfers between devices, send(): return lax.ppermute(value, AXES, pairs)  33 us
    pallas_call x1, Pallas kernels, early_products(): pl.pallas_call(body, out_shape=shape(2, 384, 768), in_specs=[SMEM, SMEM,...  15.7 us
    pallas_call x1, Pallas kernels, last_products(): pl.pallas_call(body, out_shape=(shape(768, 768), shape(1, 768), shape(4,...  15.7 us
    pallas_call x1, Pallas kernels, middle_products(): pl.pallas_call(body, out_shape=(shape(2, 384, 768), half, half), in_specs...  15 us
    unnamed x16, local copies, waits for them, and re-layouts  4.24 us
  transfers between devices with their start and end apart: 33, of which 19 were waited for; matrix products, arithmetic and copies ran while one was open for 6% of the time, Pallas kernels for 17%

profile of v6, /device:TPU:16, one launch (start us, length us, event | category | flops | bytes accessed | tf_op | source)
XLA Modules:
  0.0 184.9 jit_solution(6891018905524235062)
XLA Ops:
  0.6 1.5 slice_bitcast_fusion
  2.2 1.6 collective-permute-start
  3.8 1.7 collective-permute-start.2
  5.5 1.3 collective-permute-start.1
  6.8 0.7 collective-permute-start.3
  7.5 1.9 %collective-permute-start.5 = (f32[2,384,768]{2,1,0:T(8,128)S(1)}, f32[2,384,768]{2,1,0:T(8,128)S(1)}, u32[]{:S(2)}, u32[]{:S(2)}) collective-permute-start(f32[2,384,768]{2,1,0:T(8,128)S(1)} %bitcast.58), channel_id=1, source_target_pairs={{0,2},{1,7},{2,4},{3,1},{4,6},{5,3},{6,0},{7,5},{8,10},{9,15},{10,... | collective-permute-start | bytes 7077896 | tf_op jit(solution)/shard_map/p1z/ppermute | solution.py:25
  9.4 8.8 %collective-permute-done = f32[384,384]{1,0:T(8,128)S(1)} collective-permute-done((f32[384,384]{1,0:T(8,128)S(1)}, f32[384,384]{1,0:T(8,128)S(1)}, u32[]{:S(2)}, u32[]{:S(2)}) %collective-permute-start) | collective-permute-done | bytes 589856 | tf_op jit(solution)/shard_map/p1/ppermute | solution.py:25
  18.3 1.7 collective-permute-done.1
  20.0 2.3 %collective-permute-start.7 = (f32[384,384]{1,0:T(8,128)S(1)}, f32[384,384]{1,0:T(8,128)S(1)}, u32[]{:S(2)}, u32[]{:S(2)}) collective-permute-start(f32[384,384]{1,0:T(8,128)S(1)} %collective-permute-done.1), channel_id=1, source_target_pairs={{0,8},{1,25},{2,10},{3,27},{4,12},{5,29},{6,14},{7,31},{8,16},{9,1... | collective-permute-start | bytes 1769480 | tf_op jit(solution)/shard_map/p2/ppermute | solution.py:25
  22.9 2.6 %maximum_maximum_fusion.1 = (f32[4,384,384]{2,1,0:T(8,128)}, f32[4,384,384]{2,1,0:T(8,128)}) fusion(f32[1,384,384]{2,1,0:T(8,128)S(1)} %bitcast.63, f32[1,384,384]{2,1,0:T(8,128)S(1)} %bitcast.62, f32[1,384,384]{2,1,0:T(8,128)S(1)} %get-tuple-element.79, f32[4]{0:T(128)S(1)} %pad.19.clone, f32[1,384,384]{2,1,0:T(8,128)S(1)} %bitcast.61, ...), kind=kLoop, calls=%fused_computation.2 | loop fusion | flops 3538944 | bytes 8257552 | tf_op jit(solution)/shard_map/concatenate | solution.py:328
  25.5 4.4 %collective-permute-done.7 = f32[384,384]{1,0:T(8,128)S(1)} collective-permute-done((f32[384,384]{1,0:T(8,128)S(1)}, f32[384,384]{1,0:T(8,128)S(1)}, u32[]{:S(2)}, u32[]{:S(2)}) %collective-permute-start.7) | collective-permute-done | bytes 589856 | tf_op jit(solution)/shard_map/p2/ppermute | solution.py:25
  29.9 0.9 bitcast_dynamic-update-slice_fusion.rest_2_
  30.7 2.8 %collective-permute-done.6 = f32[384,384]{1,0:T(8,128)S(1)} collective-permute-done((f32[384,384]{1,0:T(8,128)S(1)}, f32[384,384]{1,0:T(8,128)S(1)}, u32[]{:S(2)}, u32[]{:S(2)}) %collective-permute-start.6) | collective-permute-done | bytes 589856 | tf_op jit(solution)/shard_map/p2/ppermute | solution.py:25
  33.5 0.9 bitcast_dynamic-update-slice_fusion.1.rest_0_
  34.3 4.0 %collective-permute-done.5.rest_6_.rest_2_ = f32[2,384,768]{2,1,0:T(8,128)S(1)} collective-permute-done((f32[2,384,768]{2,1,0:T(8,128)S(1)}, f32[2,384,768]{2,1,0:T(8,128)S(1)}, u32[]{:S(2)}, u32[]{:S(2)}) %collective-permute-start.5) | collective-permute-done | bytes 2359328 | tf_op jit(solution)/shard_map/p1z/ppermute | solution.py:25
  38.7 1.3 collective-permute-start.9
  41.8 0.6 pad_add_fusion.table_ref
  42.4 26.4 %collective-permute-done.10.rest_3_ = f32[4,384,384]{2,1,0:T(8,128)} collective-permute-done((f32[4,384,384]{2,1,0:T(8,128)}, f32[4,384,384]{2,1,0:T(8,128)}, u32[]{:S(2)}, u32[]{:S(2)}) %collective-permute-start.10) | collective-permute-done | bytes 2359328 | tf_op jit(solution)/shard_map/p3/ppermute | solution.py:25
  68.8 1.6 collective-permute-done.8.rest_7_.rest_3_
  70.8 3.0 %collective-permute-start.13 = (f32[4,384,384]{2,1,0:T(8,128)}, f32[4,384,384]{2,1,0:T(8,128)}, u32[]{:S(2)}, u32[]{:S(2)}) collective-permute-start(f32[4,384,384]{2,1,0:T(8,128)} %bitcast_dynamic-update-slice_fusion.rest_2_), channel_id=1, source_target_pairs={{0,96},{1,33},{2,98},{3,35},{4,100},{5,37},{6,102},{7,39},{8,104},... | collective-permute-start | bytes 7077896 | tf_op jit(solution)/shard_map/p4/ppermute | solution.py:25
  73.8 0.7 collective-permute-start.12
  74.5 3.9 %collective-permute-done.14.rest_8_.rest_6_ = f32[2,384,768]{2,1,0:T(8,128)S(1)} collective-permute-done((f32[2,384,768]{2,1,0:T(8,128)}, f32[2,384,768]{2,1,0:T(8,128)S(1)}, u32[]{:S(2)}, u32[]{:S(2)}) %collective-permute-start.14) | collective-permute-done | bytes 2359328 | tf_op jit(solution)/shard_map/p4s/ppermute | solution.py:25
  78.4 1.4 copy-done.2
  79.8 1.4 copy-done.3
  81.2 15.7 %early_products.1.rest_14_ = f32[2,384,768]{2,1,0:T(8,128)} custom-call(s32[8]{0:T(128)} %concatenate.16.where_ref, s32[24]{0:T(128)} %bitcast.70, s32[3,32]{1,0:T(4,128)} %pad_add_fusion.table_ref, f32[4,384,384]{2,1,0:T(8,128)} %bitcast_dynamic-update-slice_fusion.1.rest_0_, f32[4,384,384]{2,1,0:T(8,128)} %collective-permute-done.9.rest_1_, ...), custom_call_target="tpu_custom_call" | custom-call | flops 8400000000 | bytes 21600000 | tf_op jit(solution)/shard_map/early_products/pallas_call | solution.py:184
  96.9 3.5 %collective-permute-done.13.rest_11_ = f32[4,384,384]{2,1,0:T(8,128)} collective-permute-done((f32[4,384,384]{2,1,0:T(8,128)}, f32[4,384,384]{2,1,0:T(8,128)}, u32[]{:S(2)}, u32[]{:S(2)}) %collective-permute-start.13) | collective-permute-done | bytes 2359328 | tf_op jit(solution)/shard_map/p4/ppermute | solution.py:25
  100.5 2.5 %collective-permute-done.12.rest_10_ = f32[4,384,384]{2,1,0:T(8,128)} collective-permute-done((f32[4,384,384]{2,1,0:T(8,128)}, f32[4,384,384]{2,1,0:T(8,128)}, u32[]{:S(2)}, u32[]{:S(2)}) %collective-permute-start.12) | collective-permute-done | bytes 2359328 | tf_op jit(solution)/shard_map/p4/ppermute | solution.py:25
  103.0 1.7 collective-permute-done.11.rest_12_.rest_4_
  104.7 1.3 collective-permute-start.17
  106.0 3.5 %collective-permute-done.16.rest_13_.rest_5_ = f32[2,384,768]{2,1,0:T(8,128)S(1)} collective-permute-done((f32[2,384,768]{2,1,0:T(8,128)}, f32[2,384,768]{2,1,0:T(8,128)S(1)}, u32[]{:S(2)}, u32[]{:S(2)}) %collective-permute-start.16) | collective-permute-done | bytes 2359328 | tf_op jit(solution)/shard_map/p5s/ppermute | solution.py:25
  109.4 1.4 copy-done.4
  110.9 15.0 %middle_products.1 = (f32[2,384,768]{2,1,0:T(8,128)}, bf16[768,768]{1,0:T(8,128)(2,1)}, bf16[768,768]{1,0:T(8,128)(2,1)}) custom-call(s32[8]{0:T(128)} %concatenate.16.where_ref, s32[24]{0:T(128)} %bitcast.71, s32[3,32]{1,0:T(4,128)} %pad_add_fusion.table_ref, f32[4,384,384]{2,1,0:T(8,128)} %bitcast_dynamic-update-slice_fusion.1.rest_0_, ...), custom_call_target="tpu_custom_call" | custom-call | flops 8400000000 | bytes 21600000 | tf_op jit(solution)/shard_map/middle_products/pallas_call | solution.py:219
  125.9 9.2 %collective-permute-done.18.rest_9_ = f32[4,384,384]{2,1,0:T(8,128)} collective-permute-done((f32[4,384,384]{2,1,0:T(8,128)}, f32[4,384,384]{2,1,0:T(8,128)}, u32[]{:S(2)}, u32[]{:S(2)}) %collective-permute-start.18) | collective-permute-done | bytes 2359328 | tf_op jit(solution)/shard_map/p5/ppermute | solution.py:25
  135.1 15.7 %last_products.1 = (f32[768,768]{1,0:T(8,128)}, f32[1,768]{1,0:T(1,128)}, f32[4,96,768]{2,1,0:T(8,128)}, f32[4,96,768]{2,1,0:T(8,128)}) custom-call(s32[8]{0:T(128)} %concatenate.16.where_ref, s32[24]{0:T(128)} %bitcast.72, s32[3,32]{1,0:T(4,128)} %pad_add_fusion.table_ref, f32[2,384,768]{2,1,0:T(8,128)} %bitcast.57, ...), custom_call_target="tpu_custom_call" | custom-call | flops 8400000000 | bytes 21600000 | tf_op jit(solution)/shard_map/last_products/pallas_call | solution.py:277
  151.4 2.5 %collective-permute-done.23 = f32[1,768]{1,0:T(1,128)S(1)} collective-permute-done((f32[1,768]{1,0:T(1,128)}, f32[1,768]{1,0:T(1,128)S(1)}, u32[]{:S(2)}, u32[]{:S(2)}) %collective-permute-start.23) | collective-permute-done | bytes 3104 | tf_op jit(solution)/shard_map/swap/ppermute | solution.py:25
  153.9 0.7 add.372
  154.6 3.2 %collective-permute-start.25 = (f32[1,768]{1,0:T(1,128)S(1)}, f32[1,768]{1,0:T(1,128)S(1)}, u32[]{:S(2)}, u32[]{:S(2)}) collective-permute-start(f32[1,768]{1,0:T(1,128)S(1)} %add.372), channel_id=1, source_target_pairs={{0,6},{1,7},{2,0},{3,1},{4,2},{5,3},{6,4},{7,5},{8,14},{9,15},{10,... | collective-permute-start | bytes 9224 | tf_op jit(solution)/shard_map/ppermute | solution.py:25
  157.8 1.4 add.356
  159.4 3.5 %collective-permute-done.26 = f32[1,768]{1,0:T(1,128)S(1)} collective-permute-done((f32[1,768]{1,0:T(1,128)S(1)}, f32[1,768]{1,0:T(1,128)S(1)}, u32[]{:S(2)}, u32[]{:S(2)}) %collective-permute-start.26) | collective-permute-done | bytes 3104 | tf_op jit(solution)/shard_map/ppermute | solution.py:25
  163.5 2.9 %collective-permute-start.28 = (f32[1,768]{1,0:T(1,128)S(1)}, f32[1,768]{1,0:T(1,128)S(1)}, u32[]{:S(2)}, u32[]{:S(2)}) collective-permute-start(f32[1,768]{1,0:T(1,128)S(1)} %add_add_fusion), channel_id=1, source_target_pairs={{0,16},{1,17},{2,18},{3,19},{4,20},{5,21},{6,22},{7,23},{8,24},{9,... | collective-permute-start | bytes 9224 | tf_op jit(solution)/shard_map/ppermute | solution.py:25
  166.4 2.0 %collective-permute-start.29 = (f32[1,768]{1,0:T(1,128)S(1)}, f32[1,768]{1,0:T(1,128)S(1)}, u32[]{:S(2)}, u32[]{:S(2)}) collective-permute-start(f32[1,768]{1,0:T(1,128)S(1)} %add_add_fusion), channel_id=1, source_target_pairs={{0,8},{1,9},{2,10},{3,11},{4,12},{5,13},{6,14},{7,15},{8,16},{9,17... | collective-permute-start | bytes 9224 | tf_op jit(solution)/shard_map/ppermute | solution.py:25
  168.6 3.2 %collective-permute-start.21 = (f32[96,768]{1,0:T(8,128)S(1)}, f32[96,768]{1,0:T(8,128)S(1)}, u32[]{:S(2)}, u32[]{:S(2)}) collective-permute-start(f32[96,768]{1,0:T(8,128)S(1)} %get-tuple-element.78), channel_id=1, source_target_pairs={{0,6},{1,7},{2,0},{3,1},{4,2},{5,3},{6,4},{7,5},{8,14},{9,15},{10,... | collective-permute-start | bytes 884744 | tf_op jit(solution)/shard_map/ppermute | solution.py:25
  171.8 3.3 %collective-permute-start.30 = (f32[4,768]{1,0:T(4,128)S(1)}, f32[4,768]{1,0:T(4,128)S(1)}, u32[]{:S(2)}, u32[]{:S(2)}) collective-permute-start(f32[4,768]{1,0:T(4,128)S(1)} %get-tuple-element.84), channel_id=1, source_target_pairs={{0,96},{1,97},{2,98},{3,99},{4,100},{5,101},{6,102},{7,103},{8,104... | collective-permute-start | bytes 36872 | tf_op jit(solution)/shard_map/ppermute | solution.py:25
  175.1 1.4 collective-permute-done.30
  176.6 3.8 %collective-permute-done.31 = f32[4,768]{1,0:T(4,128)S(1)} collective-permute-done((f32[4,768]{1,0:T(4,128)S(1)}, f32[4,768]{1,0:T(4,128)S(1)}, u32[]{:S(2)}, u32[]{:S(2)}) %collective-permute-start.31) | collective-permute-done | bytes 12320 | tf_op jit(solution)/shard_map/ppermute | solution.py:25
  180.3 1.4 collective-permute-done.32
  181.8 1.7 gather_fusion
  184.1 0.8 fusion.3
  (64 shorter events, 5.3 us)
Async XLA Ops:
  0.6 6.9 %copy-start = (f32[1,768,768]{2,1,0:T(8,128)S(1)}, f32[1,768,768]{2,1,0:T(8,128)}, u32[]{:S(2)}) copy-start(f32[1,768,768]{2,1,0:T(8,128)} %param.11) | copy-start | bytes 7077892
  2.2 16.1 %collective-permute-start = (f32[384,384]{1,0:T(8,128)S(1)}, f32[384,384]{1,0:T(8,128)S(1)}, u32[]{:S(2)}, u32[]{:S(2)}) collective-permute-start(f32[384,384]{1,0:T(8,128)S(1)} %get-tuple-element.82), channel_id=1, source_target_pairs={{0,32},{1,97},{2,34},{3,99},{4,36},{5,101},{6,38},{7,103},{8,40},{... | collective-permute-start | bytes 1769480 | tf_op jit(solution)/shard_map/p1/ppermute | solution.py:25
  3.8 14.5 %collective-permute-start.2 = (f32[384,384]{1,0:T(8,128)S(1)}, f32[384,384]{1,0:T(8,128)S(1)}, u32[]{:S(2)}, u32[]{:S(2)}) collective-permute-start(f32[384,384]{1,0:T(8,128)S(1)} %get-tuple-element.82), channel_id=1, source_target_pairs={{0,96},{1,33},{2,98},{3,35},{4,100},{5,37},{6,102},{7,39},{8,104},... | collective-permute-start | bytes 1769480 | tf_op jit(solution)/shard_map/p1/ppermute | solution.py:25
  5.5 14.5 %collective-permute-start.1 = (f32[384,384]{1,0:T(8,128)S(1)}, f32[384,384]{1,0:T(8,128)S(1)}, u32[]{:S(2)}, u32[]{:S(2)}) collective-permute-start(f32[384,384]{1,0:T(8,128)S(1)} %get-tuple-element.81), channel_id=1, source_target_pairs={{0,8},{1,25},{2,10},{3,27},{4,12},{5,29},{6,14},{7,31},{8,16},{9,1... | collective-permute-start | bytes 1769480 | tf_op jit(solution)/shard_map/p1/ppermute | solution.py:25
  6.8 13.2 %collective-permute-start.3 = (f32[384,384]{1,0:T(8,128)S(1)}, f32[384,384]{1,0:T(8,128)S(1)}, u32[]{:S(2)}, u32[]{:S(2)}) collective-permute-start(f32[384,384]{1,0:T(8,128)S(1)} %get-tuple-element.81), channel_id=1, source_target_pairs={{0,24},{1,9},{2,26},{3,11},{4,28},{5,13},{6,30},{7,15},{8,0},{9,17... | collective-permute-start | bytes 1769480 | tf_op jit(solution)/shard_map/p1/ppermute | solution.py:25
  7.5 30.9 %collective-permute-start.5 = (f32[2,384,768]{2,1,0:T(8,128)S(1)}, f32[2,384,768]{2,1,0:T(8,128)S(1)}, u32[]{:S(2)}, u32[]{:S(2)}) collective-permute-start(f32[2,384,768]{2,1,0:T(8,128)S(1)} %bitcast.58), channel_id=1, source_target_pairs={{0,2},{1,7},{2,4},{3,1},{4,6},{5,3},{6,0},{7,5},{8,10},{9,15},{10,... | collective-permute-start | bytes 7077896 | tf_op jit(solution)/shard_map/p1z/ppermute | solution.py:25
  20.0 18.4 %collective-permute-start.4 = (f32[2,384,768]{2,1,0:T(8,128)S(1)}, f32[2,384,768]{2,1,0:T(8,128)}, u32[]{:S(2)}, u32[]{:S(2)}) collective-permute-start(f32[2,384,768]{2,1,0:T(8,128)S(1)} %bitcast.59), channel_id=1, source_target_pairs={{0,1},{1,0},{2,3},{3,2},{4,5},{5,4},{6,7},{7,6},{8,9},{9,8},{10,11... | collective-permute-start | bytes 7077896 | tf_op jit(solution)/shard_map/p2s/ppermute | solution.py:25
  20.0 9.9 %collective-permute-start.7 = (f32[384,384]{1,0:T(8,128)S(1)}, f32[384,384]{1,0:T(8,128)S(1)}, u32[]{:S(2)}, u32[]{:S(2)}) collective-permute-start(f32[384,384]{1,0:T(8,128)S(1)} %collective-permute-done.1), channel_id=1, source_target_pairs={{0,8},{1,25},{2,10},{3,27},{4,12},{5,29},{6,14},{7,31},{8,16},{9,1... | collective-permute-start | bytes 1769480 | tf_op jit(solution)/shard_map/p2/ppermute | solution.py:25
  22.4 11.1 %collective-permute-start.6 = (f32[384,384]{1,0:T(8,128)S(1)}, f32[384,384]{1,0:T(8,128)S(1)}, u32[]{:S(2)}, u32[]{:S(2)}) collective-permute-start(f32[384,384]{1,0:T(8,128)S(1)} %collective-permute-done), channel_id=1, source_target_pairs={{0,32},{1,97},{2,34},{3,99},{4,36},{5,101},{6,38},{7,103},{8,40},{... | collective-permute-start | bytes 1769480 | tf_op jit(solution)/shard_map/p2/ppermute | solution.py:25
  25.5 14.5 %copy-start.5 = (f32[1,96,768]{2,1,0:T(8,128)S(1)}, f32[1,96,768]{2,1,0:T(8,128)}, u32[]{:S(2)}) copy-start(f32[1,96,768]{2,1,0:T(8,128)} %param.12) | copy-start | bytes 884740
  25.5 16.9 %copy-start.6 = (s32[256]{0:T(256)S(1)}, s32[256]{0:T(256)}, u32[]{:S(2)}) copy-start(s32[256]{0:T(256)} %param.14) | copy-start | bytes 3076
  38.4 42.8 %copy-start.1 = (f32[2,384,768]{2,1,0:T(8,128)}, f32[2,384,768]{2,1,0:T(8,128)S(1)}, u32[]{:S(2)}) copy-start(f32[2,384,768]{2,1,0:T(8,128)S(1)} %collective-permute-done.5.rest_6_.rest_2_) | copy-start | bytes 7077892
  38.4 30.4 %collective-permute-start.10 = (f32[4,384,384]{2,1,0:T(8,128)}, f32[4,384,384]{2,1,0:T(8,128)}, u32[]{:S(2)}, u32[]{:S(2)}) collective-permute-start(f32[4,384,384]{2,1,0:T(8,128)} %bitcast_dynamic-update-slice_fusion.rest_2_), channel_id=1, source_target_pairs={{0,32},{1,97},{2,34},{3,99},{4,36},{5,101},{6,38},{7,103},{8,40},{... | collective-permute-start | bytes 7077896 | tf_op jit(solution)/shard_map/p3/ppermute | solution.py:25
  38.7 30.1 %collective-permute-start.9 = (f32[4,384,384]{2,1,0:T(8,128)}, f32[4,384,384]{2,1,0:T(8,128)}, u32[]{:S(2)}, u32[]{:S(2)}) collective-permute-start(f32[4,384,384]{2,1,0:T(8,128)} %bitcast_dynamic-update-slice_fusion.1.rest_0_), channel_id=1, source_target_pairs={{0,8},{1,25},{2,10},{3,27},{4,12},{5,29},{6,14},{7,31},{8,16},{9,1... | collective-permute-start | bytes 7077896 | tf_op jit(solution)/shard_map/p3/ppermute | solution.py:25
  40.0 30.4 %collective-permute-start.8 = (f32[2,384,768]{2,1,0:T(8,128)}, f32[2,384,768]{2,1,0:T(8,128)}, u32[]{:S(2)}, u32[]{:S(2)}) collective-permute-start(f32[2,384,768]{2,1,0:T(8,128)} %collective-permute-done.4.rest_5_.rest_1_), channel_id=1, source_target_pairs={{0,2},{1,7},{2,4},{3,1},{4,6},{5,3},{6,0},{7,5},{8,10},{9,15},{10,... | collective-permute-start | bytes 7077896 | tf_op jit(solution)/shard_map/p3z/ppermute | solution.py:25
  70.3 8.1 %collective-permute-start.14 = (f32[2,384,768]{2,1,0:T(8,128)}, f32[2,384,768]{2,1,0:T(8,128)S(1)}, u32[]{:S(2)}, u32[]{:S(2)}) collective-permute-start(f32[2,384,768]{2,1,0:T(8,128)} %collective-permute-done.8.rest_7_.rest_3_), channel_id=1, source_target_pairs={{0,1},{1,0},{2,3},{3,2},{4,5},{5,4},{6,7},{7,6},{8,9},{9,8},{10,11... | collective-permute-start | bytes 7077896 | tf_op jit(solution)/shard_map/p4s/ppermute | solution.py:25
  70.3 8.1 %collective-permute-start.15 = (f32[2,384,768]{2,1,0:T(8,128)S(1)}, f32[2,384,768]{2,1,0:T(8,128)S(1)}, u32[]{:S(2)}, u32[]{:S(2)}) collective-permute-start(f32[2,384,768]{2,1,0:T(8,128)S(1)} %collective-permute-done.5.rest_6_.rest_2_), channel_id=1, source_target_pairs={{0,1},{1,0},{2,3},{3,2},{4,5},{5,4},{6,7},{7,6},{8,9},{9,8},{10,11... | collective-permute-start | bytes 7077896 | tf_op jit(solution)/shard_map/p4s/ppermute | solution.py:25
  70.8 29.6 %collective-permute-start.13 = (f32[4,384,384]{2,1,0:T(8,128)}, f32[4,384,384]{2,1,0:T(8,128)}, u32[]{:S(2)}, u32[]{:S(2)}) collective-permute-start(f32[4,384,384]{2,1,0:T(8,128)} %bitcast_dynamic-update-slice_fusion.rest_2_), channel_id=1, source_target_pairs={{0,96},{1,33},{2,98},{3,35},{4,100},{5,37},{6,102},{7,39},{8,104},... | collective-permute-start | bytes 7077896 | tf_op jit(solution)/shard_map/p4/ppermute | solution.py:25
  73.8 29.2 %collective-permute-start.12 = (f32[4,384,384]{2,1,0:T(8,128)}, f32[4,384,384]{2,1,0:T(8,128)}, u32[]{:S(2)}, u32[]{:S(2)}) collective-permute-start(f32[4,384,384]{2,1,0:T(8,128)} %bitcast_dynamic-update-slice_fusion.1.rest_0_), channel_id=1, source_target_pairs={{0,24},{1,9},{2,26},{3,11},{4,28},{5,13},{6,30},{7,15},{8,0},{9,17... | collective-permute-start | bytes 7077896 | tf_op jit(solution)/shard_map/p4/ppermute | solution.py:25
  74.5 30.2 %collective-permute-start.11 = (f32[2,384,768]{2,1,0:T(8,128)S(1)}, f32[2,384,768]{2,1,0:T(8,128)}, u32[]{:S(2)}, u32[]{:S(2)}) collective-permute-start(f32[2,384,768]{2,1,0:T(8,128)S(1)} %collective-permute-done.5.rest_6_.rest_2_), channel_id=1, source_target_pairs={{0,2},{1,7},{2,4},{3,1},{4,6},{5,3},{6,0},{7,5},{8,10},{9,15},{10,... | collective-permute-start | bytes 7077896 | tf_op jit(solution)/shard_map/p4z/ppermute | solution.py:25
  78.4 1.4 copy-start.2
  79.8 1.4 copy-start.3
  104.7 4.7 %collective-permute-start.16 = (f32[2,384,768]{2,1,0:T(8,128)}, f32[2,384,768]{2,1,0:T(8,128)S(1)}, u32[]{:S(2)}, u32[]{:S(2)}) collective-permute-start(f32[2,384,768]{2,1,0:T(8,128)} %collective-permute-done.11.rest_12_.rest_4_), channel_id=1, source_target_pairs={{0,1},{1,0},{2,3},{3,2},{4,5},{5,4},{6,7},{7,6},{8,9},{9,8},{10,11... | collective-permute-start | bytes 7077896 | tf_op jit(solution)/shard_map/p5s/ppermute | solution.py:25
  104.7 30.4 %collective-permute-start.18 = (f32[4,384,384]{2,1,0:T(8,128)}, f32[4,384,384]{2,1,0:T(8,128)}, u32[]{:S(2)}, u32[]{:S(2)}) collective-permute-start(f32[4,384,384]{2,1,0:T(8,128)} %collective-permute-done.10.rest_3_), channel_id=1, source_target_pairs={{0,32},{1,97},{2,34},{3,99},{4,36},{5,101},{6,38},{7,103},{8,40},{... | collective-permute-start | bytes 7077896 | tf_op jit(solution)/shard_map/p5/ppermute | solution.py:25
  104.7 30.4 %collective-permute-start.17 = (f32[4,384,384]{2,1,0:T(8,128)}, f32[4,384,384]{2,1,0:T(8,128)}, u32[]{:S(2)}, u32[]{:S(2)}) collective-permute-start(f32[4,384,384]{2,1,0:T(8,128)} %collective-permute-done.9.rest_1_), channel_id=1, source_target_pairs={{0,8},{1,25},{2,10},{3,27},{4,12},{5,29},{6,14},{7,31},{8,16},{9,1... | collective-permute-start | bytes 7077896 | tf_op jit(solution)/shard_map/p5/ppermute | solution.py:25
  109.4 1.4 copy-start.4
  150.8 3.8 %collective-permute-start.19 = (f32[4,96,768]{2,1,0:T(8,128)}, f32[4,96,768]{2,1,0:T(8,128)S(1)}, u32[]{:S(2)}, u32[]{:S(2)}) collective-permute-start(f32[4,96,768]{2,1,0:T(8,128)} %get-tuple-element.67), channel_id=1, source_target_pairs={{0,1},{1,0},{2,3},{3,2},{4,5},{5,4},{6,7},{7,6},{8,9},{9,8},{10,11... | collective-permute-start | bytes 3538952 | tf_op jit(solution)/shard_map/swap/ppermute | solution.py:25
  150.9 3.0 %collective-permute-start.23 = (f32[1,768]{1,0:T(1,128)}, f32[1,768]{1,0:T(1,128)S(1)}, u32[]{:S(2)}, u32[]{:S(2)}) collective-permute-start(f32[1,768]{1,0:T(1,128)} %get-tuple-element.68), channel_id=1, source_target_pairs={{0,1},{1,0},{2,3},{3,2},{4,5},{5,4},{6,7},{7,6},{8,9},{9,8},{10,11... | collective-permute-start | bytes 9224 | tf_op jit(solution)/shard_map/swap/ppermute | solution.py:25
  154.6 4.8 %collective-permute-start.24 = (f32[1,768]{1,0:T(1,128)S(1)}, f32[1,768]{1,0:T(1,128)S(1)}, u32[]{:S(2)}, u32[]{:S(2)}) collective-permute-start(f32[1,768]{1,0:T(1,128)S(1)} %add.372), channel_id=1, source_target_pairs={{0,2},{1,3},{2,4},{3,5},{4,6},{5,7},{6,0},{7,1},{8,10},{9,11},{10,... | collective-permute-start | bytes 9224 | tf_op jit(solution)/shard_map/ppermute | solution.py:25
  154.6 4.8 %collective-permute-start.25 = (f32[1,768]{1,0:T(1,128)S(1)}, f32[1,768]{1,0:T(1,128)S(1)}, u32[]{:S(2)}, u32[]{:S(2)}) collective-permute-start(f32[1,768]{1,0:T(1,128)S(1)} %add.372), channel_id=1, source_target_pairs={{0,6},{1,7},{2,0},{3,1},{4,2},{5,3},{6,4},{7,5},{8,14},{9,15},{10,... | collective-permute-start | bytes 9224 | tf_op jit(solution)/shard_map/ppermute | solution.py:25
  157.8 5.1 %collective-permute-start.26 = (f32[1,768]{1,0:T(1,128)S(1)}, f32[1,768]{1,0:T(1,128)S(1)}, u32[]{:S(2)}, u32[]{:S(2)}) collective-permute-start(f32[1,768]{1,0:T(1,128)S(1)} %add.372), channel_id=1, source_target_pairs={{0,4},{1,5},{2,6},{3,7},{4,0},{5,1},{6,2},{7,3},{8,12},{9,13},{10,... | collective-permute-start | bytes 9224 | tf_op jit(solution)/shard_map/ppermute | solution.py:25
  159.2 24.2 %copy-start.7 = (f32[256]{0:T(256)S(1)}, f32[256]{0:T(256)}, u32[]{:S(2)}) copy-start(f32[256]{0:T(256)} %param.15) | copy-start | bytes 3076
  162.9 8.8 %collective-permute-start.27 = (f32[1,768]{1,0:T(1,128)S(1)}, f32[1,768]{1,0:T(1,128)S(1)}, u32[]{:S(2)}, u32[]{:S(2)}) collective-permute-start(f32[1,768]{1,0:T(1,128)S(1)} %add_add_fusion), channel_id=1, source_target_pairs={{0,24},{1,25},{2,26},{3,27},{4,28},{5,29},{6,30},{7,31},{8,0},{9,1... | collective-permute-start | bytes 9224 | tf_op jit(solution)/shard_map/ppermute | solution.py:25
  163.5 8.3 %collective-permute-start.28 = (f32[1,768]{1,0:T(1,128)S(1)}, f32[1,768]{1,0:T(1,128)S(1)}, u32[]{:S(2)}, u32[]{:S(2)}) collective-permute-start(f32[1,768]{1,0:T(1,128)S(1)} %add_add_fusion), channel_id=1, source_target_pairs={{0,16},{1,17},{2,18},{3,19},{4,20},{5,21},{6,22},{7,23},{8,24},{9,... | collective-permute-start | bytes 9224 | tf_op jit(solution)/shard_map/ppermute | solution.py:25
  166.4 5.4 %collective-permute-start.29 = (f32[1,768]{1,0:T(1,128)S(1)}, f32[1,768]{1,0:T(1,128)S(1)}, u32[]{:S(2)}, u32[]{:S(2)}) collective-permute-start(f32[1,768]{1,0:T(1,128)S(1)} %add_add_fusion), channel_id=1, source_target_pairs={{0,8},{1,9},{2,10},{3,11},{4,12},{5,13},{6,14},{7,15},{8,16},{9,17... | collective-permute-start | bytes 9224 | tf_op jit(solution)/shard_map/ppermute | solution.py:25
  168.5 15.6 %collective-permute-start.20 = (f32[96,768]{1,0:T(8,128)S(1)}, f32[96,768]{1,0:T(8,128)S(1)}, u32[]{:S(2)}, u32[]{:S(2)}) collective-permute-start(f32[96,768]{1,0:T(8,128)S(1)} %get-tuple-element.76), channel_id=1, source_target_pairs={{0,2},{1,3},{2,4},{3,5},{4,6},{5,7},{6,0},{7,1},{8,10},{9,11},{10,... | collective-permute-start | bytes 884744 | tf_op jit(solution)/shard_map/ppermute | solution.py:25
  168.6 15.5 %collective-permute-start.21 = (f32[96,768]{1,0:T(8,128)S(1)}, f32[96,768]{1,0:T(8,128)S(1)}, u32[]{:S(2)}, u32[]{:S(2)}) collective-permute-start(f32[96,768]{1,0:T(8,128)S(1)} %get-tuple-element.78), channel_id=1, source_target_pairs={{0,6},{1,7},{2,0},{3,1},{4,2},{5,3},{6,4},{7,5},{8,14},{9,15},{10,... | collective-permute-start | bytes 884744 | tf_op jit(solution)/shard_map/ppermute | solution.py:25
  171.8 12.3 %collective-permute-start.22 = (f32[96,768]{1,0:T(8,128)S(1)}, f32[96,768]{1,0:T(8,128)S(1)}, u32[]{:S(2)}, u32[]{:S(2)}) collective-permute-start(f32[96,768]{1,0:T(8,128)S(1)} %get-tuple-element.77), channel_id=1, source_target_pairs={{0,4},{1,5},{2,6},{3,7},{4,0},{5,1},{6,2},{7,3},{8,12},{9,13},{10,... | collective-permute-start | bytes 884744 | tf_op jit(solution)/shard_map/ppermute | solution.py:25
  171.8 4.7 %collective-permute-start.30 = (f32[4,768]{1,0:T(4,128)S(1)}, f32[4,768]{1,0:T(4,128)S(1)}, u32[]{:S(2)}, u32[]{:S(2)}) collective-permute-start(f32[4,768]{1,0:T(4,128)S(1)} %get-tuple-element.84), channel_id=1, source_target_pairs={{0,96},{1,97},{2,98},{3,99},{4,100},{5,101},{6,102},{7,103},{8,104... | collective-permute-start | bytes 36872 | tf_op jit(solution)/shard_map/ppermute | solution.py:25
  175.1 5.2 %collective-permute-start.31 = (f32[4,768]{1,0:T(4,128)S(1)}, f32[4,768]{1,0:T(4,128)S(1)}, u32[]{:S(2)}, u32[]{:S(2)}) collective-permute-start(f32[4,768]{1,0:T(4,128)S(1)} %get-tuple-element.84), channel_id=1, source_target_pairs={{0,64},{1,65},{2,66},{3,67},{4,68},{5,69},{6,70},{7,71},{8,72},{9,... | collective-permute-start | bytes 36872 | tf_op jit(solution)/shard_map/ppermute | solution.py:25
  176.5 5.2 %collective-permute-start.32 = (f32[4,768]{1,0:T(4,128)S(1)}, f32[4,768]{1,0:T(4,128)S(1)}, u32[]{:S(2)}, u32[]{:S(2)}) collective-permute-start(f32[4,768]{1,0:T(4,128)S(1)} %get-tuple-element.84), channel_id=1, source_target_pairs={{0,32},{1,33},{2,34},{3,35},{4,36},{5,37},{6,38},{7,39},{8,40},{9,... | collective-permute-start | bytes 36872 | tf_op jit(solution)/shard_map/ppermute | solution.py:25
